TPU v7x, 128 devices: a whole 4x4x4 slice. The times are simulated.
128 devices in a mesh: batch: 4 (over x_lo, core), tiles: 32 (over x_hi, z, y).
Axes of the slice: x: 4 (x_hi: 2, x_lo: 2; x = x_hi * 2 + x_lo), y: 4, z: 4, core: 2. Of those that a mesh axis runs over, the one named last changes fastest.
Arguments:
- hidden: bfloat16 [4, 16384, 3072], P('batch', 'tiles'), may hold values from -6 to 6
- frozen_queries: bfloat16 [4, 16384, 1536], P('batch', 'tiles'), may hold values from -108 to 108
- frozen_keys: bfloat16 [4, 16384, 1536], P('batch', 'tiles'), may hold values from -6.09 to 6.09
- frozen_values: bfloat16 [4, 16384, 1536], P('batch', 'tiles'), may hold values from -6 to 6
- reward_output_gradient: bfloat16 [4, 16384, 1536], P('batch', 'tiles'), may hold values from -6 to 6
- truncation_step: int32 [4], P('batch'), may hold values from 0 to 49
- modulation: float32 [50, 2, 3072], replicated, may hold values from -3 to 3
- adapter_down_weight: bfloat16 [3, 3072, 32], replicated, may hold values from -0.109375 to 0.109375
- adapter_up_weight: bfloat16 [3, 32, 1536], replicated, may hold values from -1 to 1
- window: int32 [128, 27], P('tiles'), may hold values from 0 to 1, as said below
Outputs:
- attended: bfloat16 [4, 16384, 1536], P('batch', 'tiles')
- grad_down: float32 [3, 3072, 32], replicated
- grad_up: float32 [3, 32, 1536], replicated
Inputs may be any that keep to these rules, and one draw needn't show every extreme that they name: `window`: entry 13, the tile itself, is 1 for every tile.
All inputs are finite; a program needn't handle non-finite values.
Results may differ from a plain program's by a relative error of at most 0.012.
The roundings to bfloat16 on the way count: a program that leaves them out, or rounds other values in their place, can miss the bound.
Values may be sent and summed in bfloat16 or wider, within the bound.
No kernel may reach another device: no remote copies, remote signals or barrier semaphores. Data moves between devices by JAX's collectives and lax.ppermute only.
A program may use at most 192 MiB of HBM per device.

v0:
```python
import math

import jax
import jax.numpy as jnp
from jax import lax
from jax.sharding import PartitionSpec as P

HEAD = 128
TILE = 128
GF = 2
GR = 2


precise_variant = lax.Precision.HIGHEST


def extended(x, sides, width):
    for axis, dim in sides:
        peers, length = (lax.axis_size(axis), x.shape[dim])
        up = [(i, (i + 1) % peers) for i in range(peers - 1)]
        down = [(j, i) for i, j in up]
        last = lax.slice_in_dim(x, length - width, length, axis=dim)
        initial = lax.slice_in_dim(x, 0, width, axis=dim)
        before = lax.ppermute(last, axis, up)
        after = lax.ppermute(initial, axis, down)
        x = jnp.concatenate([before, x, after], axis=dim)
    return x


def shifted(value, axis, steps):
    count = lax.axis_size(axis)
    initial, last = (max(0, -steps), min(count, count - steps))
    return lax.ppermute(value, axis, [(source, source + steps) for source in range(initial, last)])


def allowed_keys(window_rows, slab_index, slab_count):
    per_slab = GF * GR
    query_tile = jnp.arange(per_slab, dtype=jnp.int32)
    key_tile = jnp.arange(3 * per_slab, dtype=jnp.int32)
    key_side = key_tile // per_slab
    key_local = key_tile % per_slab
    frame_step = key_local[None, :] // GR - query_tile[:, None] // GR
    row_step = key_local[None, :] % GR - query_tile[:, None] % GR
    offset_code = (key_side[None, :] * 3 + frame_step + 1) * 3 + row_step + 1
    nearby = (jnp.abs(frame_step) <= 1) & (jnp.abs(row_step) <= 1)
    neighbour = slab_index + key_side - 1
    inside = (neighbour >= 0) & (neighbour < slab_count)
    offsets = jnp.arange(27, dtype=jnp.int32)
    listed = jnp.sum(
        jnp.where(offset_code[:, :, None] == offsets[None, None, :], window_rows[:, None, :], 0),
        axis=2,
    )
    tile_mask = nearby & inside[None, :] & (listed > 0)
    return jnp.repeat(jnp.repeat(tile_mask, TILE, axis=0), TILE, axis=1)


def attend_group(pieces, allowed):
    queries, key_rows, value_rows, out_grad = pieces
    scale_root = 1.0 / math.sqrt(HEAD)
    scores = (
        jnp.einsum("qhe,khe->hqk", queries, key_rows, preferred_element_type=jnp.float32)
        * scale_root
    )
    scores = jnp.where(allowed[None], scores, -1e30)
    row_max = jnp.max(scores, axis=2, keepdims=True)
    weights = jnp.where(allowed[None], jnp.exp(scores - row_max), 0.0)
    totals = jnp.sum(weights, axis=2, keepdims=True)
    probs = weights / totals
    probs_low = probs.astype(jnp.bfloat16)
    attended = jnp.einsum("hqk,khe->qhe", probs_low, value_rows, preferred_element_type=jnp.float32)
    prob_grad = jnp.einsum("qhe,khe->hqk", out_grad, value_rows, preferred_element_type=jnp.float32)
    centre = jnp.sum(probs * prob_grad, axis=2, keepdims=True)
    score_grad = (probs * (prob_grad - centre) * scale_root).astype(jnp.bfloat16)
    query_grad = jnp.einsum(
        "hqk,khe->qhe", score_grad, key_rows, preferred_element_type=jnp.float32
    )
    key_grad = jnp.einsum("hqk,qhe->khe", score_grad, queries, preferred_element_type=jnp.float32)
    value_grad = jnp.einsum("hqk,qhe->khe", probs_low, out_grad, preferred_element_type=jnp.float32)
    return (attended, query_grad, key_grad, value_grad)


def attend_all(queries, key_rows, value_rows, out_grad, allowed):
    across = queries.shape[1]
    groups = across // (4 * HEAD)

    def split_heads(tensor):
        return tensor.reshape(tensor.shape[0], groups, 4, HEAD).transpose(1, 0, 2, 3)

    def join_heads(tensor):
        return tensor.transpose(1, 0, 2, 3).reshape(tensor.shape[1], across)

    results = lax.map(
        lambda pieces: attend_group(pieces, allowed),
        (
            split_heads(queries),
            split_heads(key_rows),
            split_heads(value_rows),
            split_heads(out_grad),
        ),
    )
    return tuple((join_heads(result_part) for result_part in results))


def per_device(
    hidden,
    frozen_queries,
    frozen_keys,
    frozen_values,
    reward_output_gradient,
    truncation_step,
    modulation,
    adapter_down_weight,
    adapter_up_weight,
    window,
):
    slab_rows = hidden.shape[1]
    across = frozen_queries.shape[2]
    x_full = hidden[0].astype(jnp.float32)
    row_mean = jnp.mean(x_full, axis=1, keepdims=True)
    centred = x_full - row_mean
    variance = jnp.mean(centred * centred, axis=1, keepdims=True)
    normed = centred * lax.rsqrt(variance + 1e-06)
    picker = (
        lax.broadcasted_iota(jnp.int32, (modulation.shape[0],), 0) == truncation_step[0]
    ).astype(jnp.float32)
    shift_scale = jnp.einsum("s,sjd->jd", picker, modulation, precision=precise_variant)
    input_modulated = normed * (1.0 + shift_scale[1][None, :]) + shift_scale[0][None, :]
    reduced_rank_input = jnp.einsum(
        "mx,pxo->pmo",
        input_modulated.astype(jnp.bfloat16),
        adapter_down_weight,
        preferred_element_type=jnp.float32,
    ).astype(jnp.bfloat16)
    projected_output = jnp.einsum(
        "bfe,beg->bfg", reduced_rank_input, adapter_up_weight, preferred_element_type=jnp.float32
    )
    queries = (frozen_queries[0] + projected_output[0]).astype(jnp.bfloat16)
    key_rows = (frozen_keys[0] + projected_output[1]).astype(jnp.bfloat16)
    value_rows = (frozen_values[0] + projected_output[2]).astype(jnp.bfloat16)
    slab_index = lax.axis_index("tiles")
    allowed = allowed_keys(window, slab_index, lax.axis_size("tiles"))
    expanded_up_weight = adapter_up_weight.astype(jnp.float32)
    low_full = reduced_rank_input.astype(jnp.float32)
    paired = jnp.stack([key_rows, value_rows])[:, None]
    framed = extended(paired, (("tiles", 1),), 1)
    attended, query_grad, key_grad, value_grad = attend_all(
        queries,
        framed[0].reshape(3 * slab_rows, across),
        framed[1].reshape(3 * slab_rows, across),
        reward_output_gradient[0],
        allowed,
    )
    returned = jnp.stack(
        [key_grad.reshape(3, slab_rows, across), value_grad.reshape(3, slab_rows, across)]
    )
    from_above = shifted(returned[:, 0].astype(jnp.bfloat16), "tiles", -1).astype(jnp.float32)
    from_below = shifted(returned[:, 2].astype(jnp.bfloat16), "tiles", 1).astype(jnp.float32)
    owned = returned[:, 1] + from_above + from_below
    grads = jnp.stack([query_grad, owned[0], owned[1]])
    rank_grads = jnp.einsum("jth,jrh->jtr", grads, expanded_up_weight, precision=precise_variant)
    up_terms = jnp.einsum("jtr,jth->jrh", low_full, grads, precision=precise_variant)
    down_terms = jnp.einsum("td,jtr->jdr", input_modulated, rank_grads, precision=precise_variant)
    norm_factor = 1.0 / math.sqrt(
        hidden.shape[0] * lax.axis_size("batch") * slab_rows * lax.axis_size("tiles")
    )
    grad_down, grad_up = lax.psum(
        (down_terms * norm_factor, up_terms * norm_factor), ("batch", "tiles")
    )
    return (attended.astype(jnp.bfloat16)[None], grad_down, grad_up)


def solution(mesh):
    placed = (
        P("batch", "tiles", None),
        P("batch", "tiles", None),
        P("batch", "tiles", None),
        P("batch", "tiles", None),
        P("batch", "tiles", None),
        P("batch"),
        P(),
        P(),
        P(),
        P("tiles", None),
    )
    return jax.shard_map(
        per_device,
        mesh=mesh,
        in_specs=placed,
        out_specs=(P("batch", "tiles", None), P(), P()),
        check_vma=False,
    )
```

profile of v0, /device:TPU:0, one launch (start us, length us, event | category | flops | bytes accessed | tf_op | source)
XLA Modules:
  0.0 820.1 jit_solution(3635434328755650545)
XLA Ops:
  36.8 58.1 %collective-permute-done = bf16[2,1,512,1536]{3,2,0,1:T(8,128)(2,1)} collective-permute-done((bf16[2,1,512,1536]{3,2,0,1:T(8,128)(2,1)}, bf16[2,1,512,1536]{3,2,0,1:T(8,128)(2,1)}, u32[]{:S(2)}, u32[]{:S(2)}) %collective-permute-start) | collective-permute-done | bytes 3145760 | tf_op jit(solution)/shard_map/ppermute | solution.py:24
  100.6 9.2 %pad_maximum_fusion = bf16[2,3,512,1536]{3,2,0,1:T(8,128)(2,1)} fusion(bf16[2,1,512,1536]{3,2,0,1:T(8,128)(2,1)} %collective-permute-done.1, bf16[2,1,512,1536]{3,2,0,1:T(8,128)(2,1)} %maximum_bitcast_fusion, bf16[2,1,512,1536]{3,2,0,1:T(8,128)(2,1)} %collective-permute-done), kind=kLoop, calls=%fused_computation.58 | loop fusion | flops 9437184 | bytes 18874368 | tf_op jit(solution)/shard_map/concatenate | solution.py:26
  109.8 8.6 %fusion.131 = (bf16[1,3,512,1536]{3,2,0,1:T(8,128)(2,1)}, bf16[1,3,512,1536]{3,2,0,1:T(8,128)(2,1)}) fusion(bf16[2,3,512,1536]{3,2,0,1:T(8,128)(2,1)} %pad_maximum_fusion), kind=kLoop, calls=%fused_computation.147 | loop fusion | bytes 18874368 | tf_op jit(solution)/shard_map/slice | solution.py:148
  118.4 9.1 %reshape_reshape_squeeze.6 = bf16[1536,3,4,128]{3,2,1,0:T(4,128)(2,1)} reshape(bf16[1,3,512,1536]{3,2,0,1:T(8,128)(2,1)} %get-tuple-element.142) | data formatting | bytes 9437184 | tf_op jit(solution)/shard_map/reshape;reshape;squeeze | solution.py:87
  127.4 8.5 %copy.58 = bf16[1536,3,4,128]{0,3,2,1:T(8,128)(2,1)} copy(bf16[1536,3,4,128]{3,2,1,0:T(4,128)(2,1)} %reshape_reshape_squeeze.6) | data formatting | bytes 9437184 | tf_op jit(solution)/shard_map/reshape;reshape;squeeze | solution.py:87
  135.9 9.0 %reshape_reshape_squeeze.7 = bf16[1536,3,4,128]{3,2,1,0:T(4,128)(2,1)} reshape(bf16[1,3,512,1536]{3,2,0,1:T(8,128)(2,1)} %get-tuple-element.141) | data formatting | bytes 9437184 | tf_op jit(solution)/shard_map/reshape;reshape;squeeze | solution.py:87
  150.2 327.5 %while.17 = (s32[]{:T(128)}, bf16[3,512,4,128]{1,3,2,0:T(8,128)(2,1)}, f32[3,512,4,128]{1,3,2,0:T(8,128)}, f32[3,1536,4,128]{1,3,2,0:T(8,128)}, f32[3,1536,4,128...) while((s32[]{:T(128)}, ...), condition=%wide.region_7.8_spmd.clone, body=%wide.region_3.7_spmd.clone.sunk | while | flops 4910490112 | bytes 215027920 | solution.py:92
  150.4 8.3 %fusion.167 = f32[4,512,1536]{2,1,0:T(8,128)} fusion(bf16[3,1536,4,128]{3,1,2,0:T(8,128)(2,1)} %get-tuple-element.246, s32[]{:T(128)} %get-tuple-element.228, bf16[3,512,4,128]{3,1,2,0:T(8,128)(2,1)S(1)} %get-tuple-element.245), kind=kOutput, calls=%fused_computation.25.clone.1 | convolution fusion | flops 805306368 | bytes 14681088 | tf_op jit(solution)/shard_map/while/body/eval_jaxpr/qhe,khe->hqk/dot_general | solution.py:61
  160.1 16.9 %fusion.168 = (f32[4,512]{1,0:T(4,128)S(1)}, f32[4,512,1536]{2,1,0:T(8,128)}) fusion(f32[4,512,1536]{2,1,0:T(8,128)} %fusion.167, pred[512,1536]{1,0:T(8,128)(4,1)S(1)} %copy.89), kind=kOutput, calls=%fused_computation.146.clone.1 | output fusion | flops 22021632 | bytes 25960448 | tf_op jit(solution)/shard_map/while/body/eval_jaxpr/sub | solution.py:66
  192.3 28.5 %fusion.172 = f32[3,1536,4,128]{1,3,2,0:T(8,128)} fusion(f32[3,1536,4,128]{1,3,2,0:T(8,128)} %get-tuple-element.231, s32[]{:T(128)} %get-tuple-element.228, f32[4,512,1536]{2,1,0:T(8,128)} %fusion.170, bf16[3,512,4,128]{3,1,2,0:T(8,128)(2,1)S(1)} %copy-done.6, f32[4,512,1536]{2,1,0:T(8,128)} %get-tuple-element.215, f32[4,512]{1,0:T(4,128)S(1)} %get-tuple-element.216), kind=kOutput, calls=%fused_computation.20.clone.1 | convolution fusion | flops 827330048 | bytes 54019072 | tf_op jit(solution)/shard_map/while/body/eval_jaxpr/hqk,qhe->khe/dot_general | solution.py:77
  220.8 30.5 %fusion.171 = f32[3,512,4,128]{1,3,2,0:T(8,128)} fusion(f32[3,512,4,128]{1,3,2,0:T(8,128)} %get-tuple-element.230, s32[]{:T(128)} %get-tuple-element.228, f32[4,512,1536]{2,1,0:T(8,128)} %fusion.170, bf16[3,1536,4,128]{3,1,2,0:T(8,128)(2,1)} %get-tuple-element.246, f32[4,512,1536]{2,1,0:T(8,128)} %get-tuple-element.215, ...), kind=kOutput, calls=%fused_computation.37.clone.1 | convolution fusion | flops 827330048 | bytes 52970496 | tf_op jit(solution)/shard_map/while/body/eval_jaxpr/hqk,khe->qhe/dot_general | solution.py:74
  259.5 8.3 %fusion.167 = f32[4,512,1536]{2,1,0:T(8,128)} fusion(bf16[3,1536,4,128]{3,1,2,0:T(8,128)(2,1)} %get-tuple-element.246, s32[]{:T(128)} %get-tuple-element.228, bf16[3,512,4,128]{3,1,2,0:T(8,128)(2,1)S(1)} %get-tuple-element.245), kind=kOutput, calls=%fused_computation.25.clone.1 | convolution fusion | flops 805306368 | bytes 14681088 | tf_op jit(solution)/shard_map/while/body/eval_jaxpr/qhe,khe->hqk/dot_general | solution.py:61
  269.2 16.9 %fusion.168 = (f32[4,512]{1,0:T(4,128)S(1)}, f32[4,512,1536]{2,1,0:T(8,128)}) fusion(f32[4,512,1536]{2,1,0:T(8,128)} %fusion.167, pred[512,1536]{1,0:T(8,128)(4,1)S(1)} %copy.89), kind=kOutput, calls=%fused_computation.146.clone.1 | output fusion | flops 22021632 | bytes 25960448 | tf_op jit(solution)/shard_map/while/body/eval_jaxpr/sub | solution.py:66
  301.3 28.5 %fusion.172 = f32[3,1536,4,128]{1,3,2,0:T(8,128)} fusion(f32[3,1536,4,128]{1,3,2,0:T(8,128)} %get-tuple-element.231, s32[]{:T(128)} %get-tuple-element.228, f32[4,512,1536]{2,1,0:T(8,128)} %fusion.170, bf16[3,512,4,128]{3,1,2,0:T(8,128)(2,1)S(1)} %copy-done.6, f32[4,512,1536]{2,1,0:T(8,128)} %get-tuple-element.215, f32[4,512]{1,0:T(4,128)S(1)} %get-tuple-element.216), kind=kOutput, calls=%fused_computation.20.clone.1 | convolution fusion | flops 827330048 | bytes 54019072 | tf_op jit(solution)/shard_map/while/body/eval_jaxpr/hqk,qhe->khe/dot_general | solution.py:77
  329.8 30.6 %fusion.171 = f32[3,512,4,128]{1,3,2,0:T(8,128)} fusion(f32[3,512,4,128]{1,3,2,0:T(8,128)} %get-tuple-element.230, s32[]{:T(128)} %get-tuple-element.228, f32[4,512,1536]{2,1,0:T(8,128)} %fusion.170, bf16[3,1536,4,128]{3,1,2,0:T(8,128)(2,1)} %get-tuple-element.246, f32[4,512,1536]{2,1,0:T(8,128)} %get-tuple-element.215, ...), kind=kOutput, calls=%fused_computation.37.clone.1 | convolution fusion | flops 827330048 | bytes 52970496 | tf_op jit(solution)/shard_map/while/body/eval_jaxpr/hqk,khe->qhe/dot_general | solution.py:74
  378.2 16.9 %fusion.168 = (f32[4,512]{1,0:T(4,128)S(1)}, f32[4,512,1536]{2,1,0:T(8,128)}) fusion(f32[4,512,1536]{2,1,0:T(8,128)} %fusion.167, pred[512,1536]{1,0:T(8,128)(4,1)S(1)} %copy.89), kind=kOutput, calls=%fused_computation.146.clone.1 | output fusion | flops 22021632 | bytes 25960448 | tf_op jit(solution)/shard_map/while/body/eval_jaxpr/sub | solution.py:66
  410.3 28.5 %fusion.172 = f32[3,1536,4,128]{1,3,2,0:T(8,128)} fusion(f32[3,1536,4,128]{1,3,2,0:T(8,128)} %get-tuple-element.231, s32[]{:T(128)} %get-tuple-element.228, f32[4,512,1536]{2,1,0:T(8,128)} %fusion.170, bf16[3,512,4,128]{3,1,2,0:T(8,128)(2,1)S(1)} %copy-done.6, f32[4,512,1536]{2,1,0:T(8,128)} %get-tuple-element.215, f32[4,512]{1,0:T(4,128)S(1)} %get-tuple-element.216), kind=kOutput, calls=%fused_computation.20.clone.1 | convolution fusion | flops 827330048 | bytes 54019072 | tf_op jit(solution)/shard_map/while/body/eval_jaxpr/hqk,qhe->khe/dot_general | solution.py:77
  438.8 30.5 %fusion.171 = f32[3,512,4,128]{1,3,2,0:T(8,128)} fusion(f32[3,512,4,128]{1,3,2,0:T(8,128)} %get-tuple-element.230, s32[]{:T(128)} %get-tuple-element.228, f32[4,512,1536]{2,1,0:T(8,128)} %fusion.170, bf16[3,1536,4,128]{3,1,2,0:T(8,128)(2,1)} %get-tuple-element.246, f32[4,512,1536]{2,1,0:T(8,128)} %get-tuple-element.215, ...), kind=kOutput, calls=%fused_computation.37.clone.1 | convolution fusion | flops 827330048 | bytes 52970496 | tf_op jit(solution)/shard_map/while/body/eval_jaxpr/hqk,khe->qhe/dot_general | solution.py:74
  477.7 11.9 %copy.68 = f32[1536,3,4,128]{3,2,1,0:T(4,128)} copy(f32[1536,3,4,128]{0,3,2,1:T(8,128)} %bitcast.186) | data formatting | bytes 18874368 | tf_op jit(solution)/shard_map/transpose | solution.py:90
  489.7 12.1 %stack_reshape_reshape.6 = f32[1,3,512,1536]{3,2,0,1:T(8,128)} reshape(f32[1536,3,4,128]{3,2,1,0:T(4,128)} %copy.68) | data formatting | bytes 18874368 | tf_op jit(solution)/shard_map/stack;reshape;reshape | solution.py:153
  509.9 11.9 %copy.69 = f32[1536,3,4,128]{3,2,1,0:T(4,128)} copy(f32[1536,3,4,128]{0,3,2,1:T(8,128)} %bitcast.187) | data formatting | bytes 18874368 | tf_op jit(solution)/shard_map/transpose | solution.py:90
  521.8 12.1 %stack_reshape_reshape.7 = f32[1,3,512,1536]{3,2,0,1:T(8,128)} reshape(f32[1536,3,4,128]{3,2,1,0:T(4,128)} %copy.69) | data formatting | bytes 18874368 | tf_op jit(solution)/shard_map/stack;reshape;reshape | solution.py:153
  563.6 59.7 %collective-permute-done.2 = bf16[2,512,1536]{2,1,0:T(8,128)(2,1)} collective-permute-done((bf16[2,512,1536]{2,1,0:T(8,128)(2,1)}, bf16[2,512,1536]{2,1,0:T(8,128)(2,1)}, u32[]{:S(2)}, u32[]{:S(2)}) %collective-permute-start.2) | collective-permute-done | bytes 3145760 | tf_op jit(solution)/shard_map/ppermute | solution.py:33
  646.8 161.7 %all-reduce.3.cloned.1.call-done = (f32[3,3072,32]{1,2,0:T(8,128)}, f32[3,32,1536]{2,1,0:T(8,128)}) async-done(((f32[3,3072,32]{1,2,0:T(8,128)}, f32[3,32,1536]{2,1,0:T(8,128)}), (f32[3,3072,32]{1,2,0:T(8,128)}, f32[3,32,1536]{2,1,0:T(8,128)})) %all-reduce.3.cloned.1.call-update) | async-done | bytes 1769488 | tf_op jit(solution)/shard_map/psum | solution.py:166
  (126 shorter events, 188.0 us)
Async XLA Ops:
  7.2 6.2 copy-start
  7.2 7.1 copy-start.22
  7.2 801.4 %all-reduce.3.cloned.1.call-start = ((), (), s32[]{:S(2)}) async-start(), calls=%async_computation | async-start | bytes 3538944 | tf_op jit(solution)/shard_map/psum | solution.py:166
  7.2 7.0 copy-start.3
  9.8 6.0 copy-start.17
  21.6 8.8 %copy-start.19 = (s32[4,27]{1,0:T(4,128)S(1)}, s32[4,27]{1,0:T(4,128)}, u32[]{:S(2)}) copy-start(s32[4,27]{1,0:T(4,128)} %param.21) | copy-start | bytes 1300
  23.6 71.2 %collective-permute-start = (bf16[2,1,512,1536]{3,2,0,1:T(8,128)(2,1)}, bf16[2,1,512,1536]{3,2,0,1:T(8,128)(2,1)}, u32[]{:S(2)}, u32[]{:S(2)}) collective-permute-start(bf16[2,1,512,1536]{3,2,0,1:T(8,128)(2,1)} %maximum_bitcast_fusion), channel_id=1, source_target_pairs={{0,1},{1,2},{2,3},{3,4},{4,5},{5,6},{6,7},{7,8},{8,9},{9,10},{10,1... | collective-permute-start | bytes 9437192 | tf_op jit(solution)/shard_map/ppermute | solution.py:24
  28.8 71.8 %collective-permute-start.1 = (bf16[2,1,512,1536]{3,2,0,1:T(8,128)(2,1)}, bf16[2,1,512,1536]{3,2,0,1:T(8,128)(2,1)}, u32[]{:S(2)}, u32[]{:S(2)}) collective-permute-start(bf16[2,1,512,1536]{3,2,0,1:T(8,128)(2,1)} %maximum_bitcast_fusion), channel_id=1, source_target_pairs={{1,0},{2,1},{3,2},{4,3},{5,4},{6,5},{7,6},{8,7},{9,8},{10,9},{11,1... | collective-permute-start | bytes 9437192 | tf_op jit(solution)/shard_map/ppermute | solution.py:25
  150.3 8.3 %copy-start.5 = (bf16[3,512,4,128]{3,1,2,0:T(8,128)(2,1)}, bf16[3,512,4,128]{3,1,2,0:T(8,128)(2,1)S(1)}, u32[]{:S(2)}) copy-start(bf16[3,512,4,128]{3,1,2,0:T(8,128)(2,1)S(1)} %get-tuple-element.245) | copy-start | bytes 4718596 | tf_op jit(solution)/shard_map/while
  160.1 16.9 %copy-start.7 = (bf16[3,512,4,128]{1,3,2,0:T(8,128)(2,1)S(1)}, bf16[3,512,4,128]{1,3,2,0:T(8,128)(2,1)}, u32[]{:S(2)}) copy-start(bf16[3,512,4,128]{1,3,2,0:T(8,128)(2,1)} %get-tuple-element.247) | copy-start | bytes 4718596 | tf_op jit(solution)/shard_map/while
  184.4 7.8 copy-start.6
  259.5 8.3 %copy-start.5 = (bf16[3,512,4,128]{3,1,2,0:T(8,128)(2,1)}, bf16[3,512,4,128]{3,1,2,0:T(8,128)(2,1)S(1)}, u32[]{:S(2)}) copy-start(bf16[3,512,4,128]{3,1,2,0:T(8,128)(2,1)S(1)} %get-tuple-element.245) | copy-start | bytes 4718596 | tf_op jit(solution)/shard_map/while
  269.2 16.9 %copy-start.7 = (bf16[3,512,4,128]{1,3,2,0:T(8,128)(2,1)S(1)}, bf16[3,512,4,128]{1,3,2,0:T(8,128)(2,1)}, u32[]{:S(2)}) copy-start(bf16[3,512,4,128]{1,3,2,0:T(8,128)(2,1)} %get-tuple-element.247) | copy-start | bytes 4718596 | tf_op jit(solution)/shard_map/while
  293.4 7.8 copy-start.6
  368.5 8.3 %copy-start.5 = (bf16[3,512,4,128]{3,1,2,0:T(8,128)(2,1)}, bf16[3,512,4,128]{3,1,2,0:T(8,128)(2,1)S(1)}, u32[]{:S(2)}) copy-start(bf16[3,512,4,128]{3,1,2,0:T(8,128)(2,1)S(1)} %get-tuple-element.245) | copy-start | bytes 4718596 | tf_op jit(solution)/shard_map/while
  378.2 16.9 %copy-start.7 = (bf16[3,512,4,128]{1,3,2,0:T(8,128)(2,1)S(1)}, bf16[3,512,4,128]{1,3,2,0:T(8,128)(2,1)}, u32[]{:S(2)}) copy-start(bf16[3,512,4,128]{1,3,2,0:T(8,128)(2,1)} %get-tuple-element.247) | copy-start | bytes 4718596 | tf_op jit(solution)/shard_map/while
  402.5 7.8 copy-start.6
  552.4 70.8 %collective-permute-start.2 = (bf16[2,512,1536]{2,1,0:T(8,128)(2,1)}, bf16[2,512,1536]{2,1,0:T(8,128)(2,1)}, u32[]{:S(2)}, u32[]{:S(2)}) collective-permute-start(bf16[2,512,1536]{2,1,0:T(8,128)(2,1)} %get-tuple-element.139), channel_id=1, source_target_pairs={{1,0},{2,1},{3,2},{4,3},{5,4},{6,5},{7,6},{8,7},{9,8},{10,9},{11,1... | collective-permute-start | bytes 9437192 | tf_op jit(solution)/shard_map/ppermute | solution.py:33
  553.7 70.7 %collective-permute-start.3 = (bf16[2,512,1536]{2,1,0:T(8,128)(2,1)}, bf16[2,512,1536]{2,1,0:T(8,128)(2,1)}, u32[]{:S(2)}, u32[]{:S(2)}) collective-permute-start(bf16[2,512,1536]{2,1,0:T(8,128)(2,1)} %get-tuple-element.140), channel_id=1, source_target_pairs={{0,1},{1,2},{2,3},{3,4},{4,5},{5,6},{6,7},{7,8},{8,9},{9,10},{10,1... | collective-permute-start | bytes 9437192 | tf_op jit(solution)/shard_map/ppermute | solution.py:33
  563.6 66.8 %copy-start.2 = (f32[1,512,1536]{2,1,0:T(8,128)S(1)}, f32[1,512,1536]{2,1,0:T(8,128)}, u32[]{:S(2)}) copy-start(f32[1,512,1536]{2,1,0:T(8,128)} %copy.77) | copy-start | bytes 9437188
  563.6 66.8 %copy-start.12 = (f32[512,96]{0,1:S(1)}, f32[512,96]{0,1}, u32[]{:S(2)}) copy-start(f32[512,96]{0,1} %copy-done.11) | copy-start | bytes 589828
  634.7 4.7 copy-start.18
  639.4 5.8 copy-start.10
  639.4 173.4 %copy-start.1 = (f32[50,2,3072]{2,1,0:T(2,128)S(1)}, f32[50,2,3072]{2,1,0:T(2,128)}, u32[]{:S(2)}) copy-start(f32[50,2,3072]{2,1,0:T(2,128)} %param.18) | copy-start | bytes 3686404
  (10 other events, 32.5 us)
Sparse Core Ops, SparseCore 0:
  645.4 163.1 all-reduce.2
where the time goes:
time: 831 us; the launch traced here: 820 us
  matrix products  290 us (35%)
  waiting for transfers between devices  286 us (34%)
  local copies, waits for them, and re-layouts  128 us (15%)
  other arithmetic  85.4 us (10%)
  between operations  15.5 us (2%)
  starting transfers between devices  14 us (2%)
    psum x1, waiting for transfers between devices, per_device(): lax.psum((down_terms * norm_factor, up_terms * norm_factor), ('batch', 't...  162 us
    dot_general x3, matrix products, attend_group(): jnp.einsum('hqk,khe->qhe', score_grad, key_rows, preferred_element_type=j...  91.6 us
    dot_general x3, matrix products, attend_group(): jnp.einsum('hqk,qhe->khe', score_grad, queries, preferred_element_type=jn...  85.5 us
    ppermute x2, waiting for transfers between devices, shifted(): lax.ppermute(value, axis, [(source, source + steps) for source in range(i...  60.9 us
    ppermute x1, waiting for transfers between devices, extended(): before = lax.ppermute(last, axis, up)  58.1 us
    sub x3, other arithmetic, attend_group(): weights = jnp.where(allowed[None], jnp.exp(scores - row_max), 0.0)  50.7 us
    another operation x3, local copies, waits for them, and re-layouts, per_device(): jnp.stack([key_grad.reshape(3, slab_rows, across), value_grad.reshape(3,...  32.3 us
    another operation x4, local copies, waits for them, and re-layouts, split_heads(): tensor.reshape(tensor.shape[0], groups, 4, HEAD).transpose(1, 0, 2, 3)  31.8 us
  transfers between devices with their start and end apart: 5, of which 5 were waited for; matrix products, arithmetic and copies ran while one was open for 1% of the time, Pallas kernels for 0%

commit v1 on v0

v1 whole, which is shorter than its diff:
```python
import functools
import math

import jax
import jax.numpy as jnp
from jax import lax
from jax.experimental import pallas as pl
from jax.experimental.pallas import tpu as pltpu
from jax.sharding import PartitionSpec as P

HEAD = 128
TILE = 128
GF = 2
GR = 2
RANK = 32
LOG2E = 1.4426950408889634
CHUNKS = (4, 4, 4)
QBLOCK = 256
F32 = jnp.float32
BF16 = jnp.bfloat16


def tile_bias(window_rows, slab_index, slab_count):
    per_slab = GF * GR
    query_tile = jnp.arange(per_slab, dtype=jnp.int32)
    key_tile = jnp.arange(3 * per_slab, dtype=jnp.int32)
    key_side = key_tile // per_slab
    key_local = key_tile % per_slab
    frame_step = key_local[None, :] // GR - query_tile[:, None] // GR
    row_step = key_local[None, :] % GR - query_tile[:, None] % GR
    offset_code = (key_side[None, :] * 3 + frame_step + 1) * 3 + row_step + 1
    nearby = (jnp.abs(frame_step) <= 1) & (jnp.abs(row_step) <= 1)
    neighbour = slab_index + key_side - 1
    inside = (neighbour >= 0) & (neighbour < slab_count)
    offsets = jnp.arange(27, dtype=jnp.int32)
    listed = jnp.sum(
        jnp.where(offset_code[:, :, None] == offsets[None, None, :], window_rows[:, None, :], 0),
        axis=2,
    )
    tile_mask = nearby & inside[None, :] & (listed > 0)
    return jnp.repeat(jnp.where(tile_mask, 0.0, -1e30).astype(F32), TILE, axis=1)


def dot(a, b):
    return lax.dot_general(a, b, (((1,), (0,)), ((), ())), preferred_element_type=F32)


def dot_t(a, b):
    return lax.dot_general(a, b, (((1,), (1,)), ((), ())), preferred_element_type=F32)


def split_rows(x):
    hi = x.astype(BF16)
    lo = (x - hi.astype(F32)).astype(BF16)
    return hi, lo


def attend_kernel(first, slab, *refs):
    (bias, low_prev, low_own, low_next, low0_t, fq, fk, fv, out_grad, halo_prev, halo_next,
     up_wide, up) = refs[:13]
    refs = refs[13:]
    if not first:
        rq_in, rkv_in, _ = refs[:3]
        refs = refs[3:]
    attended, grad_up, rq, rkv, q_s, k_s, vl_s, kx_s, xb_s, xd_s, cat_s = refs
    head = pl.program_id(0)
    scale = 1.0 / math.sqrt(HEAD)

    @pl.when(head == 0)
    def _():
        for i, low in enumerate((low_prev, low_own, low_next)):
            vl_s[i * slab:(i + 1) * slab, HEAD:] = low[...]
        if first:
            rq[...] = jnp.zeros_like(rq)
            rkv[...] = jnp.zeros_like(rkv)
        else:
            rq[...] = rq_in[...]
            rkv[...] = rkv_in[...]

    kv_up = jnp.concatenate([up_wide[1], up_wide[2]], axis=1)
    q_s[...] = (fq[0].astype(F32) + dot(low_own[...], up_wide[0])).astype(BF16)
    sides = ((halo_prev[0], halo_prev[1], low_prev), (fk[0], fv[0], low_own),
             (halo_next[0], halo_next[1], low_next))
    lane = lax.broadcasted_iota(jnp.int32, (slab, HEAD), 1)
    up0 = up[0]
    up0_twice = jnp.concatenate([up0, up0, jnp.zeros((2 * RANK, HEAD), BF16)], axis=0)
    for i, (k_in, v_in, low) in enumerate(sides):
        rows = slice(i * slab, (i + 1) * slab)
        added = dot(low[...], kv_up)
        keys = (k_in.astype(F32) + added[:, :HEAD]).astype(BF16)
        k_s[rows, :] = keys
        vl_s[rows, :HEAD] = (v_in.astype(F32) + added[:, HEAD:]).astype(BF16)
        ku = dot_t(keys, up0_twice)
        rest = ku - ku.astype(BF16).astype(F32)
        kx_s[rows, :] = jnp.where(
            lane < RANK, ku, jnp.where(lane < 2 * RANK, rest, low[...].astype(F32))
        ).astype(BF16)
    hi, lo = split_rows(dot_t(up[1], q_s[...]))
    xb_s[...] = jnp.concatenate([hi, lo, low0_t[...]], axis=0)
    hi, lo = split_rows(dot_t(up[2], out_grad[0]))
    xd_s[...] = jnp.concatenate([hi, lo], axis=0)

    b_total = None
    d_total = None
    for start in range(0, slab, QBLOCK):
        rows = slice(start, start + QBLOCK)
        tiles = range(start // TILE, (start + QBLOCK) // TILE)
        tile_rows = jnp.concatenate(
            [jnp.broadcast_to(bias[t:t + 1, :], (TILE, 3 * slab)) for t in tiles], axis=0
        )
        scores = dot_t(q_s[rows, :], k_s[...]) * (scale * LOG2E) + tile_rows
        row_max = jnp.max(scores, axis=1, keepdims=True)
        weights = jnp.exp2(scores - row_max)
        totals = jnp.sum(weights, axis=1, keepdims=True)
        probs = weights * (1.0 / totals)
        probs_low = probs.astype(BF16)
        prob_grad = dot_t(out_grad[0, rows, :], vl_s[:, :HEAD])
        centre = jnp.sum(probs * prob_grad, axis=1, keepdims=True)
        score_grad = (probs * (prob_grad - centre) * scale).astype(BF16)
        out = dot(probs_low, vl_s[...])
        attended[0, rows, :] = out[:, :HEAD].astype(BF16)
        cat_s[rows, :HEAD] = out[:, HEAD:]
        cat_s[rows, HEAD:] = dot(score_grad, kx_s[...])
        d_part = dot(xd_s[:, rows], probs_low)
        b_part = dot(xb_s[:, rows], score_grad)
        d_total = d_part if d_total is None else d_total + d_part
        b_total = b_part if b_total is None else b_total + b_part

    cat_t = cat_s[...].T
    c_t = cat_t[:RANK]
    a_t = cat_t[HEAD:]
    rq[...] += a_t[:RANK] + a_t[RANK:2 * RANK]
    rkv[:RANK] += b_total[:RANK] + b_total[RANK:2 * RANK]
    rkv[RANK:] += d_total[:RANK] + d_total[RANK:]

    def pair(left, right):
        hi, lo = split_rows(left)
        both = dot(jnp.concatenate([hi, lo], axis=0), right)
        return both[:RANK] + both[RANK:]

    grad_up[0] = pair(b_total[2 * RANK:], k_s[...])
    grad_up[1] = pair(a_t[2 * RANK:3 * RANK], q_s[...])
    grad_up[2] = pair(c_t, out_grad[0])


def attend_chunk(h0, heads, shared, own, halos, ups, carried):
    slab = own[0].shape[1]
    across = own[0].shape[2]
    first = carried is None

    def whole(x):
        return pl.BlockSpec(x.shape, lambda h: (0,) * x.ndim)

    own_spec = pl.BlockSpec((1, slab, HEAD), lambda h: (0, 0, h0 + h))
    halo_spec = pl.BlockSpec((2, slab, HEAD), lambda h: (0, 0, h))
    in_specs = [whole(x) for x in shared] + [own_spec] * 4 + [halo_spec] * 2 + [
        pl.BlockSpec((3, x.shape[1], HEAD), lambda h: (0, 0, h0 + h)) for x in ups
    ]
    operands = [*shared, *own, *halos, *ups]
    aliases = {}
    if not first:
        attended, rq, rkv = carried
        aliases = {len(operands) + 2: 0}
        operands += [rq, rkv, attended]
        in_specs += [whole(rq), whole(rkv), pl.BlockSpec(memory_space=pl.ANY)]
    rq_shape = jax.ShapeDtypeStruct((RANK, slab), F32)
    rkv_shape = jax.ShapeDtypeStruct((2 * RANK, 3 * slab), F32)
    attended, grad_up, rq, rkv = pl.pallas_call(
        functools.partial(attend_kernel, first, slab),
        grid=(heads,),
        in_specs=in_specs,
        out_specs=[
            own_spec,
            pl.BlockSpec((3, RANK, HEAD), lambda h: (0, 0, h)),
            whole(rq_shape),
            whole(rkv_shape),
        ],
        out_shape=[
            jax.ShapeDtypeStruct((1, slab, across), BF16),
            jax.ShapeDtypeStruct((3, RANK, heads * HEAD), F32),
            rq_shape,
            rkv_shape,
        ],
        scratch_shapes=[
            pltpu.VMEM((slab, HEAD), BF16),
            pltpu.VMEM((3 * slab, HEAD), BF16),
            pltpu.VMEM((3 * slab, 2 * HEAD), BF16),
            pltpu.VMEM((3 * slab, HEAD), BF16),
            pltpu.VMEM((3 * RANK, slab), BF16),
            pltpu.VMEM((2 * RANK, slab), BF16),
            pltpu.VMEM((slab, 2 * HEAD), F32),
        ],
        input_output_aliases=aliases,
        compiler_params=pltpu.CompilerParams(
            dimension_semantics=("arbitrary",), vmem_limit_bytes=48 << 20
        ),
        name=f"attend_{h0}",
    )(*operands)
    return attended, grad_up, rq, rkv


def neighbours(value, axis):
    count = lax.axis_size(axis)
    up = [(i, i + 1) for i in range(count - 1)]
    down = [(j, i) for i, j in up]
    return lax.ppermute(value, axis, up), lax.ppermute(value, axis, down)


def reduce_everywhere(x, batch, tiles):
    count = lax.axis_size(tiles)
    parts = x.reshape(count, x.shape[0] // count, x.shape[1])
    got = lax.all_to_all(parts, tiles, 0, 0, tiled=True)
    mine = jnp.sum(got.astype(F32), axis=0)
    peers = lax.axis_size(batch)
    spread = jnp.broadcast_to(mine.astype(BF16)[None], (peers,) + mine.shape)
    got = lax.all_to_all(spread, batch, 0, 0, tiled=True)
    total = jnp.sum(got.astype(F32), axis=0).astype(BF16)
    spread = jnp.broadcast_to(total[None], (count,) + total.shape)
    return lax.all_to_all(spread, tiles, 0, 0, tiled=True).reshape(x.shape)


def per_device(
    hidden,
    frozen_queries,
    frozen_keys,
    frozen_values,
    reward_output_gradient,
    truncation_step,
    modulation,
    adapter_down_weight,
    adapter_up_weight,
    window,
):
    slab = hidden.shape[1]
    width = hidden.shape[2]
    across = frozen_queries.shape[2]
    bounds = []
    h0 = 0
    for heads in CHUNKS:
        bounds.append((h0, heads))
        h0 += heads

    def frozen_part(h0, heads):
        columns = slice(h0 * HEAD, (h0 + heads) * HEAD)
        return jnp.concatenate([frozen_keys[:, :, columns], frozen_values[:, :, columns]], axis=0)

    halos = [neighbours(frozen_part(*bounds[0]), "tiles")]

    x_full = hidden[0].astype(F32)
    row_mean = jnp.mean(x_full, axis=1, keepdims=True)
    centred = x_full - row_mean
    variance = jnp.mean(centred * centred, axis=1, keepdims=True)
    normed = centred * lax.rsqrt(variance + 1e-06)
    shift_scale = lax.dynamic_index_in_dim(modulation, truncation_step[0], 0, keepdims=False)
    x_mod = (normed * (1.0 + shift_scale[1][None, :]) + shift_scale[0][None, :]).astype(BF16)
    down = adapter_down_weight
    down_wide = jnp.concatenate([down[2], down[0], down[1], jnp.zeros_like(down[0])], axis=1)
    low = jnp.dot(x_mod, down_wide, preferred_element_type=F32).astype(BF16)
    low_prev, low_next = neighbours(low, "tiles")
    rest = [frozen_part(*b) for b in bounds[1:]]
    *rest, low = lax.optimization_barrier((*rest, low))
    halos += [neighbours(part, "tiles") for part in rest]

    up = adapter_up_weight
    pad = lambda x, before: jnp.pad(x, ((before, 3 * RANK - before), (0, 0)))
    up_wide = jnp.stack([pad(up[0], RANK), pad(up[1], 2 * RANK), pad(up[2], 0)])
    low0_t = low[:, RANK:2 * RANK].T
    bias = tile_bias(window, lax.axis_index("tiles"), lax.axis_size("tiles"))
    shared = (bias, low_prev, low, low_next, low0_t)
    own = (frozen_queries, frozen_keys, frozen_values, reward_output_gradient)
    carried = None
    grad_up_parts = []
    for (h0, heads), halo in zip(bounds, halos):
        attended, grad_up, rq, rkv = attend_chunk(
            h0, heads, shared, own, halo, (up_wide, up), carried
        )
        carried = (attended, rq, rkv)
        grad_up_parts.append(grad_up)

    norm_factor = 1.0 / math.sqrt(
        hidden.shape[0] * lax.axis_size("batch") * slab * lax.axis_size("tiles")
    )
    count = lax.axis_size("tiles")
    from_prev = lax.ppermute(rkv[:, 2 * slab:], "tiles", [(i, i + 1) for i in range(count - 1)])
    from_next = lax.ppermute(rkv[:, :slab], "tiles", [(i + 1, i) for i in range(count - 1)])
    rank_grads = jnp.concatenate([rq, rkv[:, slab:2 * slab] + from_prev + from_next], axis=0)
    hi, lo = split_rows(rank_grads)
    both = jnp.dot(jnp.concatenate([hi, lo], axis=0), x_mod, preferred_element_type=F32)
    grad_down = (both[:3 * RANK] + both[3 * RANK:]) * norm_factor
    grad_up = jnp.concatenate(grad_up_parts, axis=2) * norm_factor
    flat = jnp.concatenate(
        [grad_down.astype(BF16).reshape(-1, 128), grad_up.astype(BF16).reshape(-1, 128)], axis=0
    )
    summed = reduce_everywhere(flat, "batch", "tiles").astype(F32)
    split = 3 * RANK * width // 128
    grad_down = summed[:split].reshape(3, RANK, width).transpose(0, 2, 1)
    grad_up = summed[split:].reshape(3, RANK, across)
    return (attended, grad_down, grad_up)


def solution(mesh):
    placed = (
        P("batch", "tiles", None),
        P("batch", "tiles", None),
        P("batch", "tiles", None),
        P("batch", "tiles", None),
        P("batch", "tiles", None),
        P("batch"),
        P(),
        P(),
        P(),
        P("tiles", None),
    )
    return jax.shard_map(
        per_device,
        mesh=mesh,
        in_specs=placed,
        out_specs=(P("batch", "tiles", None), P(), P()),
        check_vma=False,
    )
```

time: 831 us -> 193 us (0.23); the launches traced: 820 us -> 193 us
  matrix products: 290 us -> 3.86 us
  waiting for transfers between devices: 286 us -> 21.5 us
  local copies, waits for them, and re-layouts: 128 us -> 5.52 us
  other arithmetic: 85.4 us -> 9.76 us
  blocking collectives: 0 us -> 63.8 us
  Pallas kernels: 0 us -> 56.9 us
  starting transfers between devices: 14 us -> 29.5 us
  between operations: 15.5 us -> 1.85 us
    dot_general x23 -> x2, matrix products: 289 us -> 3.86 us  [the longest x1 2.67 us: per_device(): jnp.dot(jnp.concatenate([hi, lo], axis=0), x_mod, preferred_element_type=...]
    psum x1 -> x0, waiting for transfers between devices: 162 us -> none  [per_device(): lax.psum((down_terms * norm_factor, up_terms * norm_factor), ('batch', 't...]
    ppermute x4 -> x10, waiting for transfers between devices: 125 us -> 21.5 us  [the longest x8 15.1 us: neighbours(): return (lax.ppermute(value, axis, up), lax.ppermute(value, axis, down))]
    another operation x8 -> x2, local copies, waits for them, and re-layouts: 67.7 us -> 0.08 us  [per_device(): up_wide = jnp.stack([pad(up[0], RANK), pad(up[1], 2 * RANK), pad(up[2], 0)])]
    all_to_all x0 -> x3, blocking collectives: none -> 63.8 us  [the longest x1 36.2 us: reduce_everywhere(): got = lax.all_to_all(parts, tiles, 0, 0, tiled=True)]
    pallas_call x0 -> x3, Pallas kernels: none -> 56.9 us  [attend_chunk(): pl.pallas_call(functools.partial(attend_kernel, first, slab), grid=(heads...]
    sub x3 -> x0, other arithmetic: 50.7 us -> none  [attend_group(): weights = jnp.where(allowed[None], jnp.exp(scores - row_max), 0.0)]
    transpose x2 -> x1, local copies, waits for them, and re-layouts: 23.9 us -> 0.01 us  [per_device(): low0_t = low[:, RANK:2 * RANK].T]
  transfers between devices with their start and end apart: 5 -> 10, of which waited for: 5 -> 6; matrix products, arithmetic and copies ran while one was open for 1% -> 2% of each run, Pallas kernels for 0% -> 20%
where the time goes in v1:
time: 193 us
  blocking collectives  63.8 us (33%)
  Pallas kernels  56.9 us (29%)
  starting transfers between devices  29.5 us (15%)
  waiting for transfers between devices  21.5 us (11%)
  other arithmetic  9.76 us (5%)
  local copies, waits for them, and re-layouts  5.52 us (3%)
  matrix products  3.86 us (2%)
    pallas_call x3, Pallas kernels, attend_chunk(): pl.pallas_call(functools.partial(attend_kernel, first, slab), grid=(heads...  56.9 us
    all_to_all x1, blocking collectives, reduce_everywhere(): got = lax.all_to_all(parts, tiles, 0, 0, tiled=True)  36.2 us
    ppermute x8, starting transfers between devices, neighbours(): return (lax.ppermute(value, axis, up), lax.ppermute(value, axis, down))  24.7 us
    all_to_all x1, blocking collectives, reduce_everywhere(): return lax.all_to_all(spread, tiles, 0, 0, tiled=True).reshape(x.shape)  20.8 us
    ppermute x8, waiting for transfers between devices, neighbours(): return (lax.ppermute(value, axis, up), lax.ppermute(value, axis, down))  15.1 us
    all_to_all x1, blocking collectives, reduce_everywhere(): got = lax.all_to_all(spread, batch, 0, 0, tiled=True)  6.84 us
    ppermute x1, waiting for transfers between devices, per_device(): lax.ppermute(rkv[:, :slab], 'tiles', [(i + 1, i) for i in range(count - 1)])  5.58 us
  transfers between devices with their start and end apart: 10, of which 6 were waited for; matrix products, arithmetic and copies ran while one was open for 2% of the time, Pallas kernels for 20%

profile of v1, /device:TPU:0, one launch (start us, length us, event | category | flops | bytes accessed | tf_op | source)
XLA Modules:
  0.0 192.6 jit_solution(5201618038000631043)
XLA Ops:
  1.4 2.5 %convert_reduce_fusion = f32[512]{0:T(512)S(1)} fusion(bf16[1,512,3072]{2,1,0:T(8,128)(2,1)} %param.10), kind=kLoop, calls=%fused_computation | loop fusion | flops 3145216 | bytes 3147776 | tf_op jit(solution)/shard_map/reduce_sum | solution.py:250
  6.7 1.7 fusion.6
  10.1 3.7 %collective-permute-start = (bf16[512,128]{0,1:T(8,128)(2,1)S(1)}, bf16[512,128]{0,1:T(8,128)(2,1)S(1)}, u32[]{:S(2)}, u32[]{:S(2)}) collective-permute-start(bf16[512,128]{0,1:T(8,128)(2,1)S(1)} %convolution_convert_fusion), channel_id=1, source_target_pairs={{0,1},{1,2},{2,3},{3,4},{4,5},{5,6},{6,7},{7,8},{8,9},{9,10},{10,1... | collective-permute-start | bytes 393224 | tf_op jit(solution)/shard_map/ppermute | solution.py:206
  13.8 1.3 collective-permute-start.1
  16.4 4.6 %collective-permute-start.6 = (bf16[2,512,512]{2,1,0:T(8,128)(2,1)}, bf16[2,512,512]{2,1,0:T(8,128)(2,1)S(1)}, u32[]{:S(2)}, u32[]{:S(2)}) collective-permute-start(bf16[2,512,512]{2,1,0:T(8,128)(2,1)} %pad_maximum_fusion.3), channel_id=1, source_target_pairs={{0,1},{1,2},{2,3},{3,4},{4,5},{5,6},{6,7},{7,8},{8,9},{9,10},{10,1... | collective-permute-start | bytes 3145736 | tf_op jit(solution)/shard_map/ppermute | solution.py:206
  21.0 1.3 collective-permute-start.7
  22.3 1.5 pad_maximum_fusion.1
  23.9 5.6 %collective-permute-start.4 = (bf16[2,512,512]{2,1,0:T(8,128)(2,1)}, bf16[2,512,512]{2,1,0:T(8,128)(2,1)}, u32[]{:S(2)}, u32[]{:S(2)}) collective-permute-start(bf16[2,512,512]{2,1,0:T(8,128)(2,1)} %get-tuple-element.20), channel_id=1, source_target_pairs={{0,1},{1,2},{2,3},{3,4},{4,5},{5,6},{6,7},{7,8},{8,9},{9,10},{10,1... | collective-permute-start | bytes 3145736 | tf_op jit(solution)/shard_map/ppermute | solution.py:206
  31.5 5.5 %collective-permute-start.2 = (bf16[2,512,512]{2,1,0:T(8,128)(2,1)}, bf16[2,512,512]{2,1,0:T(8,128)(2,1)}, u32[]{:S(2)}, u32[]{:S(2)}) collective-permute-start(bf16[2,512,512]{2,1,0:T(8,128)(2,1)} %get-tuple-element.19), channel_id=1, source_target_pairs={{0,1},{1,2},{2,3},{3,4},{4,5},{5,6},{6,7},{7,8},{8,9},{9,10},{10,1... | collective-permute-start | bytes 3145736 | tf_op jit(solution)/shard_map/ppermute | solution.py:206
  37.0 7.9 %collective-permute-done.6.refs_9_ = bf16[2,512,512]{2,1,0:T(8,128)(2,1)S(1)} collective-permute-done((bf16[2,512,512]{2,1,0:T(8,128)(2,1)}, bf16[2,512,512]{2,1,0:T(8,128)(2,1)S(1)}, u32[]{:S(2)}, u32[]{:S(2)}) %collective-permute-start.6) | collective-permute-done | bytes 1048608 | tf_op jit(solution)/shard_map/ppermute | solution.py:206
  44.9 1.5 collective-permute-start.3
  47.0 2.3 %collective-permute-done.7.refs_10_ = bf16[2,512,512]{2,1,0:T(8,128)(2,1)} collective-permute-done((bf16[2,512,512]{2,1,0:T(8,128)(2,1)}, bf16[2,512,512]{2,1,0:T(8,128)(2,1)}, u32[]{:S(2)}, u32[]{:S(2)}) %collective-permute-start.7) | collective-permute-done | bytes 1048608 | tf_op jit(solution)/shard_map/ppermute | solution.py:206
  49.3 18.9 %attend_0.1 = (bf16[1,512,1536]{2,1,0:T(8,128)(2,1)}, f32[3,32,512]{2,1,0:T(8,128)S(1)}, f32[32,512]{1,0:T(8,128)S(1)}, f32[64,1536]{1,0:T(8,128)S(1)}) custom-call(f32[4,1536]{1,0:T(4,128)S(1)} %bitcast.50, bf16[512,128]{1,0:T(8,128)(2,1)S(1)} %copy.54.refs_1_, bf16[512,128]{1,0:T(8,128)(2,1)S(1)} %copy.55.refs_2_, bf16[512,128]{1,0:T(8,128)(2,1)S(1)} %copy.56.refs_3_, ...), custom_call_target="tpu_custom_call" | custom-call | tf_op jit(solution)/shard_map/attend_0/pallas_call | solution.py:168
  68.3 3.5 %collective-permute-done.5.refs_10_ = bf16[2,512,512]{2,1,0:T(8,128)(2,1)} collective-permute-done((bf16[2,512,512]{2,1,0:T(8,128)(2,1)}, bf16[2,512,512]{2,1,0:T(8,128)(2,1)}, u32[]{:S(2)}, u32[]{:S(2)}) %collective-permute-start.5) | collective-permute-done | bytes 1048608 | tf_op jit(solution)/shard_map/ppermute | solution.py:206
  71.8 19.0 %attend_4.1 = (bf16[1,512,1536]{2,1,0:T(8,128)(2,1)}, f32[3,32,512]{2,1,0:T(8,128)S(1)}, f32[32,512]{1,0:T(8,128)S(1)}, f32[64,1536]{1,0:T(8,128)S(1)}) custom-call(f32[4,1536]{1,0:T(4,128)S(1)} %bitcast.51, bf16[512,128]{1,0:T(8,128)(2,1)S(1)} %copy.54.refs_1_, bf16[512,128]{1,0:T(8,128)(2,1)S(1)} %copy.55.refs_2_, ...), custom_call_target="tpu_custom_call", output_to_operand_aliasing={{0}: (15, {})} | custom-call | tf_op jit(solution)/shard_map/attend_4/pallas_call | solution.py:168
  90.8 1.4 collective-permute-done.3.refs_10_
  92.2 19.0 %attend_8.1 = (bf16[1,512,1536]{2,1,0:T(8,128)(2,1)}, f32[3,32,512]{2,1,0:T(8,128)S(1)}, f32[32,512]{1,0:T(8,128)S(1)}, f32[64,1536]{1,0:T(8,128)S(1)}) custom-call(f32[4,1536]{1,0:T(4,128)S(1)} %bitcast.52, bf16[512,128]{1,0:T(8,128)(2,1)S(1)} %copy.54.refs_1_, bf16[512,128]{1,0:T(8,128)(2,1)S(1)} %copy.55.refs_2_, ...), custom_call_target="tpu_custom_call", output_to_operand_aliasing={{0}: (15, {})} | custom-call | tf_op jit(solution)/shard_map/attend_8/pallas_call | solution.py:168
  111.2 3.4 %collective-permute-start.8 = (f32[64,512]{1,0:T(8,128)S(1)}, f32[64,512]{1,0:T(8,128)S(1)}, u32[]{:S(2)}, u32[]{:S(2)}) collective-permute-start(f32[64,512]{1,0:T(8,128)S(1)} %get-tuple-element.44), channel_id=1, source_target_pairs={{0,1},{1,2},{2,3},{3,4},{4,5},{5,6},{6,7},{7,8},{8,9},{9,10},{10,1... | collective-permute-start | bytes 393224 | tf_op jit(solution)/shard_map/ppermute | solution.py:284
  114.6 1.3 collective-permute-start.9
  117.1 5.6 %collective-permute-done.9 = f32[64,512]{1,0:T(8,128)S(1)} collective-permute-done((f32[64,512]{1,0:T(8,128)S(1)}, f32[64,512]{1,0:T(8,128)S(1)}, u32[]{:S(2)}, u32[]{:S(2)}) %collective-permute-start.9) | collective-permute-done | bytes 131104 | tf_op jit(solution)/shard_map/ppermute | solution.py:285
  122.8 2.7 %fusion.17 = f32[192,3072]{1,0:T(8,128)S(1)} fusion(bf16[512,3072]{1,0:T(8,128)(2,1)} %copy-done.4, bf16[96,512]{1,0:T(8,128)(2,1)S(1)} %subtract_convert_fusion, bf16[96,512]{1,0:T(8,128)(2,1)S(1)} %fusion.21), kind=kOutput, calls=%fused_computation.31 | convolution fusion | flops 604372992 | bytes 5701632 | tf_op jit(solution)/shard_map/dot_general | solution.py:288
  126.1 36.2 %all_to_all.15 = bf16[32,108,128]{2,1,0:T(8,128)(2,1)S(1)} all-to-all(bf16[32,108,128]{2,1,0:T(8,128)(2,1)S(1)} %reshape.265), channel_id=1, replica_groups=mesh['batch'=4,'tiles'=32] {'tiles'}, dimensions={0} | all-to-all | bytes 1769472 | tf_op jit(solution)/shard_map/all_to_all | solution.py:212
  162.4 6.8 %all_to_all.16 = bf16[4,108,128]{2,1,0:T(8,128)(2,1)S(1)} all-to-all(bf16[4,108,128]{2,1,0:T(8,128)(2,1)S(1)} %broadcast_in_dim.55), channel_id=1, replica_groups=mesh['batch'=4,'tiles'=32] {'batch'}, dimensions={0} | all-to-all | bytes 221184 | tf_op jit(solution)/shard_map/all_to_all | solution.py:216
  169.4 20.8 %all_to_all.17 = bf16[32,108,128]{2,1,0:T(8,128)(2,1)S(1)} all-to-all(bf16[32,108,128]{2,1,0:T(8,128)(2,1)S(1)} %broadcast_in_dim.56), channel_id=1, replica_groups=mesh['batch'=4,'tiles'=32] {'tiles'}, dimensions={0} | all-to-all | bytes 1769472 | tf_op jit(solution)/shard_map/all_to_all | solution.py:219
  (70 shorter events, 12.8 us)
Async XLA Ops:
  0.6 3.4 %copy-start.1 = (bf16[1,512,3072]{2,1,0:T(8,128)(2,1)S(1)}, bf16[1,512,3072]{2,1,0:T(8,128)(2,1)}, u32[]{:S(2)}) copy-start(bf16[1,512,3072]{2,1,0:T(8,128)(2,1)} %param.10) | copy-start | bytes 9437188
  4.0 1.1 copy-start.5
  6.7 1.7 copy-start.6
  8.4 1.7 copy-start.4
  8.4 6.6 %copy-start.2 = (bf16[1,512,1536]{2,1,0:T(8,128)(2,1)S(1)}, bf16[1,512,1536]{2,1,0:T(8,128)(2,1)}, u32[]{:S(2)}) copy-start(bf16[1,512,1536]{2,1,0:T(8,128)(2,1)} %refs_6_.5) | copy-start | bytes 4718596
  10.1 5.1 %copy-start.3 = (bf16[1,512,1536]{2,1,0:T(8,128)(2,1)S(1)}, bf16[1,512,1536]{2,1,0:T(8,128)(2,1)}, u32[]{:S(2)}) copy-start(bf16[1,512,1536]{2,1,0:T(8,128)(2,1)} %refs_7_.5) | copy-start | bytes 4718596
  10.1 20.1 %collective-permute-start = (bf16[512,128]{0,1:T(8,128)(2,1)S(1)}, bf16[512,128]{0,1:T(8,128)(2,1)S(1)}, u32[]{:S(2)}, u32[]{:S(2)}) collective-permute-start(bf16[512,128]{0,1:T(8,128)(2,1)S(1)} %convolution_convert_fusion), channel_id=1, source_target_pairs={{0,1},{1,2},{2,3},{3,4},{4,5},{5,6},{6,7},{7,8},{8,9},{9,10},{10,1... | collective-permute-start | bytes 393224 | tf_op jit(solution)/shard_map/ppermute | solution.py:206
  13.8 17.7 %collective-permute-start.1 = (bf16[512,128]{0,1:T(8,128)(2,1)S(1)}, bf16[512,128]{0,1:T(8,128)(2,1)S(1)}, u32[]{:S(2)}, u32[]{:S(2)}) collective-permute-start(bf16[512,128]{0,1:T(8,128)(2,1)S(1)} %convolution_convert_fusion), channel_id=1, source_target_pairs={{1,0},{2,1},{3,2},{4,3},{5,4},{6,5},{7,6},{8,7},{9,8},{10,9},{11,1... | collective-permute-start | bytes 393224 | tf_op jit(solution)/shard_map/ppermute | solution.py:206
  16.4 28.5 %collective-permute-start.6 = (bf16[2,512,512]{2,1,0:T(8,128)(2,1)}, bf16[2,512,512]{2,1,0:T(8,128)(2,1)S(1)}, u32[]{:S(2)}, u32[]{:S(2)}) collective-permute-start(bf16[2,512,512]{2,1,0:T(8,128)(2,1)} %pad_maximum_fusion.3), channel_id=1, source_target_pairs={{0,1},{1,2},{2,3},{3,4},{4,5},{5,6},{6,7},{7,8},{8,9},{9,10},{10,1... | collective-permute-start | bytes 3145736 | tf_op jit(solution)/shard_map/ppermute | solution.py:206
  21.0 28.3 %collective-permute-start.7 = (bf16[2,512,512]{2,1,0:T(8,128)(2,1)}, bf16[2,512,512]{2,1,0:T(8,128)(2,1)}, u32[]{:S(2)}, u32[]{:S(2)}) collective-permute-start(bf16[2,512,512]{2,1,0:T(8,128)(2,1)} %pad_maximum_fusion.3), channel_id=1, source_target_pairs={{1,0},{2,1},{3,2},{4,3},{5,4},{6,5},{7,6},{8,7},{9,8},{10,9},{11,1... | collective-permute-start | bytes 3145736 | tf_op jit(solution)/shard_map/ppermute | solution.py:206
  22.3 7.3 %copy-start.7 = (s32[4,27]{1,0:T(4,128)S(1)}, s32[4,27]{1,0:T(4,128)}, u32[]{:S(2)}) copy-start(s32[4,27]{1,0:T(4,128)} %param.19) | copy-start | bytes 1300
  22.3 7.6 %copy-start = (bf16[3,32,1536]{2,1,0:T(8,128)(2,1)S(1)}, bf16[3,32,1536]{2,1,0:T(8,128)(2,1)}, u32[]{:S(2)}) copy-start(bf16[3,32,1536]{2,1,0:T(8,128)(2,1)} %refs_12_.5) | copy-start | bytes 884740
  23.9 44.4 %collective-permute-start.4 = (bf16[2,512,512]{2,1,0:T(8,128)(2,1)}, bf16[2,512,512]{2,1,0:T(8,128)(2,1)}, u32[]{:S(2)}, u32[]{:S(2)}) collective-permute-start(bf16[2,512,512]{2,1,0:T(8,128)(2,1)} %get-tuple-element.20), channel_id=1, source_target_pairs={{0,1},{1,2},{2,3},{3,4},{4,5},{5,6},{6,7},{7,8},{8,9},{9,10},{10,1... | collective-permute-start | bytes 3145736 | tf_op jit(solution)/shard_map/ppermute | solution.py:206
  30.2 41.6 %collective-permute-start.5 = (bf16[2,512,512]{2,1,0:T(8,128)(2,1)}, bf16[2,512,512]{2,1,0:T(8,128)(2,1)}, u32[]{:S(2)}, u32[]{:S(2)}) collective-permute-start(bf16[2,512,512]{2,1,0:T(8,128)(2,1)} %get-tuple-element.20), channel_id=1, source_target_pairs={{1,0},{2,1},{3,2},{4,3},{5,4},{6,5},{7,6},{8,7},{9,8},{10,9},{11,1... | collective-permute-start | bytes 3145736 | tf_op jit(solution)/shard_map/ppermute | solution.py:206
  31.5 59.3 %collective-permute-start.2 = (bf16[2,512,512]{2,1,0:T(8,128)(2,1)}, bf16[2,512,512]{2,1,0:T(8,128)(2,1)}, u32[]{:S(2)}, u32[]{:S(2)}) collective-permute-start(bf16[2,512,512]{2,1,0:T(8,128)(2,1)} %get-tuple-element.19), channel_id=1, source_target_pairs={{0,1},{1,2},{2,3},{3,4},{4,5},{5,6},{6,7},{7,8},{8,9},{9,10},{10,1... | collective-permute-start | bytes 3145736 | tf_op jit(solution)/shard_map/ppermute | solution.py:206
  44.9 47.4 %collective-permute-start.3 = (bf16[2,512,512]{2,1,0:T(8,128)(2,1)}, bf16[2,512,512]{2,1,0:T(8,128)(2,1)}, u32[]{:S(2)}, u32[]{:S(2)}) collective-permute-start(bf16[2,512,512]{2,1,0:T(8,128)(2,1)} %get-tuple-element.19), channel_id=1, source_target_pairs={{1,0},{2,1},{3,2},{4,3},{5,4},{6,5},{7,6},{8,7},{9,8},{10,9},{11,1... | collective-permute-start | bytes 3145736 | tf_op jit(solution)/shard_map/ppermute | solution.py:206
  111.2 5.9 %collective-permute-start.8 = (f32[64,512]{1,0:T(8,128)S(1)}, f32[64,512]{1,0:T(8,128)S(1)}, u32[]{:S(2)}, u32[]{:S(2)}) collective-permute-start(f32[64,512]{1,0:T(8,128)S(1)} %get-tuple-element.44), channel_id=1, source_target_pairs={{0,1},{1,2},{2,3},{3,4},{4,5},{5,6},{6,7},{7,8},{8,9},{9,10},{10,1... | collective-permute-start | bytes 393224 | tf_op jit(solution)/shard_map/ppermute | solution.py:284
  114.6 8.1 %collective-permute-start.9 = (f32[64,512]{1,0:T(8,128)S(1)}, f32[64,512]{1,0:T(8,128)S(1)}, u32[]{:S(2)}, u32[]{:S(2)}) collective-permute-start(f32[64,512]{1,0:T(8,128)S(1)} %get-tuple-element.45), channel_id=1, source_target_pairs={{1,0},{2,1},{3,2},{4,3},{5,4},{6,5},{7,6},{8,7},{9,8},{10,9},{11,1... | collective-permute-start | bytes 393224 | tf_op jit(solution)/shard_map/ppermute | solution.py:285

commit v2 on v1

v2 whole, which is shorter than its diff:
```python
import functools
import math

import jax
import jax.numpy as jnp
from jax import lax
from jax.experimental import pallas as pl
from jax.experimental.pallas import tpu as pltpu
from jax.sharding import PartitionSpec as P

HEAD = 128
TILE = 128
GF = 2
GR = 2
RANK = 32
LOG2E = 1.4426950408889634
EARLY = 2
CHUNKS = (6, 4, 2)
QBLOCK = 512
PADDING = 8
PER_STEP = 2
F32 = jnp.float32
BF16 = jnp.bfloat16


def tile_bias(window_rows, slab_index, slab_count):
    per_slab = GF * GR
    query_tile = jnp.arange(per_slab, dtype=jnp.int32)
    key_tile = jnp.arange(3 * per_slab, dtype=jnp.int32)
    key_side = key_tile // per_slab
    key_local = key_tile % per_slab
    frame_step = key_local[None, :] // GR - query_tile[:, None] // GR
    row_step = key_local[None, :] % GR - query_tile[:, None] % GR
    offset_code = (key_side[None, :] * 3 + frame_step + 1) * 3 + row_step + 1
    nearby = (jnp.abs(frame_step) <= 1) & (jnp.abs(row_step) <= 1)
    neighbour = slab_index + key_side - 1
    inside = (neighbour >= 0) & (neighbour < slab_count)
    offsets = jnp.arange(27, dtype=jnp.int32)
    listed = jnp.sum(
        jnp.where(offset_code[:, :, None] == offsets[None, None, :], window_rows[:, None, :], 0),
        axis=2,
    )
    tile_mask = nearby & inside[None, :] & (listed > 0)
    return jnp.repeat(jnp.where(tile_mask, 0.0, -1e30).astype(F32), TILE, axis=1)


def dot(a, b):
    return lax.dot_general(a, b, (((1,), (0,)), ((), ())), preferred_element_type=F32)


def dot_t(a, b):
    return lax.dot_general(a, b, (((1,), (1,)), ((), ())), preferred_element_type=F32)


def split_rows(x):
    hi = x.astype(BF16)
    lo = (x - hi.astype(F32)).astype(BF16)
    return hi, lo


def attend_kernel(first, last, slab, *refs):
    (bias, low_own, low0_t, low_prev, low_next, fq, fk, fv, out_grad, up_wide, up) = refs[:11]
    halos = refs[11:15]
    refs = refs[15:]
    if first:
        early, refs = refs[:4], refs[4:]
    if not first:
        rq_in, rkv_in, _ = refs[:3]
        refs = refs[3:]
    attended, grad_up, rq, rkv = refs[:4]
    refs = refs[4:]
    if last:
        to_prev, to_next = refs[:2]
        refs = refs[2:]
    q_s, k_s, vl_s, kx_s, xb_s, xd_s, cat_s = refs
    scale = 1.0 / math.sqrt(HEAD)

    @pl.when(pl.program_id(0) == 0)
    def _():
        half = TILE // 2
        for n in range(PER_STEP):
            vl_s[n, slab:2 * slab, HEAD:] = low_own[...]
            for i, low in ((0, low_prev), (2, low_next)):
                for g in range(slab // half):
                    rows = slice(i * slab + g * half, i * slab + (g + 1) * half)
                    cols = slice(g // 2 * HEAD, (g // 2 + 1) * HEAD)
                    vl_s[n, rows, HEAD:] = low[g % 2, :, cols]
        if first:
            rq[...] = jnp.zeros_like(rq)
            rkv[...] = jnp.zeros_like(rkv)
        else:
            rq[...] = rq_in[...]
            rkv[...] = rkv_in[...]

    lane = lax.broadcasted_iota(jnp.int32, (slab, HEAD), 1)

    def pair(left, right):
        hi, lo = split_rows(left)
        both = dot(jnp.concatenate([hi, lo], axis=0), right)
        return both[:RANK] + both[RANK:]

    def prepare(n):
        cols = slice(n * HEAD, (n + 1) * HEAD)
        kv_up = jnp.concatenate([up_wide[1, :, cols], up_wide[2, :, cols]], axis=1)
        q_s[n] = (fq[0, :, cols].astype(F32) + dot(low_own[...], up_wide[0, :, cols])).astype(BF16)
        arrived = [halo[0, :, cols] for halo in halos]
        if first:
            begin = pl.program_id(0) == 0
            arrived = [jnp.where(begin, e[0, :, cols], a) for e, a in zip(early, arrived)]
        sides = (arrived[:2], (fk[0, :, cols], fv[0, :, cols]), arrived[2:])
        up0 = up[0, :, cols]
        up0_twice = jnp.concatenate([up0, up0, jnp.zeros((2 * RANK, HEAD), BF16)], axis=0)
        for i, (k_in, v_in) in enumerate(sides):
            rows = slice(i * slab, (i + 1) * slab)
            low = vl_s[n, rows, HEAD:]
            added = dot(low, kv_up)
            keys = (k_in.astype(F32) + added[:, :HEAD]).astype(BF16)
            k_s[n, rows, :] = keys
            vl_s[n, rows, :HEAD] = (v_in.astype(F32) + added[:, HEAD:]).astype(BF16)
            ku = dot_t(keys, up0_twice)
            rest = ku - ku.astype(BF16).astype(F32)
            kx_s[n, rows, :] = jnp.where(
                lane < RANK, ku, jnp.where(lane < 2 * RANK, rest, low.astype(F32))
            ).astype(BF16)
        hi, lo = split_rows(dot_t(up[1, :, cols], q_s[n]))
        xb_s[n] = jnp.concatenate([hi, lo, low0_t[...]], axis=0)
        hi, lo = split_rows(dot_t(up[2, :, cols], out_grad[0, :, cols]))
        xd_s[n] = jnp.concatenate([hi, lo], axis=0)

    def products(n, rows):
        cols = slice(n * HEAD, (n + 1) * HEAD)
        scores = dot_t(q_s[n, rows, :], k_s[n])
        prob_grad = dot_t(out_grad[0, rows, cols], vl_s[n, :, :HEAD])
        return scores, prob_grad

    def soften(rows, scores, prob_grad):
        tiles = range(rows.start // TILE, rows.stop // TILE)
        tile_rows = jnp.concatenate(
            [jnp.broadcast_to(bias[t:t + 1, :], (TILE, 3 * slab)) for t in tiles], axis=0
        )
        scores = scores * (scale * LOG2E) + tile_rows
        row_max = jnp.max(scores, axis=1, keepdims=True)
        weights = jnp.exp2(scores - row_max)
        totals = jnp.sum(weights, axis=1, keepdims=True)
        probs = weights * (1.0 / totals)
        centre = jnp.sum(probs * prob_grad, axis=1, keepdims=True)
        score_grad = (probs * (prob_grad - centre) * scale).astype(BF16)
        return probs.astype(BF16), score_grad

    def spread(n, rows, probs_low, score_grad):
        out = dot(probs_low, vl_s[n])
        attended[0, rows, n * HEAD:(n + 1) * HEAD] = out[:, :HEAD].astype(BF16)
        cat_s[n, rows, :HEAD] = out[:, HEAD:]
        cat_s[n, rows, HEAD:] = dot(score_grad, kx_s[n])
        return dot(xd_s[n, :, rows], probs_low), dot(xb_s[n, :, rows], score_grad)

    def finish(n, d_total, b_total):
        cols = slice(n * HEAD, (n + 1) * HEAD)
        cat_t = cat_s[n].T
        c_t = cat_t[:RANK]
        a_t = cat_t[HEAD:]
        grad_up[0, :, cols] = pair(b_total[2 * RANK:], k_s[n])
        grad_up[1, :, cols] = pair(a_t[2 * RANK:3 * RANK], q_s[n])
        grad_up[2, :, cols] = pair(c_t, out_grad[0, :, cols])
        return (a_t[:RANK] + a_t[RANK:2 * RANK], b_total[:RANK] + b_total[RANK:2 * RANK],
                d_total[:RANK] + d_total[RANK:])

    steps = [(n, slice(r, r + QBLOCK)) for n in range(PER_STEP) for r in range(0, slab, QBLOCK)]
    totals = [[None, None] for _ in range(PER_STEP)]
    for n in range(PER_STEP):
        prepare(n)
    made = {}
    soft = {}
    for i in range(len(steps) + 2):
        if i < len(steps):
            made[i] = products(*steps[i])
        if 0 <= i - 1 < len(steps):
            soft[i - 1] = soften(steps[i - 1][1], *made.pop(i - 1))
        if 0 <= i - 2 < len(steps):
            n, rows = steps[i - 2]
            parts = spread(n, rows, *soft.pop(i - 2))
            totals[n] = [p if t is None else t + p for t, p in zip(totals[n], parts)]
    shares = [finish(n, *totals[n]) for n in range(PER_STEP)]
    rq[...] += sum(s[0] for s in shares)
    rkv[:RANK] += sum(s[1] for s in shares)
    rkv[RANK:] += sum(s[2] for s in shares)

    if last:
        @pl.when(pl.program_id(0) == pl.num_programs(0) - 1)
        def _():
            to_prev[...] = rkv[:, :slab].astype(BF16)
            to_next[...] = rkv[:, 2 * slab:].astype(BF16)


def whole(x):
    return pl.BlockSpec(x.shape, lambda *_: (0,) * len(x.shape))


def attend_chunk(h0, heads, last, shared, own, ups, halo, early, carried):
    slab = own[0].shape[1]
    across = own[0].shape[2]
    first = carried is None
    steps = heads // PER_STEP
    wide = PER_STEP * HEAD
    skipped = early[0].shape[2] // wide if first else 0

    own_spec = pl.BlockSpec((1, slab, wide), lambda h: (0, 0, h0 // PER_STEP + h))

    def halo_specs(skipped):
        return [
            pl.BlockSpec((1, slab, wide), lambda h, kind=kind: (kind, 0, jnp.maximum(h - skipped, 0)))
            for kind in (0, 1, 0, 1)
        ]

    low_rows = TILE // 2
    low_spec = pl.BlockSpec((2, low_rows, shared[-1].shape[2]), lambda h: (0, slab // low_rows, 0))
    in_specs = [whole(x) for x in shared[:-2]] + [low_spec] * 2 + [own_spec] * 4 + [
        pl.BlockSpec((3, x.shape[1], wide), lambda h: (0, 0, h0 // PER_STEP + h)) for x in ups
    ] + halo_specs(skipped)
    operands = [*shared, *own, *ups, halo[0], halo[0], halo[1], halo[1]]
    if first:
        in_specs += [
            pl.BlockSpec((1, slab, wide), lambda h, kind=kind: (kind, 0, 0)) for kind in (0, 1, 0, 1)
        ]
        operands += [early[0], early[0], early[1], early[1]]
    aliases = {}
    if not first:
        attended, rq, rkv = carried
        aliases = {len(operands) + 2: 0}
        operands += [rq, rkv, attended]
        in_specs += [whole(rq), whole(rkv), pl.BlockSpec(memory_space=pl.ANY)]
    rq_shape = jax.ShapeDtypeStruct((RANK, slab), F32)
    rkv_shape = jax.ShapeDtypeStruct((2 * RANK, 3 * slab), F32)
    sent_shape = jax.ShapeDtypeStruct((2 * RANK, slab), BF16)
    return pl.pallas_call(
        functools.partial(attend_kernel, first, last, slab),
        grid=(steps,),
        in_specs=in_specs,
        out_specs=[
            own_spec,
            pl.BlockSpec((3, RANK, wide), lambda h: (0, 0, h)),
            whole(rq_shape),
            whole(rkv_shape),
        ] + [whole(sent_shape)] * (2 * last),
        out_shape=[
            jax.ShapeDtypeStruct((1, slab, across), BF16),
            jax.ShapeDtypeStruct((3, RANK, heads * HEAD), F32),
            rq_shape,
            rkv_shape,
        ] + [sent_shape] * (2 * last),
        scratch_shapes=[
            pltpu.VMEM((PER_STEP, slab, HEAD), BF16),
            pltpu.VMEM((PER_STEP, 3 * slab, HEAD), BF16),
            pltpu.VMEM((PER_STEP, 3 * slab, 2 * HEAD), BF16),
            pltpu.VMEM((PER_STEP, 3 * slab, HEAD), BF16),
            pltpu.VMEM((PER_STEP, 3 * RANK, slab), BF16),
            pltpu.VMEM((PER_STEP, 2 * RANK, slab), BF16),
            pltpu.VMEM((PER_STEP, slab, 2 * HEAD), F32),
        ],
        input_output_aliases=aliases,
        compiler_params=pltpu.CompilerParams(
            dimension_semantics=("arbitrary",), vmem_limit_bytes=48 << 20
        ),
        name=f"attend_{h0}",
    )(*operands)


def prologue_kernel(step, x, shift_scale, down, x_mod, low, low_sent, low0_t, down_s):
    del step
    width = x.shape[2]

    @pl.when(pl.program_id(0) == 0)
    def _():
        down_s[...] = jnp.concatenate(
            [down[2], down[0], down[1], jnp.zeros((RANK, width), BF16)], axis=0
        )

    x_full = x[0].astype(F32)
    centred = x_full - jnp.sum(x_full, axis=1, keepdims=True) * (1.0 / width)
    variance = jnp.sum(centred * centred, axis=1, keepdims=True) * (1.0 / width)
    normed = centred * lax.rsqrt(variance + 1e-06)
    modulated = (normed * (1.0 + shift_scale[0, 1:2, :]) + shift_scale[0, 0:1, :]).astype(BF16)
    x_mod[...] = modulated
    reduced = dot_t(modulated, down_s[...])
    low[...] = reduced.astype(BF16)
    low_sent[...] = reduced.reshape(2, TILE // 2, 4 * RANK).astype(BF16)
    low0_t[...] = reduced.T[RANK:2 * RANK].astype(BF16)


def prologue(hidden, truncation_step, modulation, down):
    _, slab, width = hidden.shape
    hidden, modulation, down = [
        pltpu.with_memory_space_constraint(x, pltpu.HBM) for x in (hidden, modulation, down)
    ]
    return pl.pallas_call(
        prologue_kernel,
        grid_spec=pltpu.PrefetchScalarGridSpec(
            num_scalar_prefetch=1,
            grid=(slab // TILE,),
            in_specs=[
                pl.BlockSpec((1, TILE, width), lambda i, step: (0, i, 0)),
                pl.BlockSpec((1, 2, width), lambda i, step: (step[0], 0, 0)),
                whole(down),
            ],
            out_specs=[
                pl.BlockSpec((TILE, width), lambda i, step: (i, 0)),
                pl.BlockSpec((TILE, 4 * RANK), lambda i, step: (i, 0)),
                pl.BlockSpec((2, TILE // 2, 4 * RANK), lambda i, step: (0, 0, i)),
                pl.BlockSpec((RANK, TILE), lambda i, step: (0, i)),
            ],
            scratch_shapes=[pltpu.VMEM((4 * RANK, width), BF16)],
        ),
        out_shape=[
            jax.ShapeDtypeStruct((slab, width), BF16),
            jax.ShapeDtypeStruct((slab, 4 * RANK), BF16),
            jax.ShapeDtypeStruct((2, TILE // 2, slab // TILE * 4 * RANK), BF16),
            jax.ShapeDtypeStruct((RANK, slab), BF16),
        ],
        compiler_params=pltpu.CompilerParams(
            dimension_semantics=("arbitrary",), vmem_limit_bytes=48 << 20
        ),
        name="prologue",
    )(truncation_step, hidden, modulation, down)


def project_kernel(factor, rq, rkv, from_prev, from_next, x_mod, *refs):
    parts, out = refs[:-1], refs[-1]
    rank_kv = rkv[...] + from_prev[...].astype(F32) + from_next[...].astype(F32)
    hi, lo = split_rows(jnp.concatenate([rq[...], rank_kv], axis=0))
    both = dot(jnp.concatenate([hi, lo], axis=0), x_mod[...])
    down = ((both[:3 * RANK] + both[3 * RANK:]) * factor).astype(BF16)
    columns = x_mod.shape[1] // HEAD
    tiles = 3 * RANK // 16
    first = pl.program_id(0) * (columns * tiles)
    for c in range(columns):
        for r in range(tiles):
            out[first + c * tiles + r] = down[16 * r:16 * r + 16, c * HEAD:(c + 1) * HEAD]

    @pl.when(pl.program_id(0) == pl.num_programs(0) - 1)
    def _():
        at = pl.num_programs(0) * (columns * tiles)
        for part in parts:
            for c in range(part.shape[2] // HEAD):
                for r in range(tiles):
                    rows = slice(16 * (r % 2), 16 * (r % 2) + 16)
                    piece = part[r // 2, rows, c * HEAD:(c + 1) * HEAD] * factor
                    out[at + r] = piece.astype(BF16)
                at = at + tiles
        for g in range(PADDING):
            out[at + g] = jnp.zeros((16, HEAD), BF16)


def project(factor, rq, rkv, from_prev, from_next, x_mod, parts):
    slab, width = x_mod.shape
    across = sum(p.shape[2] for p in parts)
    tiles = (width + across) // HEAD * (3 * RANK // 16) + PADDING
    block = width // 4
    shape = jax.ShapeDtypeStruct((tiles, 16, HEAD), BF16)
    return pl.pallas_call(
        functools.partial(project_kernel, factor),
        grid=(width // block,),
        in_specs=[
            whole(rq),
            pl.BlockSpec((2 * RANK, slab), lambda i: (0, 1)),
            whole(from_prev),
            whole(from_next),
            pl.BlockSpec((slab, block), lambda i: (0, i)),
        ] + [whole(p) for p in parts],
        out_specs=whole(shape),
        out_shape=shape,
        compiler_params=pltpu.CompilerParams(
            dimension_semantics=("arbitrary",), vmem_limit_bytes=48 << 20
        ),
        name="project",
    )(rq, rkv, from_prev, from_next, x_mod, *parts)


def unpack_kernel(packed, down, up):
    tiles = 3 * RANK // 16
    g = 0
    for out in (down, up):
        for c in range(out.shape[2] // HEAD):
            for r in range(tiles):
                rows = slice(16 * (r % 2), 16 * (r % 2) + 16)
                out[r // 2, rows, c * HEAD:(c + 1) * HEAD] = packed[g].astype(F32)
                g += 1


def unpack(packed, width, across):
    shapes = [jax.ShapeDtypeStruct((3, RANK, n), F32) for n in (width, across)]
    return pl.pallas_call(unpack_kernel, out_shape=shapes, name="unpack")(packed)


def neighbours(before, after, axis):
    count = lax.axis_size(axis)
    up = [(i, (i + 1) % count) for i in range(count)]
    down = [(j, i) for i, j in up]
    return lax.ppermute(before, axis, up), lax.ppermute(after, axis, down)


def reduce_everywhere(x, batch, tiles):
    count = lax.axis_size(tiles)
    parts = x.reshape(count, x.shape[0] // count * 16, HEAD)
    got = lax.all_to_all(parts, tiles, 0, 0, tiled=True)
    mine = jnp.sum(got.astype(F32), axis=0).astype(BF16)
    peers = lax.axis_size(batch)
    one, two, three = [
        lax.ppermute(mine, batch, [(i, i ^ d) for i in range(peers)]).astype(F32) for d in (1, 2, 3)
    ]
    total = ((mine.astype(F32) + one) + (two + three)).astype(BF16)
    spread = jnp.broadcast_to(total[None], (count,) + total.shape)
    return lax.all_to_all(spread, tiles, 0, 0, tiled=True).reshape(x.shape)


def per_device(
    hidden,
    frozen_queries,
    frozen_keys,
    frozen_values,
    reward_output_gradient,
    truncation_step,
    modulation,
    adapter_down_weight,
    adapter_up_weight,
    window,
):
    slab = hidden.shape[1]
    width = hidden.shape[2]
    across = frozen_queries.shape[2]
    bounds = []
    h0 = 0
    for heads in CHUNKS:
        bounds.append((h0, heads))
        h0 += heads

    def frozen_part(h0, heads):
        columns = slice(h0 * HEAD, (h0 + heads) * HEAD)
        return jnp.concatenate([frozen_keys[:, :, columns], frozen_values[:, :, columns]], axis=0)

    part = frozen_part(0, EARLY)
    early = neighbours(part, part, "tiles")
    x_mod, low, low_sent, low0_t = prologue(
        hidden, truncation_step, modulation, adapter_down_weight.transpose(0, 2, 1)
    )
    bounds[0] = (EARLY, CHUNKS[0] - EARLY)
    parts = [frozen_part(*b) for b in bounds]
    *early, low_sent = lax.optimization_barrier((*early, low_sent))
    parts[0] = jnp.concatenate([parts[0], low_sent], axis=1)
    bounds[0] = (0, CHUNKS[0])
    parts = lax.optimization_barrier(parts)
    halos = [neighbours(part, part, "tiles") for part in parts]

    up = adapter_up_weight
    pad = lambda x, before: jnp.pad(x, ((before, 3 * RANK - before), (0, 0)))
    up_wide = jnp.stack([pad(up[0], RANK), pad(up[1], 2 * RANK), pad(up[2], 0)])
    bias = tile_bias(window, lax.axis_index("tiles"), lax.axis_size("tiles"))
    shared = (bias, low, low0_t, *halos[0])
    own = (frozen_queries, frozen_keys, frozen_values, reward_output_gradient)
    carried = None
    grad_up_parts = []
    for i, ((h0, heads), halo) in enumerate(zip(bounds, halos)):
        attended, grad_up, rq, rkv, *sent = attend_chunk(
            h0, heads, i == len(bounds) - 1, shared, own, (up_wide, up), halo, early, carried
        )
        carried = (attended, rq, rkv)
        grad_up_parts.append(grad_up)

    norm_factor = 1.0 / math.sqrt(
        hidden.shape[0] * lax.axis_size("batch") * slab * lax.axis_size("tiles")
    )
    to_prev, to_next = sent
    from_prev, from_next = neighbours(to_next, to_prev, "tiles")
    packed = project(norm_factor, rq, rkv, from_prev, from_next, x_mod, grad_up_parts)
    packed = reduce_everywhere(packed, "batch", "tiles")
    grad_down, grad_up = unpack(packed, width, across)
    return (attended, grad_down.transpose(0, 2, 1), grad_up)


def solution(mesh):
    placed = (
        P("batch", "tiles", None),
        P("batch", "tiles", None),
        P("batch", "tiles", None),
        P("batch", "tiles", None),
        P("batch", "tiles", None),
        P("batch"),
        P(),
        P(),
        P(),
        P("tiles", None),
    )
    return jax.shard_map(
        per_device,
        mesh=mesh,
        in_specs=placed,
        out_specs=(P("batch", "tiles", None), P(), P()),
        check_vma=False,
    )
```

time: 193 us -> 176 us (0.912)
  blocking collectives: 63.8 us -> 44.1 us
  starting transfers between devices: 29.5 us -> 36.3 us
  other arithmetic: 9.76 us -> 4.59 us
  matrix products: 3.86 us -> 0 us
  Pallas kernels: 56.9 us -> 59.6 us
  waiting for transfers between devices: 21.5 us -> 24.2 us
    all_to_all x1, blocking collectives: 36.2 us -> 22.7 us  [reduce_everywhere(): got = lax.all_to_all(parts, tiles, 0, 0, tiled=True)]
    all_to_all x1 -> x0, blocking collectives: 6.84 us -> none  [reduce_everywhere(): got = lax.all_to_all(spread, batch, 0, 0, tiled=True)]
    ppermute x10 -> x13, starting transfers between devices: 29.5 us -> 36.3 us  [the longest x10 34.3 us: neighbours(): return (lax.ppermute(before, axis, up), lax.ppermute(after, axis, down))]
    dot_general x2 -> x0, matrix products: 3.86 us -> none  [the longest x1 2.67 us: per_device(): jnp.dot(jnp.concatenate([hi, lo], axis=0), x_mod, preferred_element_type=...]
    reduce_sum x4 -> x1, other arithmetic: 3.66 us -> 0.14 us  [reduce_everywhere(): mine = jnp.sum(got.astype(F32), axis=0).astype(BF16)]
    pallas_call x3 -> x6, Pallas kernels: 56.9 us -> 59.6 us  [the longest x3 50.1 us: attend_chunk(): pl.pallas_call(functools.partial(attend_kernel, first, last, slab), grid=...]
    ppermute x10 -> x13, waiting for transfers between devices: 21.5 us -> 24.2 us  [the longest x10 21.7 us: neighbours(): return (lax.ppermute(before, axis, up), lax.ppermute(after, axis, down))]
    reshape x4 -> x0, local copies, waits for them, and re-layouts: 2.52 us -> none  [the longest x1 1.19 us: per_device(): grad_down = summed[:split].reshape(3, RANK, width).transpose(0, 2, 1)]
  transfers between devices with their start and end apart: 10 -> 13, of which waited for: 6 -> 4; matrix products, arithmetic and copies ran while one was open for 2% -> 3% of each run, Pallas kernels for 20% -> 26%
where the time goes in v2:
time: 176 us
  Pallas kernels  59.6 us (34%)
  blocking collectives  44.1 us (25%)
  starting transfers between devices  36.3 us (21%)
  waiting for transfers between devices  24.2 us (14%)
  local copies, waits for them, and re-layouts  5.68 us (3%)
  other arithmetic  4.59 us (3%)
    pallas_call x3, Pallas kernels, attend_chunk(): pl.pallas_call(functools.partial(attend_kernel, first, last, slab), grid=...  50.1 us
    ppermute x10, starting transfers between devices, neighbours(): return (lax.ppermute(before, axis, up), lax.ppermute(after, axis, down))  34.3 us
    all_to_all x1, blocking collectives, reduce_everywhere(): got = lax.all_to_all(parts, tiles, 0, 0, tiled=True)  22.7 us
    ppermute x10, waiting for transfers between devices, neighbours(): return (lax.ppermute(before, axis, up), lax.ppermute(after, axis, down))  21.7 us
    all_to_all x1, blocking collectives, reduce_everywhere(): return lax.all_to_all(spread, tiles, 0, 0, tiled=True).reshape(x.shape)  21.4 us
    pallas_call x1, Pallas kernels, prologue(): pl.pallas_call(prologue_kernel, grid_spec=pltpu.PrefetchScalarGridSpec(nu...  5.32 us
  transfers between devices with their start and end apart: 13, of which 4 were waited for; matrix products, arithmetic and copies ran while one was open for 3% of the time, Pallas kernels for 26%

profile of v2, /device:TPU:0, one launch (start us, length us, event | category | flops | bytes accessed | tf_op | source)
XLA Modules:
  0.0 175.9 jit_solution(7948993672744446900)
XLA Ops:
  0.6 1.3 fusion.9
  2.0 1.7 collective-permute-start
  3.7 7.5 %collective-permute-start.1 = (bf16[2,512,256]{2,1,0:T(8,128)(2,1)S(1)}, bf16[2,512,256]{2,1,0:T(8,128)(2,1)S(1)}, u32[]{:S(2)}, u32[]{:S(2)}) collective-permute-start(bf16[2,512,256]{2,1,0:T(8,128)(2,1)S(1)} %pad_maximum_fusion.3), channel_id=1, source_target_pairs={{1,0},{2,1},{3,2},{4,3},{5,4},{6,5},{7,6},{8,7},{9,8},{10,9},{11,1... | collective-permute-start | bytes 1572872 | tf_op jit(solution)/shard_map/ppermute | solution.py:398
  12.7 5.3 %prologue.1 = (bf16[512,3072]{1,0:T(8,128)(2,1)S(1)}, bf16[512,128]{1,0:T(8,128)(2,1)S(1)}, bf16[2,64,512]{2,1,0:T(8,128)(2,1)S(1)}, bf16[32,512]{1,0:T(8,128)(2,1)S(1)}) custom-call(s32[1]{0:T(128)S(6)} %copy.21.step, bf16[1,512,3072]{2,1,0:T(8,128)(2,1)} %x.7, f32[50,2,3072]{2,1,0:T(2,128)} %shift_scale.1, bf16[3,32,3072]{2,1,0:T(8,128)(2,1)} %bitcast.26), custom_call_target="tpu_custom_call" | custom-call | tf_op jit(solution)/shard_map/prologue/pallas_call | solution.py:295
  18.2 1.4 copy-done.3
  19.6 1.1 pad_maximum_fusion.2
  20.8 2.2 %collective-permute-done.refs_15_.refs_16_ = bf16[2,512,256]{2,1,0:T(8,128)(2,1)S(1)} collective-permute-done((bf16[2,512,256]{2,1,0:T(8,128)(2,1)S(1)}, bf16[2,512,256]{2,1,0:T(8,128)(2,1)S(1)}, u32[]{:S(2)}, u32[]{:S(2)}) %collective-permute-start) | collective-permute-done | bytes 524320 | tf_op jit(solution)/shard_map/ppermute | solution.py:398
  23.8 1.1 pad_maximum_fusion
  26.0 7.7 %collective-permute-start.3 = (bf16[2,576,512]{2,1,0:T(8,128)(2,1)}, bf16[2,576,512]{2,1,0:T(8,128)(2,1)S(1)}, u32[]{:S(2)}, u32[]{:S(2)}) collective-permute-start(bf16[2,576,512]{2,1,0:T(8,128)(2,1)} %pad_maximum_fusion), channel_id=1, source_target_pairs={{1,0},{2,1},{3,2},{4,3},{5,4},{6,5},{7,6},{8,7},{9,8},{10,9},{11,1... | collective-permute-start | bytes 3538952 | tf_op jit(solution)/shard_map/ppermute | solution.py:398
  33.7 7.7 %collective-permute-start.7 = (bf16[2,512,512]{2,1,0:T(8,128)(2,1)}, bf16[2,512,512]{2,1,0:T(8,128)(2,1)}, u32[]{:S(2)}, u32[]{:S(2)}) collective-permute-start(bf16[2,512,512]{2,1,0:T(8,128)(2,1)} %pad_maximum_fusion.2), channel_id=1, source_target_pairs={{1,0},{2,1},{3,2},{4,3},{5,4},{6,5},{7,6},{8,7},{9,8},{10,9},{11,1... | collective-permute-start | bytes 3145736 | tf_op jit(solution)/shard_map/ppermute | solution.py:398
  42.5 17.3 %collective-permute-done.2.refs_3_.refs_11_.refs_12_ = bf16[2,576,512]{2,1,0:T(8,128)(2,1)S(1)} collective-permute-done((bf16[2,576,512]{2,1,0:T(8,128)(2,1)}, bf16[2,576,512]{2,1,0:T(8,128)(2,1)S(1)}, u32[]{:S(2)}, u32[]{:S(2)}) %collective-permute-start.2) | collective-permute-done | bytes 1179680 | tf_op jit(solution)/shard_map/ppermute | solution.py:398
  59.7 1.8 %collective-permute-start.5 = (bf16[2,512,256]{2,1,0:T(8,128)(2,1)}, bf16[2,512,256]{2,1,0:T(8,128)(2,1)S(1)}, u32[]{:S(2)}, u32[]{:S(2)}) collective-permute-start(bf16[2,512,256]{2,1,0:T(8,128)(2,1)} %pad_maximum_fusion.4), channel_id=1, source_target_pairs={{1,0},{2,1},{3,2},{4,3},{5,4},{6,5},{7,6},{8,7},{9,8},{10,9},{11,1... | collective-permute-start | bytes 1572872 | tf_op jit(solution)/shard_map/ppermute | solution.py:398
  61.6 1.0 pad_bitcast_fusion
  62.8 24.1 %attend_0.1 = (bf16[1,512,1536]{2,1,0:T(8,128)(2,1)}, f32[3,32,768]{2,1,0:T(8,128)S(1)}, f32[32,512]{1,0:T(8,128)S(1)}, f32[64,1536]{1,0:T(8,128)S(1)}) custom-call(f32[4,1536]{1,0:T(4,128)S(1)} %bitcast.22, bf16[512,128]{1,0:T(8,128)(2,1)S(1)} %get-tuple-element.29.refs_1_, bf16[32,512]{1,0:T(8,128)(2,1)S(1)} %get-tuple-element.30.refs_2_, ...), custom_call_target="tpu_custom_call" | custom-call | tf_op jit(solution)/shard_map/attend_0/pallas_call | solution.py:235
  86.9 17.0 %attend_6.1 = (bf16[1,512,1536]{2,1,0:T(8,128)(2,1)}, f32[3,32,512]{2,1,0:T(8,128)S(1)}, f32[32,512]{1,0:T(8,128)S(1)}, f32[64,1536]{1,0:T(8,128)S(1)}) custom-call(f32[4,1536]{1,0:T(4,128)S(1)} %bitcast.23, bf16[512,128]{1,0:T(8,128)(2,1)S(1)} %get-tuple-element.29.refs_1_, ...), custom_call_target="tpu_custom_call", output_to_operand_aliasing={{0}: (17, {})} | custom-call | tf_op jit(solution)/shard_map/attend_6/pallas_call | solution.py:235
  104.0 9.1 %attend_10.1 = (bf16[1,512,1536]{2,1,0:T(8,128)(2,1)}, f32[3,32,256]{2,1,0:T(8,128)S(1)}, f32[32,512]{1,0:T(8,128)S(1)}, f32[64,1536]{1,0:T(8,128)S(1)}, bf16[64...) custom-call(f32[4,1536]{1,0:T(4,128)S(1)} %bitcast.24, ...), custom_call_target="tpu_custom_call", output_to_operand_aliasing={{0}: (17, {})} | custom-call | tf_op jit(solution)/shard_map/attend_10/pallas_call | solution.py:235
  113.2 7.5 %collective-permute-start.9 = (bf16[64,512]{1,0:T(8,128)(2,1)S(1)}, bf16[64,512]{1,0:T(8,128)(2,1)S(1)}, u32[]{:S(2)}, u32[]{:S(2)}) collective-permute-start(bf16[64,512]{1,0:T(8,128)(2,1)S(1)} %get-tuple-element.48), channel_id=1, source_target_pairs={{1,0},{2,1},{3,2},{4,3},{5,4},{6,5},{7,6},{8,7},{9,8},{10,9},{11,1... | collective-permute-start | bytes 196616 | tf_op jit(solution)/shard_map/ppermute | solution.py:398
  120.8 2.2 %collective-permute-done.8.from_prev = bf16[64,512]{1,0:T(8,128)(2,1)S(1)} collective-permute-done((bf16[64,512]{1,0:T(8,128)(2,1)S(1)}, bf16[64,512]{1,0:T(8,128)(2,1)S(1)}, u32[]{:S(2)}, u32[]{:S(2)}) %collective-permute-start.8) | collective-permute-done | bytes 65568 | tf_op jit(solution)/shard_map/ppermute | solution.py:398
  123.0 1.7 project.1
  124.7 22.7 %all_to_all.10 = bf16[32,112,128]{2,1,0:T(8,128)(2,1)S(1)} all-to-all(bf16[32,112,128]{2,1,0:T(8,128)(2,1)S(1)} %bitcast.21), channel_id=1, replica_groups=mesh['batch'=4,'tiles'=32] {'tiles'}, dimensions={0} | all-to-all | bytes 1835008 | tf_op jit(solution)/shard_map/all_to_all | solution.py:404
  148.3 1.2 collective-permute-start.12
  149.5 2.4 %collective-permute-done.11 = bf16[112,128]{1,0:T(8,128)(2,1)S(1)} collective-permute-done((bf16[112,128]{1,0:T(8,128)(2,1)S(1)}, bf16[112,128]{1,0:T(8,128)(2,1)S(1)}, u32[]{:S(2)}, u32[]{:S(2)}) %collective-permute-start.11) | collective-permute-done | bytes 28704 | tf_op jit(solution)/shard_map/ppermute | solution.py:408
  152.0 21.4 %all_to_all.11 = bf16[32,112,128]{2,1,0:T(8,128)(2,1)} all-to-all(bf16[32,112,128]{2,1,0:T(8,128)(2,1)S(1)} %broadcast_in_dim.43), channel_id=1, replica_groups=mesh['batch'=4,'tiles'=32] {'tiles'}, dimensions={0} | all-to-all | bytes 1835008 | tf_op jit(solution)/shard_map/all_to_all | solution.py:412
  173.4 2.5 %unpack.1 = (f32[3,32,3072]{2,1,0:T(8,128)}, f32[3,32,1536]{2,1,0:T(8,128)}) custom-call(bf16[224,16,128]{2,1,0:T(8,128)(2,1)} %bitcast.25), custom_call_target="tpu_custom_call" | custom-call | tf_op jit(solution)/shard_map/unpack/pallas_call | solution.py:391
  (57 shorter events, 5.5 us)
Async XLA Ops:
  2.0 21.0 %collective-permute-start = (bf16[2,512,256]{2,1,0:T(8,128)(2,1)S(1)}, bf16[2,512,256]{2,1,0:T(8,128)(2,1)S(1)}, u32[]{:S(2)}, u32[]{:S(2)}) collective-permute-start(bf16[2,512,256]{2,1,0:T(8,128)(2,1)S(1)} %pad_maximum_fusion.3), channel_id=1, source_target_pairs={{0,1},{1,2},{2,3},{3,4},{4,5},{5,6},{6,7},{7,8},{8,9},{9,10},{10,1... | collective-permute-start | bytes 1572872 | tf_op jit(solution)/shard_map/ppermute | solution.py:398
  3.7 19.3 %collective-permute-start.1 = (bf16[2,512,256]{2,1,0:T(8,128)(2,1)S(1)}, bf16[2,512,256]{2,1,0:T(8,128)(2,1)S(1)}, u32[]{:S(2)}, u32[]{:S(2)}) collective-permute-start(bf16[2,512,256]{2,1,0:T(8,128)(2,1)S(1)} %pad_maximum_fusion.3), channel_id=1, source_target_pairs={{1,0},{2,1},{3,2},{4,3},{5,4},{6,5},{7,6},{8,7},{9,8},{10,9},{11,1... | collective-permute-start | bytes 1572872 | tf_op jit(solution)/shard_map/ppermute | solution.py:398
  11.2 13.7 %copy-start.10 = (s32[12]{0:T(128)}, s32[12]{0:T(128)S(1)}, u32[]{:S(2)}) copy-start(s32[12]{0:T(128)S(1)} %get-tuple-element.68) | copy-start | bytes 148
  11.2 13.7 %copy-start.11 = (s32[12]{0:T(128)}, s32[12]{0:T(128)S(1)}, u32[]{:S(2)}) copy-start(s32[12]{0:T(128)S(1)} %get-tuple-element.69) | copy-start | bytes 148
  12.7 5.4 %copy-start.7 = (bf16[1,512,1536]{2,1,0:T(8,128)(2,1)S(1)}, bf16[1,512,1536]{2,1,0:T(8,128)(2,1)}, u32[]{:S(2)}) copy-start(bf16[1,512,1536]{2,1,0:T(8,128)(2,1)} %refs_6_.5) | copy-start | bytes 4718596
  12.7 5.4 %copy-start.8 = (bf16[1,512,1536]{2,1,0:T(8,128)(2,1)S(1)}, bf16[1,512,1536]{2,1,0:T(8,128)(2,1)}, u32[]{:S(2)}) copy-start(bf16[1,512,1536]{2,1,0:T(8,128)(2,1)} %refs_7_.5) | copy-start | bytes 4718596
  18.0 1.6 copy-start.3
  20.7 4.2 %copy-start.9 = (s32[4,27]{1,0:T(4,128)S(1)}, s32[4,27]{1,0:T(4,128)}, u32[]{:S(2)}) copy-start(s32[4,27]{1,0:T(4,128)} %param.19) | copy-start | bytes 1300
  20.7 4.6 %copy-start.2 = (bf16[3,32,1536]{2,1,0:T(8,128)(2,1)S(1)}, bf16[3,32,1536]{2,1,0:T(8,128)(2,1)}, u32[]{:S(2)}) copy-start(bf16[3,32,1536]{2,1,0:T(8,128)(2,1)} %refs_10_.5) | copy-start | bytes 884740
  24.9 34.8 %collective-permute-start.2 = (bf16[2,576,512]{2,1,0:T(8,128)(2,1)}, bf16[2,576,512]{2,1,0:T(8,128)(2,1)S(1)}, u32[]{:S(2)}, u32[]{:S(2)}) collective-permute-start(bf16[2,576,512]{2,1,0:T(8,128)(2,1)} %pad_maximum_fusion), channel_id=1, source_target_pairs={{0,1},{1,2},{2,3},{3,4},{4,5},{5,6},{6,7},{7,8},{8,9},{9,10},{10,1... | collective-permute-start | bytes 3538952 | tf_op jit(solution)/shard_map/ppermute | solution.py:398
  26.0 36.8 %collective-permute-start.3 = (bf16[2,576,512]{2,1,0:T(8,128)(2,1)}, bf16[2,576,512]{2,1,0:T(8,128)(2,1)S(1)}, u32[]{:S(2)}, u32[]{:S(2)}) collective-permute-start(bf16[2,576,512]{2,1,0:T(8,128)(2,1)} %pad_maximum_fusion), channel_id=1, source_target_pairs={{1,0},{2,1},{3,2},{4,3},{5,4},{6,5},{7,6},{8,7},{9,8},{10,9},{11,1... | collective-permute-start | bytes 3538952 | tf_op jit(solution)/shard_map/ppermute | solution.py:398
  33.7 53.1 %collective-permute-start.6 = (bf16[2,512,512]{2,1,0:T(8,128)(2,1)}, bf16[2,512,512]{2,1,0:T(8,128)(2,1)}, u32[]{:S(2)}, u32[]{:S(2)}) collective-permute-start(bf16[2,512,512]{2,1,0:T(8,128)(2,1)} %pad_maximum_fusion.2), channel_id=1, source_target_pairs={{0,1},{1,2},{2,3},{3,4},{4,5},{5,6},{6,7},{7,8},{8,9},{9,10},{10,1... | collective-permute-start | bytes 3145736 | tf_op jit(solution)/shard_map/ppermute | solution.py:398
  33.7 53.1 %collective-permute-start.7 = (bf16[2,512,512]{2,1,0:T(8,128)(2,1)}, bf16[2,512,512]{2,1,0:T(8,128)(2,1)}, u32[]{:S(2)}, u32[]{:S(2)}) collective-permute-start(bf16[2,512,512]{2,1,0:T(8,128)(2,1)} %pad_maximum_fusion.2), channel_id=1, source_target_pairs={{1,0},{2,1},{3,2},{4,3},{5,4},{6,5},{7,6},{8,7},{9,8},{10,9},{11,1... | collective-permute-start | bytes 3145736 | tf_op jit(solution)/shard_map/ppermute | solution.py:398
  42.4 61.5 %collective-permute-start.4 = (bf16[2,512,256]{2,1,0:T(8,128)(2,1)}, bf16[2,512,256]{2,1,0:T(8,128)(2,1)S(1)}, u32[]{:S(2)}, u32[]{:S(2)}) collective-permute-start(bf16[2,512,256]{2,1,0:T(8,128)(2,1)} %pad_maximum_fusion.4), channel_id=1, source_target_pairs={{0,1},{1,2},{2,3},{3,4},{4,5},{5,6},{6,7},{7,8},{8,9},{9,10},{10,1... | collective-permute-start | bytes 1572872 | tf_op jit(solution)/shard_map/ppermute | solution.py:398
  59.7 44.2 %collective-permute-start.5 = (bf16[2,512,256]{2,1,0:T(8,128)(2,1)}, bf16[2,512,256]{2,1,0:T(8,128)(2,1)S(1)}, u32[]{:S(2)}, u32[]{:S(2)}) collective-permute-start(bf16[2,512,256]{2,1,0:T(8,128)(2,1)} %pad_maximum_fusion.4), channel_id=1, source_target_pairs={{1,0},{2,1},{3,2},{4,3},{5,4},{6,5},{7,6},{8,7},{9,8},{10,9},{11,1... | collective-permute-start | bytes 1572872 | tf_op jit(solution)/shard_map/ppermute | solution.py:398
  61.6 1.2 copy-start.6
  62.8 24.1 %copy-start = (bf16[3,128,1536]{2,1,0:T(8,128)(2,1)}, bf16[3,128,1536]{2,1,0:T(8,128)(2,1)S(1)}, u32[]{:S(2)}) copy-start(bf16[3,128,1536]{2,1,0:T(8,128)(2,1)S(1)} %pad_maximum_fusion.1.refs_9_) | copy-start | bytes 3538948
  86.9 17.0 %copy-start.1 = (bf16[3,128,1536]{2,1,0:T(8,128)(2,1)S(1)}, bf16[3,128,1536]{2,1,0:T(8,128)(2,1)}, u32[]{:S(2)}) copy-start(bf16[3,128,1536]{2,1,0:T(8,128)(2,1)} %copy-done) | copy-start | bytes 3538948
  103.9 19.1 %copy-start.4 = (bf16[512,3072]{1,0:T(8,128)(2,1)S(1)}, bf16[512,3072]{1,0:T(8,128)(2,1)}, u32[]{:S(2)}) copy-start(bf16[512,3072]{1,0:T(8,128)(2,1)} %copy-done.3) | copy-start | bytes 9437188
  113.0 10.0 %collective-permute-start.8 = (bf16[64,512]{1,0:T(8,128)(2,1)S(1)}, bf16[64,512]{1,0:T(8,128)(2,1)S(1)}, u32[]{:S(2)}, u32[]{:S(2)}) collective-permute-start(bf16[64,512]{1,0:T(8,128)(2,1)S(1)} %get-tuple-element.47), channel_id=1, source_target_pairs={{0,1},{1,2},{2,3},{3,4},{4,5},{5,6},{6,7},{7,8},{8,9},{9,10},{10,1... | collective-permute-start | bytes 196616 | tf_op jit(solution)/shard_map/ppermute | solution.py:398
  113.2 9.8 %collective-permute-start.9 = (bf16[64,512]{1,0:T(8,128)(2,1)S(1)}, bf16[64,512]{1,0:T(8,128)(2,1)S(1)}, u32[]{:S(2)}, u32[]{:S(2)}) collective-permute-start(bf16[64,512]{1,0:T(8,128)(2,1)S(1)} %get-tuple-element.48), channel_id=1, source_target_pairs={{1,0},{2,1},{3,2},{4,3},{5,4},{6,5},{7,6},{8,7},{9,8},{10,9},{11,1... | collective-permute-start | bytes 196616 | tf_op jit(solution)/shard_map/ppermute | solution.py:398
  147.5 2.0 %collective-permute-start.10 = (bf16[112,128]{1,0:T(8,128)(2,1)S(1)}, bf16[112,128]{1,0:T(8,128)(2,1)S(1)}, u32[]{:S(2)}, u32[]{:S(2)}) collective-permute-start(bf16[112,128]{1,0:T(8,128)(2,1)S(1)} %reduce_sum.22), channel_id=1, source_target_pairs={{0,32},{32,0},{64,96},{96,64},{1,33},{33,1},{65,97},{97,65},{2,34}... | collective-permute-start | bytes 86024 | tf_op jit(solution)/shard_map/ppermute | solution.py:408
  147.6 4.2 %collective-permute-start.11 = (bf16[112,128]{1,0:T(8,128)(2,1)S(1)}, bf16[112,128]{1,0:T(8,128)(2,1)S(1)}, u32[]{:S(2)}, u32[]{:S(2)}) collective-permute-start(bf16[112,128]{1,0:T(8,128)(2,1)S(1)} %reduce_sum.22), channel_id=1, source_target_pairs={{0,64},{32,96},{64,0},{96,32},{1,65},{33,97},{65,1},{97,33},{2,66}... | collective-permute-start | bytes 86024 | tf_op jit(solution)/shard_map/ppermute | solution.py:408
  148.3 3.6 %collective-permute-start.12 = (bf16[112,128]{1,0:T(8,128)(2,1)S(1)}, bf16[112,128]{1,0:T(8,128)(2,1)S(1)}, u32[]{:S(2)}, u32[]{:S(2)}) collective-permute-start(bf16[112,128]{1,0:T(8,128)(2,1)S(1)} %reduce_sum.22), channel_id=1, source_target_pairs={{0,96},{32,64},{64,32},{96,0},{1,97},{33,65},{65,33},{97,1},{2,98}... | collective-permute-start | bytes 86024 | tf_op jit(solution)/shard_map/ppermute | solution.py:408
  (1 other events, 0.8 us)

commit v3 on v2

--- a/solution.py
+++ b/solution.py
@@ -14,7 +14,8 @@
 GR = 2
 RANK = 32
 LOG2E = 1.4426950408889634
-EARLY = 2
+EARLY = 4
+ATTEND_FLOPS = 4_600_000_000
 CHUNKS = (6, 4, 2)
 QBLOCK = 512
 PADDING = 8
@@ -77,12 +78,11 @@
 
     @pl.when(pl.program_id(0) == 0)
     def _():
-        half = TILE // 2
         for n in range(PER_STEP):
             vl_s[n, slab:2 * slab, HEAD:] = low_own[...]
             for i, low in ((0, low_prev), (2, low_next)):
-                for g in range(slab // half):
-                    rows = slice(i * slab + g * half, i * slab + (g + 1) * half)
+                for g in range(slab // TILE):
+                    rows = slice(i * slab + g * TILE, i * slab + (g + 1) * TILE)
                     cols = slice(g // 2 * HEAD, (g // 2 + 1) * HEAD)
                     vl_s[n, rows, HEAD:] = low[g % 2, :, cols]
         if first:
@@ -105,7 +105,7 @@
         q_s[n] = (fq[0, :, cols].astype(F32) + dot(low_own[...], up_wide[0, :, cols])).astype(BF16)
         arrived = [halo[0, :, cols] for halo in halos]
         if first:
-            begin = pl.program_id(0) == 0
+            begin = pl.program_id(0) < EARLY // PER_STEP
             arrived = [jnp.where(begin, e[0, :, cols], a) for e, a in zip(early, arrived)]
         sides = (arrived[:2], (fk[0, :, cols], fv[0, :, cols]), arrived[2:])
         up0 = up[0, :, cols]
@@ -212,15 +212,16 @@
             for kind in (0, 1, 0, 1)
         ]
 
-    low_rows = TILE // 2
-    low_spec = pl.BlockSpec((2, low_rows, shared[-1].shape[2]), lambda h: (0, slab // low_rows, 0))
+    low_spec = pl.BlockSpec((2, TILE, shared[-1].shape[2]), lambda h: (0, slab // TILE, 0))
     in_specs = [whole(x) for x in shared[:-2]] + [low_spec] * 2 + [own_spec] * 4 + [
         pl.BlockSpec((3, x.shape[1], wide), lambda h: (0, 0, h0 // PER_STEP + h)) for x in ups
     ] + halo_specs(skipped)
     operands = [*shared, *own, *ups, halo[0], halo[0], halo[1], halo[1]]
     if first:
         in_specs += [
-            pl.BlockSpec((1, slab, wide), lambda h, kind=kind: (kind, 0, 0)) for kind in (0, 1, 0, 1)
+            pl.BlockSpec(
+                (1, slab, wide), lambda h, kind=kind: (kind, 0, jnp.minimum(h, skipped - 1))
+            ) for kind in (0, 1, 0, 1)
         ]
         operands += [early[0], early[0], early[1], early[1]]
     aliases = {}
@@ -261,6 +262,10 @@
         compiler_params=pltpu.CompilerParams(
             dimension_semantics=("arbitrary",), vmem_limit_bytes=48 << 20
         ),
+        cost_estimate=pl.CostEstimate(
+            flops=heads * ATTEND_FLOPS, transcendentals=heads * 3 * slab * slab,
+            bytes_accessed=heads * 10 * slab * HEAD * 2,
+        ),
         name=f"attend_{h0}",
     )(*operands)
 
@@ -283,7 +288,7 @@
     x_mod[...] = modulated
     reduced = dot_t(modulated, down_s[...])
     low[...] = reduced.astype(BF16)
-    low_sent[...] = reduced.reshape(2, TILE // 2, 4 * RANK).astype(BF16)
+    low_sent[0] = reduced.astype(BF16)
     low0_t[...] = reduced.T[RANK:2 * RANK].astype(BF16)
 
 
@@ -305,7 +310,7 @@
             out_specs=[
                 pl.BlockSpec((TILE, width), lambda i, step: (i, 0)),
                 pl.BlockSpec((TILE, 4 * RANK), lambda i, step: (i, 0)),
-                pl.BlockSpec((2, TILE // 2, 4 * RANK), lambda i, step: (0, 0, i)),
+                pl.BlockSpec((1, TILE, 4 * RANK), lambda i, step: (i % 2, 0, i // 2)),
                 pl.BlockSpec((RANK, TILE), lambda i, step: (0, i)),
             ],
             scratch_shapes=[pltpu.VMEM((4 * RANK, width), BF16)],
@@ -313,7 +318,7 @@
         out_shape=[
             jax.ShapeDtypeStruct((slab, width), BF16),
             jax.ShapeDtypeStruct((slab, 4 * RANK), BF16),
-            jax.ShapeDtypeStruct((2, TILE // 2, slab // TILE * 4 * RANK), BF16),
+            jax.ShapeDtypeStruct((2, TILE, slab // TILE // 2 * 4 * RANK), BF16),
             jax.ShapeDtypeStruct((RANK, slab), BF16),
         ],
         compiler_params=pltpu.CompilerParams(

time: 176 us -> 174 us (0.989)
  other arithmetic: 4.59 us -> 2.08 us
  waiting for transfers between devices: 24.2 us -> 26.6 us
    ppermute x10, waiting for transfers between devices: 21.7 us -> 24.2 us  [neighbours(): return (lax.ppermute(before, axis, up), lax.ppermute(after, axis, down))]
  transfers between devices with their start and end apart: 13 -> 13, of which waited for: 4 -> 5; matrix products, arithmetic and copies ran while one was open for 3% -> 1% of each run, Pallas kernels for 26% -> 26%
where the time goes in v3:
time: 174 us; the launch traced here: 173 us
  Pallas kernels  58.6 us (34%)
  blocking collectives  44.1 us (25%)
  starting transfers between devices  36.1 us (21%)
  waiting for transfers between devices  26.6 us (15%)
  local copies, waits for them, and re-layouts  4.14 us (2%)
  other arithmetic  2.08 us (1%)
    pallas_call x3, Pallas kernels, attend_chunk(): pl.pallas_call(functools.partial(attend_kernel, first, last, slab), grid=...  49.1 us
    ppermute x10, starting transfers between devices, neighbours(): return (lax.ppermute(before, axis, up), lax.ppermute(after, axis, down))  34.1 us
    ppermute x10, waiting for transfers between devices, neighbours(): return (lax.ppermute(before, axis, up), lax.ppermute(after, axis, down))  24.2 us
    all_to_all x1, blocking collectives, reduce_everywhere(): got = lax.all_to_all(parts, tiles, 0, 0, tiled=True)  22.7 us
    all_to_all x1, blocking collectives, reduce_everywhere(): return lax.all_to_all(spread, tiles, 0, 0, tiled=True).reshape(x.shape)  21.4 us
    pallas_call x1, Pallas kernels, prologue(): pl.pallas_call(prologue_kernel, grid_spec=pltpu.PrefetchScalarGridSpec(nu...  5.33 us
  transfers between devices with their start and end apart: 13, of which 5 were waited for; matrix products, arithmetic and copies ran while one was open for 1% of the time, Pallas kernels for 26%

profile of v3, /device:TPU:0, one launch (start us, length us, event | category | flops | bytes accessed | tf_op | source)
XLA Modules:
  0.0 173.1 jit_solution(383629381104171425)
XLA Ops:
  0.6 1.7 fusion.11
  2.3 1.1 pad_maximum_fusion.1
  3.4 1.7 collective-permute-start
  5.0 7.4 %collective-permute-start.1 = (bf16[2,512,512]{2,1,0:T(8,128)(2,1)}, bf16[2,512,512]{2,1,0:T(8,128)(2,1)S(1)}, u32[]{:S(2)}, u32[]{:S(2)}) collective-permute-start(bf16[2,512,512]{2,1,0:T(8,128)(2,1)} %pad_maximum_fusion.1), channel_id=1, source_target_pairs={{1,0},{2,1},{3,2},{4,3},{5,4},{6,5},{7,6},{8,7},{9,8},{10,9},{11,1... | collective-permute-start | bytes 3145736 | tf_op jit(solution)/shard_map/ppermute | solution.py:403
  13.8 5.3 %prologue.1 = (bf16[512,3072]{1,0:T(8,128)(2,1)S(1)}, bf16[512,128]{1,0:T(8,128)(2,1)S(1)}, bf16[2,128,256]{2,1,0:T(8,128)(2,1)S(1)}, bf16[32,512]{1,0:T(8,128)(2,1)S(1)}) custom-call(s32[1]{0:T(128)S(6)} %copy.21.step, bf16[1,512,3072]{2,1,0:T(8,128)(2,1)} %x.7, f32[50,2,3072]{2,1,0:T(2,128)} %shift_scale.1, bf16[3,32,3072]{2,1,0:T(8,128)(2,1)} %bitcast.26), custom_call_target="tpu_custom_call" | custom-call | tf_op jit(solution)/shard_map/prologue/pallas_call | solution.py:300
  19.2 1.3 fusion.9
  20.6 0.8 copy-done
  21.4 14.4 %collective-permute-done.refs_15_.refs_16_ = bf16[2,512,512]{2,1,0:T(8,128)(2,1)S(1)} collective-permute-done((bf16[2,512,512]{2,1,0:T(8,128)(2,1)}, bf16[2,512,512]{2,1,0:T(8,128)(2,1)S(1)}, u32[]{:S(2)}, u32[]{:S(2)}) %collective-permute-start) | collective-permute-done | bytes 1048608 | tf_op jit(solution)/shard_map/ppermute | solution.py:403
  35.9 7.7 %collective-permute-start.3 = (bf16[2,640,256]{2,1,0:T(8,128)(2,1)S(1)}, bf16[2,640,256]{2,1,0:T(8,128)(2,1)S(1)}, u32[]{:S(2)}, u32[]{:S(2)}) collective-permute-start(bf16[2,640,256]{2,1,0:T(8,128)(2,1)S(1)} %pad_maximum_fusion.3), channel_id=1, source_target_pairs={{1,0},{2,1},{3,2},{4,3},{5,4},{6,5},{7,6},{8,7},{9,8},{10,9},{11,1... | collective-permute-start | bytes 1966088 | tf_op jit(solution)/shard_map/ppermute | solution.py:403
  44.0 7.7 %collective-permute-start.7 = (bf16[2,512,512]{2,1,0:T(8,128)(2,1)S(1)}, bf16[2,512,512]{2,1,0:T(8,128)(2,1)S(1)}, u32[]{:S(2)}, u32[]{:S(2)}) collective-permute-start(bf16[2,512,512]{2,1,0:T(8,128)(2,1)S(1)} %pad_maximum_fusion.2), channel_id=1, source_target_pairs={{1,0},{2,1},{3,2},{4,3},{5,4},{6,5},{7,6},{8,7},{9,8},{10,9},{11,1... | collective-permute-start | bytes 3145736 | tf_op jit(solution)/shard_map/ppermute | solution.py:403
  51.7 7.6 %collective-permute-done.2.refs_3_.refs_11_.refs_12_ = bf16[2,640,256]{2,1,0:T(8,128)(2,1)S(1)} collective-permute-done((bf16[2,640,256]{2,1,0:T(8,128)(2,1)S(1)}, bf16[2,640,256]{2,1,0:T(8,128)(2,1)S(1)}, u32[]{:S(2)}, u32[]{:S(2)}) %collective-permute-start.2) | collective-permute-done | bytes 655392 | tf_op jit(solution)/shard_map/ppermute | solution.py:403
  59.3 1.7 %collective-permute-start.5 = (bf16[2,512,256]{2,1,0:T(8,128)(2,1)S(1)}, bf16[2,512,256]{2,1,0:T(8,128)(2,1)S(1)}, u32[]{:S(2)}, u32[]{:S(2)}) collective-permute-start(bf16[2,512,256]{2,1,0:T(8,128)(2,1)S(1)} %pad_maximum_fusion.4), channel_id=1, source_target_pairs={{1,0},{2,1},{3,2},{4,3},{5,4},{6,5},{7,6},{8,7},{9,8},{10,9},{11,1... | collective-permute-start | bytes 1572872 | tf_op jit(solution)/shard_map/ppermute | solution.py:403
  61.0 23.6 %attend_0.1 = (bf16[1,512,1536]{2,1,0:T(8,128)(2,1)}, f32[3,32,768]{2,1,0:T(8,128)S(1)}, f32[32,512]{1,0:T(8,128)S(1)}, f32[64,1536]{1,0:T(8,128)S(1)}) custom-call(f32[4,1536]{1,0:T(4,128)S(1)} %bitcast.22, bf16[512,128]{1,0:T(8,128)(2,1)S(1)} %get-tuple-element.29.refs_1_, bf16[32,512]{1,0:T(8,128)(2,1)S(1)} %get-tuple-element.30.refs_2_, ...), custom_call_target="tpu_custom_call" | custom-call | flops 27599998976 | bytes 7864320 | tf_op jit(solution)/shard_map/attend_0/pallas_call | solution.py:236
  84.6 16.6 %attend_6.1 = (bf16[1,512,1536]{2,1,0:T(8,128)(2,1)}, f32[3,32,512]{2,1,0:T(8,128)S(1)}, f32[32,512]{1,0:T(8,128)S(1)}, f32[64,1536]{1,0:T(8,128)S(1)}) custom-call(f32[4,1536]{1,0:T(4,128)S(1)} %bitcast.23, bf16[512,128]{1,0:T(8,128)(2,1)S(1)} %get-tuple-element.29.refs_1_, ...), custom_call_target="tpu_custom_call", output_to_operand_aliasing={{0}: (17, {})} | custom-call | flops 18400000000 | bytes 5242880 | tf_op jit(solution)/shard_map/attend_6/pallas_call | solution.py:236
  101.2 8.9 %attend_10.1 = (bf16[1,512,1536]{2,1,0:T(8,128)(2,1)}, f32[3,32,256]{2,1,0:T(8,128)S(1)}, f32[32,512]{1,0:T(8,128)S(1)}, f32[64,1536]{1,0:T(8,128)S(1)}, bf16[64...) custom-call(f32[4,1536]{1,0:T(4,128)S(1)} %bitcast.24, ...), custom_call_target="tpu_custom_call", output_to_operand_aliasing={{0}: (17, {})} | custom-call | flops 9200000000 | bytes 2621440 | tf_op jit(solution)/shard_map/attend_10/pallas_call | solution.py:236
  110.5 7.5 %collective-permute-start.9 = (bf16[64,512]{1,0:T(8,128)(2,1)S(1)}, bf16[64,512]{1,0:T(8,128)(2,1)S(1)}, u32[]{:S(2)}, u32[]{:S(2)}) collective-permute-start(bf16[64,512]{1,0:T(8,128)(2,1)S(1)} %get-tuple-element.48), channel_id=1, source_target_pairs={{1,0},{2,1},{3,2},{4,3},{5,4},{6,5},{7,6},{8,7},{9,8},{10,9},{11,1... | collective-permute-start | bytes 196616 | tf_op jit(solution)/shard_map/ppermute | solution.py:403
  117.9 2.2 %collective-permute-done.8.from_prev = bf16[64,512]{1,0:T(8,128)(2,1)S(1)} collective-permute-done((bf16[64,512]{1,0:T(8,128)(2,1)S(1)}, bf16[64,512]{1,0:T(8,128)(2,1)S(1)}, u32[]{:S(2)}, u32[]{:S(2)}) %collective-permute-start.8) | collective-permute-done | bytes 65568 | tf_op jit(solution)/shard_map/ppermute | solution.py:403
  120.2 1.7 project.1
  121.9 22.7 %all_to_all.10 = bf16[32,112,128]{2,1,0:T(8,128)(2,1)S(1)} all-to-all(bf16[32,112,128]{2,1,0:T(8,128)(2,1)S(1)} %bitcast.21), channel_id=1, replica_groups=mesh['batch'=4,'tiles'=32] {'tiles'}, dimensions={0} | all-to-all | bytes 1835008 | tf_op jit(solution)/shard_map/all_to_all | solution.py:409
  144.8 0.7 collective-permute-start.11
  145.5 1.2 collective-permute-start.12
  146.7 2.4 %collective-permute-done.11 = bf16[112,128]{1,0:T(8,128)(2,1)S(1)} collective-permute-done((bf16[112,128]{1,0:T(8,128)(2,1)S(1)}, bf16[112,128]{1,0:T(8,128)(2,1)S(1)}, u32[]{:S(2)}, u32[]{:S(2)}) %collective-permute-start.11) | collective-permute-done | bytes 28704 | tf_op jit(solution)/shard_map/ppermute | solution.py:413
  149.2 21.4 %all_to_all.11 = bf16[32,112,128]{2,1,0:T(8,128)(2,1)} all-to-all(bf16[32,112,128]{2,1,0:T(8,128)(2,1)S(1)} %broadcast_in_dim.43), channel_id=1, replica_groups=mesh['batch'=4,'tiles'=32] {'tiles'}, dimensions={0} | all-to-all | bytes 1835008 | tf_op jit(solution)/shard_map/all_to_all | solution.py:417
  170.6 2.5 %unpack.1 = (f32[3,32,3072]{2,1,0:T(8,128)}, f32[3,32,1536]{2,1,0:T(8,128)}) custom-call(bf16[224,16,128]{2,1,0:T(8,128)(2,1)} %bitcast.25), custom_call_target="tpu_custom_call" | custom-call | tf_op jit(solution)/shard_map/unpack/pallas_call | solution.py:396
  (37 shorter events, 2.0 us)
Async XLA Ops:
  2.3 10.2 %copy-start.1 = (s32[4,27]{1,0:T(4,128)S(1)}, s32[4,27]{1,0:T(4,128)}, u32[]{:S(2)}) copy-start(s32[4,27]{1,0:T(4,128)} %param.19) | copy-start | bytes 1300
  3.4 32.4 %collective-permute-start = (bf16[2,512,512]{2,1,0:T(8,128)(2,1)}, bf16[2,512,512]{2,1,0:T(8,128)(2,1)S(1)}, u32[]{:S(2)}, u32[]{:S(2)}) collective-permute-start(bf16[2,512,512]{2,1,0:T(8,128)(2,1)} %pad_maximum_fusion.1), channel_id=1, source_target_pairs={{0,1},{1,2},{2,3},{3,4},{4,5},{5,6},{6,7},{7,8},{8,9},{9,10},{10,1... | collective-permute-start | bytes 3145736 | tf_op jit(solution)/shard_map/ppermute | solution.py:403
  5.0 30.7 %collective-permute-start.1 = (bf16[2,512,512]{2,1,0:T(8,128)(2,1)}, bf16[2,512,512]{2,1,0:T(8,128)(2,1)S(1)}, u32[]{:S(2)}, u32[]{:S(2)}) collective-permute-start(bf16[2,512,512]{2,1,0:T(8,128)(2,1)} %pad_maximum_fusion.1), channel_id=1, source_target_pairs={{1,0},{2,1},{3,2},{4,3},{5,4},{6,5},{7,6},{8,7},{9,8},{10,9},{11,1... | collective-permute-start | bytes 3145736 | tf_op jit(solution)/shard_map/ppermute | solution.py:403
  20.4 1.0 copy-start
  35.8 23.5 %collective-permute-start.2 = (bf16[2,640,256]{2,1,0:T(8,128)(2,1)S(1)}, bf16[2,640,256]{2,1,0:T(8,128)(2,1)S(1)}, u32[]{:S(2)}, u32[]{:S(2)}) collective-permute-start(bf16[2,640,256]{2,1,0:T(8,128)(2,1)S(1)} %pad_maximum_fusion.3), channel_id=1, source_target_pairs={{0,1},{1,2},{2,3},{3,4},{4,5},{5,6},{6,7},{7,8},{8,9},{9,10},{10,1... | collective-permute-start | bytes 1966088 | tf_op jit(solution)/shard_map/ppermute | solution.py:403
  35.9 25.1 %collective-permute-start.3 = (bf16[2,640,256]{2,1,0:T(8,128)(2,1)S(1)}, bf16[2,640,256]{2,1,0:T(8,128)(2,1)S(1)}, u32[]{:S(2)}, u32[]{:S(2)}) collective-permute-start(bf16[2,640,256]{2,1,0:T(8,128)(2,1)S(1)} %pad_maximum_fusion.3), channel_id=1, source_target_pairs={{1,0},{2,1},{3,2},{4,3},{5,4},{6,5},{7,6},{8,7},{9,8},{10,9},{11,1... | collective-permute-start | bytes 1966088 | tf_op jit(solution)/shard_map/ppermute | solution.py:403
  43.9 40.7 %collective-permute-start.6 = (bf16[2,512,512]{2,1,0:T(8,128)(2,1)S(1)}, bf16[2,512,512]{2,1,0:T(8,128)(2,1)S(1)}, u32[]{:S(2)}, u32[]{:S(2)}) collective-permute-start(bf16[2,512,512]{2,1,0:T(8,128)(2,1)S(1)} %pad_maximum_fusion.2), channel_id=1, source_target_pairs={{0,1},{1,2},{2,3},{3,4},{4,5},{5,6},{6,7},{7,8},{8,9},{9,10},{10,1... | collective-permute-start | bytes 3145736 | tf_op jit(solution)/shard_map/ppermute | solution.py:403
  44.0 40.7 %collective-permute-start.7 = (bf16[2,512,512]{2,1,0:T(8,128)(2,1)S(1)}, bf16[2,512,512]{2,1,0:T(8,128)(2,1)S(1)}, u32[]{:S(2)}, u32[]{:S(2)}) collective-permute-start(bf16[2,512,512]{2,1,0:T(8,128)(2,1)S(1)} %pad_maximum_fusion.2), channel_id=1, source_target_pairs={{1,0},{2,1},{3,2},{4,3},{5,4},{6,5},{7,6},{8,7},{9,8},{10,9},{11,1... | collective-permute-start | bytes 3145736 | tf_op jit(solution)/shard_map/ppermute | solution.py:403
  51.7 49.5 %collective-permute-start.4 = (bf16[2,512,256]{2,1,0:T(8,128)(2,1)S(1)}, bf16[2,512,256]{2,1,0:T(8,128)(2,1)S(1)}, u32[]{:S(2)}, u32[]{:S(2)}) collective-permute-start(bf16[2,512,256]{2,1,0:T(8,128)(2,1)S(1)} %pad_maximum_fusion.4), channel_id=1, source_target_pairs={{0,1},{1,2},{2,3},{3,4},{4,5},{5,6},{6,7},{7,8},{8,9},{9,10},{10,1... | collective-permute-start | bytes 1572872 | tf_op jit(solution)/shard_map/ppermute | solution.py:403
  59.3 41.9 %collective-permute-start.5 = (bf16[2,512,256]{2,1,0:T(8,128)(2,1)S(1)}, bf16[2,512,256]{2,1,0:T(8,128)(2,1)S(1)}, u32[]{:S(2)}, u32[]{:S(2)}) collective-permute-start(bf16[2,512,256]{2,1,0:T(8,128)(2,1)S(1)} %pad_maximum_fusion.4), channel_id=1, source_target_pairs={{1,0},{2,1},{3,2},{4,3},{5,4},{6,5},{7,6},{8,7},{9,8},{10,9},{11,1... | collective-permute-start | bytes 1572872 | tf_op jit(solution)/shard_map/ppermute | solution.py:403
  110.2 10.0 %collective-permute-start.8 = (bf16[64,512]{1,0:T(8,128)(2,1)S(1)}, bf16[64,512]{1,0:T(8,128)(2,1)S(1)}, u32[]{:S(2)}, u32[]{:S(2)}) collective-permute-start(bf16[64,512]{1,0:T(8,128)(2,1)S(1)} %get-tuple-element.47), channel_id=1, source_target_pairs={{0,1},{1,2},{2,3},{3,4},{4,5},{5,6},{6,7},{7,8},{8,9},{9,10},{10,1... | collective-permute-start | bytes 196616 | tf_op jit(solution)/shard_map/ppermute | solution.py:403
  110.5 9.7 %collective-permute-start.9 = (bf16[64,512]{1,0:T(8,128)(2,1)S(1)}, bf16[64,512]{1,0:T(8,128)(2,1)S(1)}, u32[]{:S(2)}, u32[]{:S(2)}) collective-permute-start(bf16[64,512]{1,0:T(8,128)(2,1)S(1)} %get-tuple-element.48), channel_id=1, source_target_pairs={{1,0},{2,1},{3,2},{4,3},{5,4},{6,5},{7,6},{8,7},{9,8},{10,9},{11,1... | collective-permute-start | bytes 196616 | tf_op jit(solution)/shard_map/ppermute | solution.py:403
  144.7 2.0 %collective-permute-start.10 = (bf16[112,128]{1,0:T(8,128)(2,1)S(1)}, bf16[112,128]{1,0:T(8,128)(2,1)S(1)}, u32[]{:S(2)}, u32[]{:S(2)}) collective-permute-start(bf16[112,128]{1,0:T(8,128)(2,1)S(1)} %reduce_sum.22), channel_id=1, source_target_pairs={{0,32},{32,0},{64,96},{96,64},{1,33},{33,1},{65,97},{97,65},{2,34}... | collective-permute-start | bytes 86024 | tf_op jit(solution)/shard_map/ppermute | solution.py:413
  144.8 4.2 %collective-permute-start.11 = (bf16[112,128]{1,0:T(8,128)(2,1)S(1)}, bf16[112,128]{1,0:T(8,128)(2,1)S(1)}, u32[]{:S(2)}, u32[]{:S(2)}) collective-permute-start(bf16[112,128]{1,0:T(8,128)(2,1)S(1)} %reduce_sum.22), channel_id=1, source_target_pairs={{0,64},{32,96},{64,0},{96,32},{1,65},{33,97},{65,1},{97,33},{2,66}... | collective-permute-start | bytes 86024 | tf_op jit(solution)/shard_map/ppermute | solution.py:413
  145.5 3.6 %collective-permute-start.12 = (bf16[112,128]{1,0:T(8,128)(2,1)S(1)}, bf16[112,128]{1,0:T(8,128)(2,1)S(1)}, u32[]{:S(2)}, u32[]{:S(2)}) collective-permute-start(bf16[112,128]{1,0:T(8,128)(2,1)S(1)} %reduce_sum.22), channel_id=1, source_target_pairs={{0,96},{32,64},{64,32},{96,0},{1,97},{33,65},{65,33},{97,1},{2,98}... | collective-permute-start | bytes 86024 | tf_op jit(solution)/shard_map/ppermute | solution.py:413

commit v4 on v3

--- a/solution.py
+++ b/solution.py
@@ -14,7 +14,6 @@
 GR = 2
 RANK = 32
 LOG2E = 1.4426950408889634
-EARLY = 4
 ATTEND_FLOPS = 4_600_000_000
 CHUNKS = (6, 4, 2)
 QBLOCK = 512
@@ -63,8 +62,6 @@
     (bias, low_own, low0_t, low_prev, low_next, fq, fk, fv, out_grad, up_wide, up) = refs[:11]
     halos = refs[11:15]
     refs = refs[15:]
-    if first:
-        early, refs = refs[:4], refs[4:]
     if not first:
         rq_in, rkv_in, _ = refs[:3]
         refs = refs[3:]
@@ -73,18 +70,18 @@
     if last:
         to_prev, to_next = refs[:2]
         refs = refs[2:]
-    q_s, k_s, vl_s, kx_s, xb_s, xd_s, cat_s = refs
+    q_s, kl_s, vl_s, xb_s, xd_s, dq_s, cat_s = refs
     scale = 1.0 / math.sqrt(HEAD)
 
     @pl.when(pl.program_id(0) == 0)
     def _():
         for n in range(PER_STEP):
             vl_s[n, slab:2 * slab, HEAD:] = low_own[...]
+            kl_s[n, slab:2 * slab, HEAD:] = low_own[...]
             for i, low in ((0, low_prev), (2, low_next)):
-                for g in range(slab // TILE):
-                    rows = slice(i * slab + g * TILE, i * slab + (g + 1) * TILE)
-                    cols = slice(g // 2 * HEAD, (g // 2 + 1) * HEAD)
-                    vl_s[n, rows, HEAD:] = low[g % 2, :, cols]
+                rows = slice(i * slab, (i + 1) * slab)
+                vl_s[n, rows, HEAD:] = low[...]
+                kl_s[n, rows, HEAD:] = low[...]
         if first:
             rq[...] = jnp.zeros_like(rq)
             rkv[...] = jnp.zeros_like(rkv)
@@ -92,8 +89,6 @@
             rq[...] = rq_in[...]
             rkv[...] = rkv_in[...]
 
-    lane = lax.broadcasted_iota(jnp.int32, (slab, HEAD), 1)
-
     def pair(left, right):
         hi, lo = split_rows(left)
         both = dot(jnp.concatenate([hi, lo], axis=0), right)
@@ -104,32 +99,21 @@
         kv_up = jnp.concatenate([up_wide[1, :, cols], up_wide[2, :, cols]], axis=1)
         q_s[n] = (fq[0, :, cols].astype(F32) + dot(low_own[...], up_wide[0, :, cols])).astype(BF16)
         arrived = [halo[0, :, cols] for halo in halos]
-        if first:
-            begin = pl.program_id(0) < EARLY // PER_STEP
-            arrived = [jnp.where(begin, e[0, :, cols], a) for e, a in zip(early, arrived)]
         sides = (arrived[:2], (fk[0, :, cols], fv[0, :, cols]), arrived[2:])
-        up0 = up[0, :, cols]
-        up0_twice = jnp.concatenate([up0, up0, jnp.zeros((2 * RANK, HEAD), BF16)], axis=0)
         for i, (k_in, v_in) in enumerate(sides):
             rows = slice(i * slab, (i + 1) * slab)
             low = vl_s[n, rows, HEAD:]
             added = dot(low, kv_up)
-            keys = (k_in.astype(F32) + added[:, :HEAD]).astype(BF16)
-            k_s[n, rows, :] = keys
+            kl_s[n, rows, :HEAD] = (k_in.astype(F32) + added[:, :HEAD]).astype(BF16)
             vl_s[n, rows, :HEAD] = (v_in.astype(F32) + added[:, HEAD:]).astype(BF16)
-            ku = dot_t(keys, up0_twice)
-            rest = ku - ku.astype(BF16).astype(F32)
-            kx_s[n, rows, :] = jnp.where(
-                lane < RANK, ku, jnp.where(lane < 2 * RANK, rest, low.astype(F32))
-            ).astype(BF16)
         hi, lo = split_rows(dot_t(up[1, :, cols], q_s[n]))
-        xb_s[n] = jnp.concatenate([hi, lo, low0_t[...]], axis=0)
+        xb_s[n] = jnp.concatenate([hi, lo], axis=0)
         hi, lo = split_rows(dot_t(up[2, :, cols], out_grad[0, :, cols]))
         xd_s[n] = jnp.concatenate([hi, lo], axis=0)
 
     def products(n, rows):
         cols = slice(n * HEAD, (n + 1) * HEAD)
-        scores = dot_t(q_s[n, rows, :], k_s[n])
+        scores = dot_t(q_s[n, rows, :], kl_s[n, :, :HEAD])
         prob_grad = dot_t(out_grad[0, rows, cols], vl_s[n, :, :HEAD])
         return scores, prob_grad
 
@@ -151,19 +135,23 @@
         out = dot(probs_low, vl_s[n])
         attended[0, rows, n * HEAD:(n + 1) * HEAD] = out[:, :HEAD].astype(BF16)
         cat_s[n, rows, :HEAD] = out[:, HEAD:]
-        cat_s[n, rows, HEAD:] = dot(score_grad, kx_s[n])
+        out = dot(score_grad, kl_s[n])
+        hi, lo = split_rows(out[:, :HEAD])
+        dq_s[n, rows, :HEAD] = hi
+        dq_s[n, rows, HEAD:] = lo
+        cat_s[n, rows, HEAD:] = out[:, HEAD:]
         return dot(xd_s[n, :, rows], probs_low), dot(xb_s[n, :, rows], score_grad)
 
     def finish(n, d_total, b_total):
         cols = slice(n * HEAD, (n + 1) * HEAD)
         cat_t = cat_s[n].T
-        c_t = cat_t[:RANK]
-        a_t = cat_t[HEAD:]
-        grad_up[0, :, cols] = pair(b_total[2 * RANK:], k_s[n])
-        grad_up[1, :, cols] = pair(a_t[2 * RANK:3 * RANK], q_s[n])
-        grad_up[2, :, cols] = pair(c_t, out_grad[0, :, cols])
-        return (a_t[:RANK] + a_t[RANK:2 * RANK], b_total[:RANK] + b_total[RANK:2 * RANK],
-                d_total[:RANK] + d_total[RANK:])
+        both = dot(low0_t[...], dq_s[n])
+        grad_up[0, :, cols] = both[:, :HEAD] + both[:, HEAD:]
+        grad_up[1, :, cols] = pair(cat_t[HEAD + 2 * RANK:HEAD + 3 * RANK], q_s[n])
+        grad_up[2, :, cols] = pair(cat_t[:RANK], out_grad[0, :, cols])
+        up0 = up[0, :, cols]
+        return (dot_t(jnp.concatenate([up0, up0], axis=1), dq_s[n]),
+                b_total[:RANK] + b_total[RANK:], d_total[:RANK] + d_total[RANK:])
 
     steps = [(n, slice(r, r + QBLOCK)) for n in range(PER_STEP) for r in range(0, slab, QBLOCK)]
     totals = [[None, None] for _ in range(PER_STEP)]
@@ -196,34 +184,19 @@
     return pl.BlockSpec(x.shape, lambda *_: (0,) * len(x.shape))
 
 
-def attend_chunk(h0, heads, last, shared, own, ups, halo, early, carried):
+def attend_chunk(h0, heads, last, shared, own, ups, halo, carried):
     slab = own[0].shape[1]
     across = own[0].shape[2]
     first = carried is None
     steps = heads // PER_STEP
     wide = PER_STEP * HEAD
-    skipped = early[0].shape[2] // wide if first else 0
 
     own_spec = pl.BlockSpec((1, slab, wide), lambda h: (0, 0, h0 // PER_STEP + h))
-
-    def halo_specs(skipped):
-        return [
-            pl.BlockSpec((1, slab, wide), lambda h, kind=kind: (kind, 0, jnp.maximum(h - skipped, 0)))
-            for kind in (0, 1, 0, 1)
-        ]
-
-    low_spec = pl.BlockSpec((2, TILE, shared[-1].shape[2]), lambda h: (0, slab // TILE, 0))
-    in_specs = [whole(x) for x in shared[:-2]] + [low_spec] * 2 + [own_spec] * 4 + [
+    halo_specs = [pl.BlockSpec((1, slab, wide), lambda h, kind=kind: (kind, 0, h)) for kind in (0, 1)]
+    in_specs = [whole(x) for x in shared] + [own_spec] * 4 + [
         pl.BlockSpec((3, x.shape[1], wide), lambda h: (0, 0, h0 // PER_STEP + h)) for x in ups
-    ] + halo_specs(skipped)
+    ] + halo_specs * 2
     operands = [*shared, *own, *ups, halo[0], halo[0], halo[1], halo[1]]
-    if first:
-        in_specs += [
-            pl.BlockSpec(
-                (1, slab, wide), lambda h, kind=kind: (kind, 0, jnp.minimum(h, skipped - 1))
-            ) for kind in (0, 1, 0, 1)
-        ]
-        operands += [early[0], early[0], early[1], early[1]]
     aliases = {}
     if not first:
         attended, rq, rkv = carried
@@ -251,11 +224,11 @@
         ] + [sent_shape] * (2 * last),
         scratch_shapes=[
             pltpu.VMEM((PER_STEP, slab, HEAD), BF16),
-            pltpu.VMEM((PER_STEP, 3 * slab, HEAD), BF16),
             pltpu.VMEM((PER_STEP, 3 * slab, 2 * HEAD), BF16),
-            pltpu.VMEM((PER_STEP, 3 * slab, HEAD), BF16),
-            pltpu.VMEM((PER_STEP, 3 * RANK, slab), BF16),
+            pltpu.VMEM((PER_STEP, 3 * slab, 2 * HEAD), BF16),
             pltpu.VMEM((PER_STEP, 2 * RANK, slab), BF16),
+            pltpu.VMEM((PER_STEP, 2 * RANK, slab), BF16),
+            pltpu.VMEM((PER_STEP, slab, 2 * HEAD), BF16),
             pltpu.VMEM((PER_STEP, slab, 2 * HEAD), F32),
         ],
         input_output_aliases=aliases,
@@ -270,7 +243,32 @@
     )(*operands)
 
 
-def prologue_kernel(step, x, shift_scale, down, x_mod, low, low_sent, low0_t, down_s):
+def pack_kernel(keys, values, out, sems):
+    columns = pl.ds(0, out.shape[2])
+    copies = [
+        pltpu.make_async_copy(ref.at[0, :, columns], out.at[i], sems.at[i])
+        for i, ref in enumerate((keys, values))
+    ]
+    for copy in copies:
+        copy.start()
+    for copy in copies:
+        copy.wait()
+
+
+def pack(keys, values, heads):
+    keys, values = [pltpu.with_memory_space_constraint(x, pltpu.HBM) for x in (keys, values)]
+    hbm = pl.BlockSpec(memory_space=pltpu.HBM)
+    return pl.pallas_call(
+        pack_kernel,
+        in_specs=[hbm, hbm],
+        out_specs=hbm,
+        out_shape=jax.ShapeDtypeStruct((2, keys.shape[1], heads * HEAD), BF16),
+        scratch_shapes=[pltpu.SemaphoreType.DMA((2,))],
+        name="pack",
+    )(keys, values)
+
+
+def prologue_kernel(step, x, shift_scale, down, x_mod, low, low0_t, down_s):
     del step
     width = x.shape[2]
 
@@ -288,7 +286,6 @@
     x_mod[...] = modulated
     reduced = dot_t(modulated, down_s[...])
     low[...] = reduced.astype(BF16)
-    low_sent[0] = reduced.astype(BF16)
     low0_t[...] = reduced.T[RANK:2 * RANK].astype(BF16)
 
 
@@ -310,7 +307,6 @@
             out_specs=[
                 pl.BlockSpec((TILE, width), lambda i, step: (i, 0)),
                 pl.BlockSpec((TILE, 4 * RANK), lambda i, step: (i, 0)),
-                pl.BlockSpec((1, TILE, 4 * RANK), lambda i, step: (i % 2, 0, i // 2)),
                 pl.BlockSpec((RANK, TILE), lambda i, step: (0, i)),
             ],
             scratch_shapes=[pltpu.VMEM((4 * RANK, width), BF16)],
@@ -318,7 +314,6 @@
         out_shape=[
             jax.ShapeDtypeStruct((slab, width), BF16),
             jax.ShapeDtypeStruct((slab, 4 * RANK), BF16),
-            jax.ShapeDtypeStruct((2, TILE, slab // TILE // 2 * 4 * RANK), BF16),
             jax.ShapeDtypeStruct((RANK, slab), BF16),
         ],
         compiler_params=pltpu.CompilerParams(
@@ -442,30 +437,27 @@
         columns = slice(h0 * HEAD, (h0 + heads) * HEAD)
         return jnp.concatenate([frozen_keys[:, :, columns], frozen_values[:, :, columns]], axis=0)
 
-    part = frozen_part(0, EARLY)
+    part = pack(frozen_keys, frozen_values, CHUNKS[0])
     early = neighbours(part, part, "tiles")
-    x_mod, low, low_sent, low0_t = prologue(
+    x_mod, low, low0_t = prologue(
         hidden, truncation_step, modulation, adapter_down_weight.transpose(0, 2, 1)
     )
-    bounds[0] = (EARLY, CHUNKS[0] - EARLY)
-    parts = [frozen_part(*b) for b in bounds]
-    *early, low_sent = lax.optimization_barrier((*early, low_sent))
-    parts[0] = jnp.concatenate([parts[0], low_sent], axis=1)
-    bounds[0] = (0, CHUNKS[0])
-    parts = lax.optimization_barrier(parts)
-    halos = [neighbours(part, part, "tiles") for part in parts]
+    parts = [frozen_part(*b) for b in bounds[1:]]
+    early, low, parts = lax.optimization_barrier((early, low, parts))
+    lows = neighbours(low, low, "tiles")
+    halos = [early] + [neighbours(part, part, "tiles") for part in parts]
 
     up = adapter_up_weight
     pad = lambda x, before: jnp.pad(x, ((before, 3 * RANK - before), (0, 0)))
     up_wide = jnp.stack([pad(up[0], RANK), pad(up[1], 2 * RANK), pad(up[2], 0)])
     bias = tile_bias(window, lax.axis_index("tiles"), lax.axis_size("tiles"))
-    shared = (bias, low, low0_t, *halos[0])
+    shared = (bias, low, low0_t, *lows)
     own = (frozen_queries, frozen_keys, frozen_values, reward_output_gradient)
     carried = None
     grad_up_parts = []
     for i, ((h0, heads), halo) in enumerate(zip(bounds, halos)):
         attended, grad_up, rq, rkv, *sent = attend_chunk(
-            h0, heads, i == len(bounds) - 1, shared, own, (up_wide, up), halo, early, carried
+            h0, heads, i == len(bounds) - 1, shared, own, (up_wide, up), halo, carried
         )
         carried = (attended, rq, rkv)
         grad_up_parts.append(grad_up)

time: 174 us -> 226 us (1.30)
  Pallas kernels: 58.6 us -> 104 us
  starting transfers between devices: 36.1 us -> 42.2 us
  waiting for transfers between devices: 26.6 us -> 31.4 us
  local copies, waits for them, and re-layouts: 4.14 us -> 1.21 us
    pallas_call x0 -> x1, Pallas kernels: none -> 48.8 us  [pack(): pl.pallas_call(pack_kernel, in_specs=[hbm, hbm], out_specs=hbm, out_shape...]
    ppermute x10, starting transfers between devices: 34.1 us -> 40.2 us  [neighbours(): return (lax.ppermute(before, axis, up), lax.ppermute(after, axis, down))]
    ppermute x10, waiting for transfers between devices: 24.2 us -> 29 us  [neighbours(): return (lax.ppermute(before, axis, up), lax.ppermute(after, axis, down))]
    pallas_call x3, Pallas kernels: 49.1 us -> 45.9 us  [attend_chunk(): pl.pallas_call(functools.partial(attend_kernel, first, last, slab), grid=...]
    slice x2 -> x4, local copies, waits for them, and re-layouts: 2.94 us -> 0.01 us  [frozen_part(): frozen_keys[:, :, columns]]
  transfers between devices with their start and end apart: 13 -> 13, of which waited for: 5 -> 4; matrix products, arithmetic and copies ran while one was open for 1% -> 0% of each run, Pallas kernels for 26% -> 19%
where the time goes in v4:
time: 226 us
  Pallas kernels  104 us (46%)
  blocking collectives  44.1 us (20%)
  starting transfers between devices  42.2 us (19%)
  waiting for transfers between devices  31.4 us (14%)
    pallas_call x1, Pallas kernels, pack(): pl.pallas_call(pack_kernel, in_specs=[hbm, hbm], out_specs=hbm, out_shape...  48.8 us
    pallas_call x3, Pallas kernels, attend_chunk(): pl.pallas_call(functools.partial(attend_kernel, first, last, slab), grid=...  45.9 us
    ppermute x10, starting transfers between devices, neighbours(): return (lax.ppermute(before, axis, up), lax.ppermute(after, axis, down))  40.2 us
    ppermute x10, waiting for transfers between devices, neighbours(): return (lax.ppermute(before, axis, up), lax.ppermute(after, axis, down))  29 us
    all_to_all x1, blocking collectives, reduce_everywhere(): got = lax.all_to_all(parts, tiles, 0, 0, tiled=True)  22.7 us
    all_to_all x1, blocking collectives, reduce_everywhere(): return lax.all_to_all(spread, tiles, 0, 0, tiled=True).reshape(x.shape)  21.4 us
    pallas_call x1, Pallas kernels, prologue(): pl.pallas_call(prologue_kernel, grid_spec=pltpu.PrefetchScalarGridSpec(nu...  5.26 us
  transfers between devices with their start and end apart: 13, of which 4 were waited for; matrix products, arithmetic and copies ran while one was open for 0% of the time, Pallas kernels for 19%

profile of v4, /device:TPU:0, one launch (start us, length us, event | category | flops | bytes accessed | tf_op | source)
XLA Modules:
  0.0 225.6 jit_solution(18027147329689230010)
XLA Ops:
  0.6 48.8 %pack.1 = bf16[2,512,768]{2,1,0:T(8,128)(2,1)} custom-call(bf16[1,512,1536]{2,1,0:T(8,128)(2,1)} %refs_6_.5, bf16[1,512,1536]{2,1,0:T(8,128)(2,1)} %refs_7_.5), custom_call_target="tpu_custom_call" | custom-call | tf_op jit(solution)/shard_map/pack/pallas_call | solution.py:261
  49.4 1.7 collective-permute-start
  51.1 7.5 %collective-permute-start.1 = (bf16[2,512,768]{2,1,0:T(8,128)(2,1)}, bf16[2,512,768]{2,1,0:T(8,128)(2,1)}, u32[]{:S(2)}, u32[]{:S(2)}) collective-permute-start(bf16[2,512,768]{2,1,0:T(8,128)(2,1)} %pack.1), channel_id=1, source_target_pairs={{1,0},{2,1},{3,2},{4,3},{5,4},{6,5},{7,6},{8,7},{9,8},{10,9},{11,1... | collective-permute-start | bytes 4718600 | tf_op jit(solution)/shard_map/ppermute | solution.py:398
  58.7 0.3 select_reduce_fusion
  60.0 5.3 %prologue.1 = (bf16[512,3072]{1,0:T(8,128)(2,1)S(1)}, bf16[512,128]{1,0:T(8,128)(2,1)S(1)}, bf16[32,512]{1,0:T(8,128)(2,1)S(1)}) custom-call(s32[1]{0:T(128)S(6)} %copy.21.step, bf16[1,512,3072]{2,1,0:T(8,128)(2,1)} %x.7, f32[50,2,3072]{2,1,0:T(2,128)} %shift_scale.1, bf16[3,32,3072]{2,1,0:T(8,128)(2,1)} %bitcast.26), custom_call_target="tpu_custom_call" | custom-call | tf_op jit(solution)/shard_map/prologue/pallas_call | solution.py:297
  65.4 0.8 copy-done.1
  66.3 0.1 pad_maximum_fusion.refs_9_
  66.5 26.7 %collective-permute-done.refs_11_.refs_12_ = bf16[2,512,768]{2,1,0:T(8,128)(2,1)} collective-permute-done((bf16[2,512,768]{2,1,0:T(8,128)(2,1)}, bf16[2,512,768]{2,1,0:T(8,128)(2,1)}, u32[]{:S(2)}, u32[]{:S(2)}) %collective-permute-start) | collective-permute-done | bytes 1572896 | tf_op jit(solution)/shard_map/ppermute | solution.py:398
  93.2 7.7 %collective-permute-start.3 = (bf16[512,128]{1,0:T(8,128)(2,1)S(1)}, bf16[512,128]{1,0:T(8,128)(2,1)S(1)}, u32[]{:S(2)}, u32[]{:S(2)}) collective-permute-start(bf16[512,128]{1,0:T(8,128)(2,1)S(1)} %get-tuple-element.28.refs_1_), channel_id=1, source_target_pairs={{1,0},{2,1},{3,2},{4,3},{5,4},{6,5},{7,6},{8,7},{9,8},{10,9},{11,1... | collective-permute-start | bytes 393224 | tf_op jit(solution)/shard_map/ppermute | solution.py:398
  101.2 7.7 %collective-permute-start.7 = (bf16[2,512,512]{2,1,0:T(8,128)(2,1)S(1)}, bf16[2,512,512]{2,1,0:T(8,128)(2,1)S(1)}, u32[]{:S(2)}, u32[]{:S(2)}) collective-permute-start(bf16[2,512,512]{2,1,0:T(8,128)(2,1)S(1)} %pad_maximum_fusion.1), channel_id=1, source_target_pairs={{1,0},{2,1},{3,2},{4,3},{5,4},{6,5},{7,6},{8,7},{9,8},{10,9},{11,1... | collective-permute-start | bytes 3145736 | tf_op jit(solution)/shard_map/ppermute | solution.py:398
  108.9 7.7 %collective-permute-start.5 = (bf16[2,512,256]{2,1,0:T(8,128)(2,1)S(1)}, bf16[2,512,256]{2,1,0:T(8,128)(2,1)S(1)}, u32[]{:S(2)}, u32[]{:S(2)}) collective-permute-start(bf16[2,512,256]{2,1,0:T(8,128)(2,1)S(1)} %pad_maximum_fusion.2), channel_id=1, source_target_pairs={{1,0},{2,1},{3,2},{4,3},{5,4},{6,5},{7,6},{8,7},{9,8},{10,9},{11,1... | collective-permute-start | bytes 1572872 | tf_op jit(solution)/shard_map/ppermute | solution.py:398
  116.7 21.8 %attend_0.1 = (bf16[1,512,1536]{2,1,0:T(8,128)(2,1)}, f32[3,32,768]{2,1,0:T(8,128)S(1)}, f32[32,512]{1,0:T(8,128)S(1)}, f32[64,1536]{1,0:T(8,128)S(1)}) custom-call(f32[4,1536]{1,0:T(4,128)S(1)} %bitcast.22, bf16[512,128]{1,0:T(8,128)(2,1)S(1)} %get-tuple-element.28.refs_1_, bf16[32,512]{1,0:T(8,128)(2,1)S(1)} %get-tuple-element.29.refs_2_, ...), custom_call_target="tpu_custom_call" | custom-call | flops 27599998976 | bytes 7864320 | tf_op jit(solution)/shard_map/attend_0/pallas_call | solution.py:209
  138.4 15.6 %attend_6.1 = (bf16[1,512,1536]{2,1,0:T(8,128)(2,1)}, f32[3,32,512]{2,1,0:T(8,128)S(1)}, f32[32,512]{1,0:T(8,128)S(1)}, f32[64,1536]{1,0:T(8,128)S(1)}) custom-call(f32[4,1536]{1,0:T(4,128)S(1)} %bitcast.23, bf16[512,128]{1,0:T(8,128)(2,1)S(1)} %get-tuple-element.28.refs_1_, ...), custom_call_target="tpu_custom_call", output_to_operand_aliasing={{0}: (17, {})} | custom-call | flops 18400000000 | bytes 5242880 | tf_op jit(solution)/shard_map/attend_6/pallas_call | solution.py:209
  154.1 8.5 %attend_10.1 = (bf16[1,512,1536]{2,1,0:T(8,128)(2,1)}, f32[3,32,256]{2,1,0:T(8,128)S(1)}, f32[32,512]{1,0:T(8,128)S(1)}, f32[64,1536]{1,0:T(8,128)S(1)}, bf16[64...) custom-call(f32[4,1536]{1,0:T(4,128)S(1)} %bitcast.24, ...), custom_call_target="tpu_custom_call", output_to_operand_aliasing={{0}: (17, {})} | custom-call | flops 9200000000 | bytes 2621440 | tf_op jit(solution)/shard_map/attend_10/pallas_call | solution.py:209
  162.6 7.7 %collective-permute-start.9 = (bf16[64,512]{1,0:T(8,128)(2,1)S(1)}, bf16[64,512]{1,0:T(8,128)(2,1)S(1)}, u32[]{:S(2)}, u32[]{:S(2)}) collective-permute-start(bf16[64,512]{1,0:T(8,128)(2,1)S(1)} %get-tuple-element.44), channel_id=1, source_target_pairs={{1,0},{2,1},{3,2},{4,3},{5,4},{6,5},{7,6},{8,7},{9,8},{10,9},{11,1... | collective-permute-start | bytes 196616 | tf_op jit(solution)/shard_map/ppermute | solution.py:398
  170.4 2.2 collective-permute-done.8.from_prev
  172.6 1.7 project.1
  174.3 22.7 %all_to_all.10 = bf16[32,112,128]{2,1,0:T(8,128)(2,1)S(1)} all-to-all(bf16[32,112,128]{2,1,0:T(8,128)(2,1)S(1)} %bitcast.21), channel_id=1, replica_groups=mesh['batch'=4,'tiles'=32] {'tiles'}, dimensions={0} | all-to-all | bytes 1835008 | tf_op jit(solution)/shard_map/all_to_all | solution.py:404
  197.0 0.1 reduce_sum.22
  197.3 0.7 collective-permute-start.11
  198.0 1.2 collective-permute-start.12
  199.1 2.3 %collective-permute-done.11 = bf16[112,128]{1,0:T(8,128)(2,1)S(1)} collective-permute-done((bf16[112,128]{1,0:T(8,128)(2,1)S(1)}, bf16[112,128]{1,0:T(8,128)(2,1)S(1)}, u32[]{:S(2)}, u32[]{:S(2)}) %collective-permute-start.11) | collective-permute-done | bytes 28704 | tf_op jit(solution)/shard_map/ppermute | solution.py:408
  201.7 21.4 %all_to_all.11 = bf16[32,112,128]{2,1,0:T(8,128)(2,1)} all-to-all(bf16[32,112,128]{2,1,0:T(8,128)(2,1)S(1)} %broadcast_in_dim.43), channel_id=1, replica_groups=mesh['batch'=4,'tiles'=32] {'tiles'}, dimensions={0} | all-to-all | bytes 1835008 | tf_op jit(solution)/shard_map/all_to_all | solution.py:412
  223.1 2.5 %unpack.1 = (f32[3,32,3072]{2,1,0:T(8,128)}, f32[3,32,1536]{2,1,0:T(8,128)}) custom-call(bf16[224,16,128]{2,1,0:T(8,128)(2,1)} %bitcast.25), custom_call_target="tpu_custom_call" | custom-call | tf_op jit(solution)/shard_map/unpack/pallas_call | solution.py:391
  (48 shorter events, 1.1 us)
Async XLA Ops:
  0.6 58.1 %copy-start.4 = (s32[4,27]{1,0:T(4,128)S(1)}, s32[4,27]{1,0:T(4,128)}, u32[]{:S(2)}) copy-start(s32[4,27]{1,0:T(4,128)} %param.19) | copy-start | bytes 1300
  49.4 43.8 %collective-permute-start = (bf16[2,512,768]{2,1,0:T(8,128)(2,1)}, bf16[2,512,768]{2,1,0:T(8,128)(2,1)}, u32[]{:S(2)}, u32[]{:S(2)}) collective-permute-start(bf16[2,512,768]{2,1,0:T(8,128)(2,1)} %pack.1), channel_id=1, source_target_pairs={{0,1},{1,2},{2,3},{3,4},{4,5},{5,6},{6,7},{7,8},{8,9},{9,10},{10,1... | collective-permute-start | bytes 4718600 | tf_op jit(solution)/shard_map/ppermute | solution.py:398
  51.1 42.1 %collective-permute-start.1 = (bf16[2,512,768]{2,1,0:T(8,128)(2,1)}, bf16[2,512,768]{2,1,0:T(8,128)(2,1)}, u32[]{:S(2)}, u32[]{:S(2)}) collective-permute-start(bf16[2,512,768]{2,1,0:T(8,128)(2,1)} %pack.1), channel_id=1, source_target_pairs={{1,0},{2,1},{3,2},{4,3},{5,4},{6,5},{7,6},{8,7},{9,8},{10,9},{11,1... | collective-permute-start | bytes 4718600 | tf_op jit(solution)/shard_map/ppermute | solution.py:398
  59.9 5.3 %slice-start.1 = ((bf16[1,512,1536]{2,1,0:T(8,128)(2,1)}), bf16[1,512,256]{2,1,0:T(8,128)(2,1)S(1)}, s32[]{:S(2)}) async-start(bf16[1,512,1536]{2,1,0:T(8,128)(2,1)} %refs_6_.5), calls=%async_computation.3 | async-start | bytes 524288 | tf_op jit(solution)/shard_map/slice | solution.py:438
  59.9 5.3 %slice-start.3 = ((bf16[1,512,1536]{2,1,0:T(8,128)(2,1)}), bf16[1,512,256]{2,1,0:T(8,128)(2,1)S(1)}, s32[]{:S(2)}) async-start(bf16[1,512,1536]{2,1,0:T(8,128)(2,1)} %refs_7_.5), calls=%async_computation.5 | async-start | bytes 524288 | tf_op jit(solution)/shard_map/slice | solution.py:438
  59.9 5.4 %slice-start = ((bf16[1,512,1536]{2,1,0:T(8,128)(2,1)}), bf16[1,512,512]{2,1,0:T(8,128)(2,1)S(1)}, s32[]{:S(2)}) async-start(bf16[1,512,1536]{2,1,0:T(8,128)(2,1)} %refs_6_.5), calls=%async_computation.2 | async-start | bytes 1048576 | tf_op jit(solution)/shard_map/slice | solution.py:438
  59.9 5.4 %slice-start.2 = ((bf16[1,512,1536]{2,1,0:T(8,128)(2,1)}), bf16[1,512,512]{2,1,0:T(8,128)(2,1)S(1)}, s32[]{:S(2)}) async-start(bf16[1,512,1536]{2,1,0:T(8,128)(2,1)} %refs_7_.5), calls=%async_computation.4 | async-start | bytes 1048576 | tf_op jit(solution)/shard_map/slice | solution.py:438
  65.2 1.0 copy-start.1
  66.3 50.4 %copy-start = (bf16[1,512,1536]{2,1,0:T(8,128)(2,1)S(1)}, bf16[1,512,1536]{2,1,0:T(8,128)(2,1)}, u32[]{:S(2)}) copy-start(bf16[1,512,1536]{2,1,0:T(8,128)(2,1)} %refs_6_.5) | copy-start | bytes 4718596
  66.3 50.4 %copy-start.2 = (bf16[1,512,1536]{2,1,0:T(8,128)(2,1)S(1)}, bf16[1,512,1536]{2,1,0:T(8,128)(2,1)}, u32[]{:S(2)}) copy-start(bf16[1,512,1536]{2,1,0:T(8,128)(2,1)} %refs_5_.5) | copy-start | bytes 4718596
  93.2 15.7 %collective-permute-start.2 = (bf16[512,128]{1,0:T(8,128)(2,1)S(1)}, bf16[512,128]{1,0:T(8,128)(2,1)S(1)}, u32[]{:S(2)}, u32[]{:S(2)}) collective-permute-start(bf16[512,128]{1,0:T(8,128)(2,1)S(1)} %get-tuple-element.28.refs_1_), channel_id=1, source_target_pairs={{0,1},{1,2},{2,3},{3,4},{4,5},{5,6},{6,7},{7,8},{8,9},{9,10},{10,1... | collective-permute-start | bytes 393224 | tf_op jit(solution)/shard_map/ppermute | solution.py:398
  93.2 23.4 %collective-permute-start.3 = (bf16[512,128]{1,0:T(8,128)(2,1)S(1)}, bf16[512,128]{1,0:T(8,128)(2,1)S(1)}, u32[]{:S(2)}, u32[]{:S(2)}) collective-permute-start(bf16[512,128]{1,0:T(8,128)(2,1)S(1)} %get-tuple-element.28.refs_1_), channel_id=1, source_target_pairs={{1,0},{2,1},{3,2},{4,3},{5,4},{6,5},{7,6},{8,7},{9,8},{10,9},{11,1... | collective-permute-start | bytes 393224 | tf_op jit(solution)/shard_map/ppermute | solution.py:398
  101.1 37.3 %collective-permute-start.6 = (bf16[2,512,512]{2,1,0:T(8,128)(2,1)S(1)}, bf16[2,512,512]{2,1,0:T(8,128)(2,1)S(1)}, u32[]{:S(2)}, u32[]{:S(2)}) collective-permute-start(bf16[2,512,512]{2,1,0:T(8,128)(2,1)S(1)} %pad_maximum_fusion.1), channel_id=1, source_target_pairs={{0,1},{1,2},{2,3},{3,4},{4,5},{5,6},{6,7},{7,8},{8,9},{9,10},{10,1... | collective-permute-start | bytes 3145736 | tf_op jit(solution)/shard_map/ppermute | solution.py:398
  101.2 37.3 %collective-permute-start.7 = (bf16[2,512,512]{2,1,0:T(8,128)(2,1)S(1)}, bf16[2,512,512]{2,1,0:T(8,128)(2,1)S(1)}, u32[]{:S(2)}, u32[]{:S(2)}) collective-permute-start(bf16[2,512,512]{2,1,0:T(8,128)(2,1)S(1)} %pad_maximum_fusion.1), channel_id=1, source_target_pairs={{1,0},{2,1},{3,2},{4,3},{5,4},{6,5},{7,6},{8,7},{9,8},{10,9},{11,1... | collective-permute-start | bytes 3145736 | tf_op jit(solution)/shard_map/ppermute | solution.py:398
  108.9 45.2 %collective-permute-start.4 = (bf16[2,512,256]{2,1,0:T(8,128)(2,1)S(1)}, bf16[2,512,256]{2,1,0:T(8,128)(2,1)S(1)}, u32[]{:S(2)}, u32[]{:S(2)}) collective-permute-start(bf16[2,512,256]{2,1,0:T(8,128)(2,1)S(1)} %pad_maximum_fusion.2), channel_id=1, source_target_pairs={{0,1},{1,2},{2,3},{3,4},{4,5},{5,6},{6,7},{7,8},{8,9},{9,10},{10,1... | collective-permute-start | bytes 1572872 | tf_op jit(solution)/shard_map/ppermute | solution.py:398
  108.9 45.2 %collective-permute-start.5 = (bf16[2,512,256]{2,1,0:T(8,128)(2,1)S(1)}, bf16[2,512,256]{2,1,0:T(8,128)(2,1)S(1)}, u32[]{:S(2)}, u32[]{:S(2)}) collective-permute-start(bf16[2,512,256]{2,1,0:T(8,128)(2,1)S(1)} %pad_maximum_fusion.2), channel_id=1, source_target_pairs={{1,0},{2,1},{3,2},{4,3},{5,4},{6,5},{7,6},{8,7},{9,8},{10,9},{11,1... | collective-permute-start | bytes 1572872 | tf_op jit(solution)/shard_map/ppermute | solution.py:398
  138.4 15.7 %copy-start.3 = (bf16[1,512,1536]{2,1,0:T(8,128)(2,1)S(1)}, bf16[1,512,1536]{2,1,0:T(8,128)(2,1)}, u32[]{:S(2)}) copy-start(bf16[1,512,1536]{2,1,0:T(8,128)(2,1)} %refs_5_.5) | copy-start | bytes 4718596
  162.6 10.0 %collective-permute-start.8 = (bf16[64,512]{1,0:T(8,128)(2,1)S(1)}, bf16[64,512]{1,0:T(8,128)(2,1)S(1)}, u32[]{:S(2)}, u32[]{:S(2)}) collective-permute-start(bf16[64,512]{1,0:T(8,128)(2,1)S(1)} %get-tuple-element.43), channel_id=1, source_target_pairs={{0,1},{1,2},{2,3},{3,4},{4,5},{5,6},{6,7},{7,8},{8,9},{9,10},{10,1... | collective-permute-start | bytes 196616 | tf_op jit(solution)/shard_map/ppermute | solution.py:398
  162.6 10.0 %collective-permute-start.9 = (bf16[64,512]{1,0:T(8,128)(2,1)S(1)}, bf16[64,512]{1,0:T(8,128)(2,1)S(1)}, u32[]{:S(2)}, u32[]{:S(2)}) collective-permute-start(bf16[64,512]{1,0:T(8,128)(2,1)S(1)} %get-tuple-element.44), channel_id=1, source_target_pairs={{1,0},{2,1},{3,2},{4,3},{5,4},{6,5},{7,6},{8,7},{9,8},{10,9},{11,1... | collective-permute-start | bytes 196616 | tf_op jit(solution)/shard_map/ppermute | solution.py:398
  197.2 2.0 collective-permute-start.10
  197.3 4.2 %collective-permute-start.11 = (bf16[112,128]{1,0:T(8,128)(2,1)S(1)}, bf16[112,128]{1,0:T(8,128)(2,1)S(1)}, u32[]{:S(2)}, u32[]{:S(2)}) collective-permute-start(bf16[112,128]{1,0:T(8,128)(2,1)S(1)} %reduce_sum.22), channel_id=1, source_target_pairs={{0,64},{32,96},{64,0},{96,32},{1,65},{33,97},{65,1},{97,33},{2,66}... | collective-permute-start | bytes 86024 | tf_op jit(solution)/shard_map/ppermute | solution.py:408
  198.0 3.6 %collective-permute-start.12 = (bf16[112,128]{1,0:T(8,128)(2,1)S(1)}, bf16[112,128]{1,0:T(8,128)(2,1)S(1)}, u32[]{:S(2)}, u32[]{:S(2)}) collective-permute-start(bf16[112,128]{1,0:T(8,128)(2,1)S(1)} %reduce_sum.22), channel_id=1, source_target_pairs={{0,96},{32,64},{64,32},{96,0},{1,97},{33,65},{65,33},{97,1},{2,98}... | collective-permute-start | bytes 86024 | tf_op jit(solution)/shard_map/ppermute | solution.py:408

commit v5 on v4

--- a/solution.py
+++ b/solution.py
@@ -80,8 +80,8 @@
             kl_s[n, slab:2 * slab, HEAD:] = low_own[...]
             for i, low in ((0, low_prev), (2, low_next)):
                 rows = slice(i * slab, (i + 1) * slab)
-                vl_s[n, rows, HEAD:] = low[...]
-                kl_s[n, rows, HEAD:] = low[...]
+                vl_s[n, rows, HEAD:] = low[0]
+                kl_s[n, rows, HEAD:] = low[0]
         if first:
             rq[...] = jnp.zeros_like(rq)
             rkv[...] = jnp.zeros_like(rkv)
@@ -98,7 +98,8 @@
         cols = slice(n * HEAD, (n + 1) * HEAD)
         kv_up = jnp.concatenate([up_wide[1, :, cols], up_wide[2, :, cols]], axis=1)
         q_s[n] = (fq[0, :, cols].astype(F32) + dot(low_own[...], up_wide[0, :, cols])).astype(BF16)
-        arrived = [halo[0, :, cols] for halo in halos]
+        at = n if first else (0, slice(None), cols)
+        arrived = [halo[at] for halo in halos]
         sides = (arrived[:2], (fk[0, :, cols], fv[0, :, cols]), arrived[2:])
         for i, (k_in, v_in) in enumerate(sides):
             rows = slice(i * slab, (i + 1) * slab)
@@ -184,7 +185,7 @@
     return pl.BlockSpec(x.shape, lambda *_: (0,) * len(x.shape))
 
 
-def attend_chunk(h0, heads, last, shared, own, ups, halo, carried):
+def attend_chunk(h0, heads, last, shared, lows, own, ups, halo, carried):
     slab = own[0].shape[1]
     across = own[0].shape[2]
     first = carried is None
@@ -192,11 +193,20 @@
     wide = PER_STEP * HEAD
 
     own_spec = pl.BlockSpec((1, slab, wide), lambda h: (0, 0, h0 // PER_STEP + h))
-    halo_specs = [pl.BlockSpec((1, slab, wide), lambda h, kind=kind: (kind, 0, h)) for kind in (0, 1)]
-    in_specs = [whole(x) for x in shared] + [own_spec] * 4 + [
+    low_spec = pl.BlockSpec((1, slab, HEAD), lambda h: (lows[0].shape[0] - 1, 0, 0))
+    if first:
+        halo_specs = [
+            pl.BlockSpec((PER_STEP, slab, HEAD), lambda h, skip=skip: (skip + h, 0, 0))
+            for skip in (0, steps)
+        ]
+    else:
+        halo_specs = [
+            pl.BlockSpec((1, slab, wide), lambda h, kind=kind: (kind, 0, h)) for kind in (0, 1)
+        ]
+    in_specs = [whole(x) for x in shared] + [low_spec] * 2 + [own_spec] * 4 + [
         pl.BlockSpec((3, x.shape[1], wide), lambda h: (0, 0, h0 // PER_STEP + h)) for x in ups
     ] + halo_specs * 2
-    operands = [*shared, *own, *ups, halo[0], halo[0], halo[1], halo[1]]
+    operands = [*shared, *lows, *own, *ups, halo[0], halo[0], halo[1], halo[1]]
     aliases = {}
     if not first:
         attended, rq, rkv = carried
@@ -243,34 +253,10 @@
     )(*operands)
 
 
-def pack_kernel(keys, values, out, sems):
-    columns = pl.ds(0, out.shape[2])
-    copies = [
-        pltpu.make_async_copy(ref.at[0, :, columns], out.at[i], sems.at[i])
-        for i, ref in enumerate((keys, values))
-    ]
-    for copy in copies:
-        copy.start()
-    for copy in copies:
-        copy.wait()
-
-
-def pack(keys, values, heads):
-    keys, values = [pltpu.with_memory_space_constraint(x, pltpu.HBM) for x in (keys, values)]
-    hbm = pl.BlockSpec(memory_space=pltpu.HBM)
-    return pl.pallas_call(
-        pack_kernel,
-        in_specs=[hbm, hbm],
-        out_specs=hbm,
-        out_shape=jax.ShapeDtypeStruct((2, keys.shape[1], heads * HEAD), BF16),
-        scratch_shapes=[pltpu.SemaphoreType.DMA((2,))],
-        name="pack",
-    )(keys, values)
-
-
-def prologue_kernel(step, x, shift_scale, down, x_mod, low, low0_t, down_s):
+def prologue_kernel(step, x, shift_scale, down, fk, fv, x_mod, first_halo, low0_t, down_s):
     del step
     width = x.shape[2]
+    heads = fk.shape[2] // HEAD
 
     @pl.when(pl.program_id(0) == 0)
     def _():
@@ -285,15 +271,20 @@
     modulated = (normed * (1.0 + shift_scale[0, 1:2, :]) + shift_scale[0, 0:1, :]).astype(BF16)
     x_mod[...] = modulated
     reduced = dot_t(modulated, down_s[...])
-    low[...] = reduced.astype(BF16)
+    for n in range(heads):
+        first_halo[n] = fk[0, :, n * HEAD:(n + 1) * HEAD]
+        first_halo[heads + n] = fv[0, :, n * HEAD:(n + 1) * HEAD]
+    first_halo[2 * heads] = reduced.astype(BF16)
     low0_t[...] = reduced.T[RANK:2 * RANK].astype(BF16)
 
 
-def prologue(hidden, truncation_step, modulation, down):
+def prologue(hidden, truncation_step, modulation, down, frozen_keys, frozen_values, heads):
     _, slab, width = hidden.shape
-    hidden, modulation, down = [
-        pltpu.with_memory_space_constraint(x, pltpu.HBM) for x in (hidden, modulation, down)
+    hidden, modulation, down, frozen_keys, frozen_values = [
+        pltpu.with_memory_space_constraint(x, pltpu.HBM)
+        for x in (hidden, modulation, down, frozen_keys, frozen_values)
     ]
+    frozen_spec = pl.BlockSpec((1, TILE, heads * HEAD), lambda i, step: (0, i, 0))
     return pl.pallas_call(
         prologue_kernel,
         grid_spec=pltpu.PrefetchScalarGridSpec(
@@ -303,24 +294,26 @@
                 pl.BlockSpec((1, TILE, width), lambda i, step: (0, i, 0)),
                 pl.BlockSpec((1, 2, width), lambda i, step: (step[0], 0, 0)),
                 whole(down),
+                frozen_spec,
+                frozen_spec,
             ],
             out_specs=[
                 pl.BlockSpec((TILE, width), lambda i, step: (i, 0)),
-                pl.BlockSpec((TILE, 4 * RANK), lambda i, step: (i, 0)),
+                pl.BlockSpec((2 * heads + 1, TILE, HEAD), lambda i, step: (0, i, 0)),
                 pl.BlockSpec((RANK, TILE), lambda i, step: (0, i)),
             ],
             scratch_shapes=[pltpu.VMEM((4 * RANK, width), BF16)],
         ),
         out_shape=[
             jax.ShapeDtypeStruct((slab, width), BF16),
-            jax.ShapeDtypeStruct((slab, 4 * RANK), BF16),
+            jax.ShapeDtypeStruct((2 * heads + 1, slab, HEAD), BF16),
             jax.ShapeDtypeStruct((RANK, slab), BF16),
         ],
         compiler_params=pltpu.CompilerParams(
             dimension_semantics=("arbitrary",), vmem_limit_bytes=48 << 20
         ),
         name="prologue",
-    )(truncation_step, hidden, modulation, down)
+    )(truncation_step, hidden, modulation, down, frozen_keys, frozen_values)
 
 
 def project_kernel(factor, rq, rkv, from_prev, from_next, x_mod, *refs):
@@ -433,31 +426,31 @@
         bounds.append((h0, heads))
         h0 += heads
 
-    def frozen_part(h0, heads):
+    def frozen_part(keys, values, h0, heads):
         columns = slice(h0 * HEAD, (h0 + heads) * HEAD)
-        return jnp.concatenate([frozen_keys[:, :, columns], frozen_values[:, :, columns]], axis=0)
-
-    part = pack(frozen_keys, frozen_values, CHUNKS[0])
-    early = neighbours(part, part, "tiles")
-    x_mod, low, low0_t = prologue(
-        hidden, truncation_step, modulation, adapter_down_weight.transpose(0, 2, 1)
+        return jnp.concatenate([keys[:, :, columns], values[:, :, columns]], axis=0)
+
+    x_mod, first_halo, low0_t = prologue(
+        hidden, truncation_step, modulation, adapter_down_weight.transpose(0, 2, 1),
+        frozen_keys, frozen_values, CHUNKS[0],
     )
-    parts = [frozen_part(*b) for b in bounds[1:]]
-    early, low, parts = lax.optimization_barrier((early, low, parts))
-    lows = neighbours(low, low, "tiles")
-    halos = [early] + [neighbours(part, part, "tiles") for part in parts]
+    halos = [neighbours(first_halo, first_halo, "tiles")]
+    first_halo, keys, values = lax.optimization_barrier((first_halo, frozen_keys, frozen_values))
+    parts = [frozen_part(keys, values, *b) for b in bounds[1:]]
+    halos += [neighbours(part, part, "tiles") for part in parts]
+    low = first_halo[2 * CHUNKS[0]]
 
     up = adapter_up_weight
     pad = lambda x, before: jnp.pad(x, ((before, 3 * RANK - before), (0, 0)))
     up_wide = jnp.stack([pad(up[0], RANK), pad(up[1], 2 * RANK), pad(up[2], 0)])
     bias = tile_bias(window, lax.axis_index("tiles"), lax.axis_size("tiles"))
-    shared = (bias, low, low0_t, *lows)
+    shared = (bias, low, low0_t)
     own = (frozen_queries, frozen_keys, frozen_values, reward_output_gradient)
     carried = None
     grad_up_parts = []
     for i, ((h0, heads), halo) in enumerate(zip(bounds, halos)):
         attended, grad_up, rq, rkv, *sent = attend_chunk(
-            h0, heads, i == len(bounds) - 1, shared, own, (up_wide, up), halo, carried
+            h0, heads, i == len(bounds) - 1, shared, halos[0], own, (up_wide, up), halo, carried
         )
         carried = (attended, rq, rkv)
         grad_up_parts.append(grad_up)

time: 226 us -> 166 us (0.73)
  Pallas kernels: 104 us -> 56.6 us
  starting transfers between devices: 42.2 us -> 29 us
    pallas_call x1 -> x0, Pallas kernels: 48.8 us -> none  [pack(): pl.pallas_call(pack_kernel, in_specs=[hbm, hbm], out_specs=hbm, out_shape...]
    ppermute x10 -> x8, starting transfers between devices: 40.2 us -> 26.8 us  [neighbours(): return (lax.ppermute(before, axis, up), lax.ppermute(after, axis, down))]
    ppermute x10 -> x8, waiting for transfers between devices: 29 us -> 29.5 us  [neighbours(): return (lax.ppermute(before, axis, up), lax.ppermute(after, axis, down))]
  transfers between devices with their start and end apart: 13 -> 11, of which waited for: 4 -> 4; matrix products, arithmetic and copies ran while one was open for 0% -> 2% of each run, Pallas kernels for 19% -> 23%
where the time goes in v5:
time: 166 us
  Pallas kernels  56.6 us (34%)
  blocking collectives  43.5 us (26%)
  waiting for transfers between devices  31.9 us (19%)
  starting transfers between devices  29 us (17%)
  other arithmetic  2.73 us (2%)
    pallas_call x3, Pallas kernels, attend_chunk(): pl.pallas_call(functools.partial(attend_kernel, first, last, slab), grid=...  46.9 us
    ppermute x8, waiting for transfers between devices, neighbours(): return (lax.ppermute(before, axis, up), lax.ppermute(after, axis, down))  29.5 us
    ppermute x8, starting transfers between devices, neighbours(): return (lax.ppermute(before, axis, up), lax.ppermute(after, axis, down))  26.8 us
    all_to_all x1, blocking collectives, reduce_everywhere(): got = lax.all_to_all(parts, tiles, 0, 0, tiled=True)  22.7 us
    all_to_all x1, blocking collectives, reduce_everywhere(): return lax.all_to_all(spread, tiles, 0, 0, tiled=True).reshape(x.shape)  20.8 us
    pallas_call x1, Pallas kernels, prologue(): pl.pallas_call(prologue_kernel, grid_spec=pltpu.PrefetchScalarGridSpec(nu...  5.61 us
  transfers between devices with their start and end apart: 11, of which 4 were waited for; matrix products, arithmetic and copies ran while one was open for 2% of the time, Pallas kernels for 23%

profile of v5, /device:TPU:0, one launch (start us, length us, event | category | flops | bytes accessed | tf_op | source)
XLA Modules:
  0.0 165.9 jit_solution(2656066147221699033)
XLA Ops:
  1.3 5.6 %prologue.1 = (bf16[512,3072]{1,0:T(8,128)(2,1)S(1)}, bf16[13,512,128]{2,1,0:T(8,128)(2,1)S(1)}, bf16[32,512]{1,0:T(8,128)(2,1)S(1)}) custom-call(s32[1]{0:T(128)S(6)} %copy.21.step, bf16[1,512,3072]{2,1,0:T(8,128)(2,1)} %x.7, f32[50,2,3072]{2,1,0:T(2,128)} %shift_scale.1, bf16[3,32,3072]{2,1,0:T(8,128)(2,1)} %bitcast.28, bf16[1,512,1536]{2,1,0:T(8,128)(2,1)} %refs_6_.5, ...), custom_call_target="tpu_custom_call" | custom-call | tf_op jit(solution)/shard_map/prologue/pallas_call | solution.py:288
  6.9 1.7 %collective-permute-start = (bf16[13,512,128]{2,1,0:T(8,128)(2,1)S(1)}, bf16[13,512,128]{2,1,0:T(8,128)(2,1)}, u32[]{:S(2)}, u32[]{:S(2)}) collective-permute-start(bf16[13,512,128]{2,1,0:T(8,128)(2,1)S(1)} %get-tuple-element.26), channel_id=1, source_target_pairs={{0,1},{1,2},{2,3},{3,4},{4,5},{5,6},{6,7},{7,8},{8,9},{9,10},{10,1... | collective-permute-start | bytes 5111816 | tf_op jit(solution)/shard_map/ppermute | solution.py:391
  8.7 7.5 %collective-permute-start.1 = (bf16[13,512,128]{2,1,0:T(8,128)(2,1)S(1)}, bf16[13,512,128]{2,1,0:T(8,128)(2,1)}, u32[]{:S(2)}, u32[]{:S(2)}) collective-permute-start(bf16[13,512,128]{2,1,0:T(8,128)(2,1)S(1)} %get-tuple-element.26), channel_id=1, source_target_pairs={{1,0},{2,1},{3,2},{4,3},{5,4},{6,5},{7,6},{8,7},{9,8},{10,9},{11,1... | collective-permute-start | bytes 5111816 | tf_op jit(solution)/shard_map/ppermute | solution.py:391
  16.1 1.1 pad_maximum_fusion.1
  17.3 7.7 %collective-permute-start.5 = (bf16[2,512,512]{2,1,0:T(8,128)(2,1)}, bf16[2,512,512]{2,1,0:T(8,128)(2,1)}, u32[]{:S(2)}, u32[]{:S(2)}) collective-permute-start(bf16[2,512,512]{2,1,0:T(8,128)(2,1)} %pad_maximum_fusion.1), channel_id=1, source_target_pairs={{1,0},{2,1},{3,2},{4,3},{5,4},{6,5},{7,6},{8,7},{9,8},{10,9},{11,1... | collective-permute-start | bytes 3145736 | tf_op jit(solution)/shard_map/ppermute | solution.py:391
  25.0 0.8 pad_maximum_fusion.2
  26.0 0.3 select_reduce_fusion
  26.8 0.1 pad_maximum_fusion.refs_9_
  27.0 27.2 %collective-permute-done.refs_3_.refs_11_.refs_12_ = bf16[13,512,128]{2,1,0:T(8,128)(2,1)} collective-permute-done((bf16[13,512,128]{2,1,0:T(8,128)(2,1)S(1)}, bf16[13,512,128]{2,1,0:T(8,128)(2,1)}, u32[]{:S(2)}, u32[]{:S(2)}) %collective-permute-start) | collective-permute-done | bytes 1703968 | tf_op jit(solution)/shard_map/ppermute | solution.py:391
  54.2 2.1 %collective-permute-start.3 = (bf16[2,512,256]{2,1,0:T(8,128)(2,1)}, bf16[2,512,256]{2,1,0:T(8,128)(2,1)S(1)}, u32[]{:S(2)}, u32[]{:S(2)}) collective-permute-start(bf16[2,512,256]{2,1,0:T(8,128)(2,1)} %pad_maximum_fusion.2), channel_id=1, source_target_pairs={{1,0},{2,1},{3,2},{4,3},{5,4},{6,5},{7,6},{8,7},{9,8},{10,9},{11,1... | collective-permute-start | bytes 1572872 | tf_op jit(solution)/shard_map/ppermute | solution.py:391
  56.3 22.1 %attend_0.1 = (bf16[1,512,1536]{2,1,0:T(8,128)(2,1)}, f32[3,32,768]{2,1,0:T(8,128)S(1)}, f32[32,512]{1,0:T(8,128)S(1)}, f32[64,1536]{1,0:T(8,128)S(1)}) custom-call(f32[4,1536]{1,0:T(4,128)S(1)} %bitcast.24, bf16[512,128]{1,0:T(8,128)(2,1)S(1)} %slice_bitcast_fusion.refs_1_, bf16[32,512]{1,0:T(8,128)(2,1)S(1)} %copy-done.7, ...), custom_call_target="tpu_custom_call" | custom-call | flops 27599998976 | bytes 7864320 | tf_op jit(solution)/shard_map/attend_0/pallas_call | solution.py:219
  78.4 15.9 %attend_6.1 = (bf16[1,512,1536]{2,1,0:T(8,128)(2,1)}, f32[3,32,512]{2,1,0:T(8,128)S(1)}, f32[32,512]{1,0:T(8,128)S(1)}, f32[64,1536]{1,0:T(8,128)S(1)}) custom-call(f32[4,1536]{1,0:T(4,128)S(1)} %bitcast.25, bf16[512,128]{1,0:T(8,128)(2,1)S(1)} %slice_bitcast_fusion.refs_1_, bf16[32,512]{1,0:T(8,128)(2,1)S(1)} %copy-done.7, ...), custom_call_target="tpu_custom_call", output_to_operand_aliasing={{0}: (17, {})} | custom-call | flops 18400000000 | bytes 5242880 | tf_op jit(solution)/shard_map/attend_6/pallas_call | solution.py:219
  94.3 8.9 %attend_10.1 = (bf16[1,512,1536]{2,1,0:T(8,128)(2,1)}, f32[3,32,256]{2,1,0:T(8,128)S(1)}, f32[32,512]{1,0:T(8,128)S(1)}, f32[64,1536]{1,0:T(8,128)S(1)}, bf16[64...) custom-call(f32[4,1536]{1,0:T(4,128)S(1)} %bitcast.26, ...), custom_call_target="tpu_custom_call", output_to_operand_aliasing={{0}: (17, {})} | custom-call | flops 9200000000 | bytes 2621440 | tf_op jit(solution)/shard_map/attend_10/pallas_call | solution.py:219
  103.2 7.7 %collective-permute-start.7 = (bf16[64,512]{1,0:T(8,128)(2,1)S(1)}, bf16[64,512]{1,0:T(8,128)(2,1)S(1)}, u32[]{:S(2)}, u32[]{:S(2)}) collective-permute-start(bf16[64,512]{1,0:T(8,128)(2,1)S(1)} %get-tuple-element.40), channel_id=1, source_target_pairs={{1,0},{2,1},{3,2},{4,3},{5,4},{6,5},{7,6},{8,7},{9,8},{10,9},{11,1... | collective-permute-start | bytes 196616 | tf_op jit(solution)/shard_map/ppermute | solution.py:391
  111.0 2.2 %collective-permute-done.6.from_prev = bf16[64,512]{1,0:T(8,128)(2,1)S(1)} collective-permute-done((bf16[64,512]{1,0:T(8,128)(2,1)S(1)}, bf16[64,512]{1,0:T(8,128)(2,1)S(1)}, u32[]{:S(2)}, u32[]{:S(2)}) %collective-permute-start.6) | collective-permute-done | bytes 65568 | tf_op jit(solution)/shard_map/ppermute | solution.py:391
  113.2 1.7 %project.1 = bf16[224,16,128]{2,1,0:T(8,128)(2,1)S(1)} custom-call(f32[32,512]{1,0:T(8,128)S(1)} %get-tuple-element.37.rq, f32[64,1536]{1,0:T(8,128)S(1)} %get-tuple-element.38.rkv, bf16[64,512]{1,0:T(8,128)(2,1)S(1)} %collective-permute-done.6.from_prev, bf16[64,512]{1,0:T(8,128)(2,1)S(1)} %collective-permute-done.7.from_next, ...), custom_call_target="tpu_custom_call" | custom-call | tf_op jit(solution)/shard_map/project/pallas_call | solution.py:352
  114.9 22.7 %all_to_all.10 = bf16[32,112,128]{2,1,0:T(8,128)(2,1)S(1)} all-to-all(bf16[32,112,128]{2,1,0:T(8,128)(2,1)S(1)} %bitcast.23), channel_id=1, replica_groups=mesh['batch'=4,'tiles'=32] {'tiles'}, dimensions={0} | all-to-all | bytes 1835008 | tf_op jit(solution)/shard_map/all_to_all | solution.py:397
  137.6 0.1 reduce_sum.22
  137.8 0.7 collective-permute-start.8
  138.5 1.4 collective-permute-start.9
  139.9 1.2 collective-permute-done.10
  141.1 1.3 collective-permute-done.9
  142.6 20.8 %all_to_all.11 = bf16[32,112,128]{2,1,0:T(8,128)(2,1)} all-to-all(bf16[32,112,128]{2,1,0:T(8,128)(2,1)S(1)} %broadcast_in_dim.43), channel_id=1, replica_groups=mesh['batch'=4,'tiles'=32] {'tiles'}, dimensions={0} | all-to-all | bytes 1835008 | tf_op jit(solution)/shard_map/all_to_all | solution.py:405
  163.4 2.5 %unpack.1 = (f32[3,32,3072]{2,1,0:T(8,128)}, f32[3,32,1536]{2,1,0:T(8,128)}) custom-call(bf16[224,16,128]{2,1,0:T(8,128)(2,1)} %bitcast.27), custom_call_target="tpu_custom_call" | custom-call | tf_op jit(solution)/shard_map/unpack/pallas_call | solution.py:384
  (52 shorter events, 0.9 us)
Async XLA Ops:
  6.9 10.3 %copy-start.1 = (bf16[512,3072]{1,0:T(8,128)(2,1)}, bf16[512,3072]{1,0:T(8,128)(2,1)S(1)}, u32[]{:S(2)}) copy-start(bf16[512,3072]{1,0:T(8,128)(2,1)S(1)} %get-tuple-element.41.x_mod) | copy-start | bytes 9437188
  6.9 10.3 %copy-start.6 = (bf16[32,512]{1,0:T(8,128)(2,1)}, bf16[32,512]{1,0:T(8,128)(2,1)S(1)}, u32[]{:S(2)}) copy-start(bf16[32,512]{1,0:T(8,128)(2,1)S(1)} %get-tuple-element.27.refs_2_) | copy-start | bytes 98308
  6.9 9.2 %slice-start = ((bf16[1,512,1536]{2,1,0:T(8,128)(2,1)}), bf16[1,512,512]{2,1,0:T(8,128)(2,1)S(1)}, s32[]{:S(2)}) async-start(bf16[1,512,1536]{2,1,0:T(8,128)(2,1)} %refs_6_.5), calls=%async_computation.2 | async-start | bytes 1048576 | tf_op jit(solution)/shard_map/slice | solution.py:431
  6.9 9.2 %slice-start.2 = ((bf16[1,512,1536]{2,1,0:T(8,128)(2,1)}), bf16[1,512,512]{2,1,0:T(8,128)(2,1)S(1)}, s32[]{:S(2)}) async-start(bf16[1,512,1536]{2,1,0:T(8,128)(2,1)} %refs_7_.5), calls=%async_computation.4 | async-start | bytes 1048576 | tf_op jit(solution)/shard_map/slice | solution.py:431
  6.9 47.2 %collective-permute-start = (bf16[13,512,128]{2,1,0:T(8,128)(2,1)S(1)}, bf16[13,512,128]{2,1,0:T(8,128)(2,1)}, u32[]{:S(2)}, u32[]{:S(2)}) collective-permute-start(bf16[13,512,128]{2,1,0:T(8,128)(2,1)S(1)} %get-tuple-element.26), channel_id=1, source_target_pairs={{0,1},{1,2},{2,3},{3,4},{4,5},{5,6},{6,7},{7,8},{8,9},{9,10},{10,1... | collective-permute-start | bytes 5111816 | tf_op jit(solution)/shard_map/ppermute | solution.py:391
  8.7 47.6 %collective-permute-start.1 = (bf16[13,512,128]{2,1,0:T(8,128)(2,1)S(1)}, bf16[13,512,128]{2,1,0:T(8,128)(2,1)}, u32[]{:S(2)}, u32[]{:S(2)}) collective-permute-start(bf16[13,512,128]{2,1,0:T(8,128)(2,1)S(1)} %get-tuple-element.26), channel_id=1, source_target_pairs={{1,0},{2,1},{3,2},{4,3},{5,4},{6,5},{7,6},{8,7},{9,8},{10,9},{11,1... | collective-permute-start | bytes 5111816 | tf_op jit(solution)/shard_map/ppermute | solution.py:391
  16.1 8.9 %slice-start.1 = ((bf16[1,512,1536]{2,1,0:T(8,128)(2,1)}), bf16[1,512,256]{2,1,0:T(8,128)(2,1)S(1)}, s32[]{:S(2)}) async-start(bf16[1,512,1536]{2,1,0:T(8,128)(2,1)} %refs_6_.5), calls=%async_computation.3 | async-start | bytes 524288 | tf_op jit(solution)/shard_map/slice | solution.py:431
  16.1 8.9 %slice-start.3 = ((bf16[1,512,1536]{2,1,0:T(8,128)(2,1)}), bf16[1,512,256]{2,1,0:T(8,128)(2,1)S(1)}, s32[]{:S(2)}) async-start(bf16[1,512,1536]{2,1,0:T(8,128)(2,1)} %refs_7_.5), calls=%async_computation.5 | async-start | bytes 524288 | tf_op jit(solution)/shard_map/slice | solution.py:431
  17.2 8.8 %copy-start.8 = (s32[4,27]{1,0:T(4,128)S(1)}, s32[4,27]{1,0:T(4,128)}, u32[]{:S(2)}) copy-start(s32[4,27]{1,0:T(4,128)} %param.19) | copy-start | bytes 1300
  17.2 9.4 %copy-start.3 = (bf16[3,32,1536]{2,1,0:T(8,128)(2,1)S(1)}, bf16[3,32,1536]{2,1,0:T(8,128)(2,1)}, u32[]{:S(2)}) copy-start(bf16[3,32,1536]{2,1,0:T(8,128)(2,1)} %refs_10_.5) | copy-start | bytes 884740
  17.2 61.1 %collective-permute-start.4 = (bf16[2,512,512]{2,1,0:T(8,128)(2,1)}, bf16[2,512,512]{2,1,0:T(8,128)(2,1)S(1)}, u32[]{:S(2)}, u32[]{:S(2)}) collective-permute-start(bf16[2,512,512]{2,1,0:T(8,128)(2,1)} %pad_maximum_fusion.1), channel_id=1, source_target_pairs={{0,1},{1,2},{2,3},{3,4},{4,5},{5,6},{6,7},{7,8},{8,9},{9,10},{10,1... | collective-permute-start | bytes 3145736 | tf_op jit(solution)/shard_map/ppermute | solution.py:391
  17.3 61.0 %collective-permute-start.5 = (bf16[2,512,512]{2,1,0:T(8,128)(2,1)}, bf16[2,512,512]{2,1,0:T(8,128)(2,1)}, u32[]{:S(2)}, u32[]{:S(2)}) collective-permute-start(bf16[2,512,512]{2,1,0:T(8,128)(2,1)} %pad_maximum_fusion.1), channel_id=1, source_target_pairs={{1,0},{2,1},{3,2},{4,3},{5,4},{6,5},{7,6},{8,7},{9,8},{10,9},{11,1... | collective-permute-start | bytes 3145736 | tf_op jit(solution)/shard_map/ppermute | solution.py:391
  25.9 68.4 %collective-permute-start.2 = (bf16[2,512,256]{2,1,0:T(8,128)(2,1)}, bf16[2,512,256]{2,1,0:T(8,128)(2,1)}, u32[]{:S(2)}, u32[]{:S(2)}) collective-permute-start(bf16[2,512,256]{2,1,0:T(8,128)(2,1)} %pad_maximum_fusion.2), channel_id=1, source_target_pairs={{0,1},{1,2},{2,3},{3,4},{4,5},{5,6},{6,7},{7,8},{8,9},{9,10},{10,1... | collective-permute-start | bytes 1572872 | tf_op jit(solution)/shard_map/ppermute | solution.py:391
  26.7 29.5 %copy-start = (bf16[1,512,1536]{2,1,0:T(8,128)(2,1)S(1)}, bf16[1,512,1536]{2,1,0:T(8,128)(2,1)}, u32[]{:S(2)}) copy-start(bf16[1,512,1536]{2,1,0:T(8,128)(2,1)} %refs_6_.5) | copy-start | bytes 4718596
  26.7 29.5 %copy-start.4 = (bf16[1,512,1536]{2,1,0:T(8,128)(2,1)S(1)}, bf16[1,512,1536]{2,1,0:T(8,128)(2,1)}, u32[]{:S(2)}) copy-start(bf16[1,512,1536]{2,1,0:T(8,128)(2,1)} %refs_5_.5) | copy-start | bytes 4718596
  26.8 29.5 %copy-start.7 = (bf16[32,512]{1,0:T(8,128)(2,1)S(1)}, bf16[32,512]{1,0:T(8,128)(2,1)}, u32[]{:S(2)}) copy-start(bf16[32,512]{1,0:T(8,128)(2,1)} %copy-done.6) | copy-start | bytes 98308
  54.2 40.1 %collective-permute-start.3 = (bf16[2,512,256]{2,1,0:T(8,128)(2,1)}, bf16[2,512,256]{2,1,0:T(8,128)(2,1)S(1)}, u32[]{:S(2)}, u32[]{:S(2)}) collective-permute-start(bf16[2,512,256]{2,1,0:T(8,128)(2,1)} %pad_maximum_fusion.2), channel_id=1, source_target_pairs={{1,0},{2,1},{3,2},{4,3},{5,4},{6,5},{7,6},{8,7},{9,8},{10,9},{11,1... | collective-permute-start | bytes 1572872 | tf_op jit(solution)/shard_map/ppermute | solution.py:391
  78.4 15.9 %copy-start.5 = (bf16[1,512,1536]{2,1,0:T(8,128)(2,1)S(1)}, bf16[1,512,1536]{2,1,0:T(8,128)(2,1)}, u32[]{:S(2)}) copy-start(bf16[1,512,1536]{2,1,0:T(8,128)(2,1)} %refs_5_.5) | copy-start | bytes 4718596
  94.3 18.9 %copy-start.2 = (bf16[512,3072]{1,0:T(8,128)(2,1)S(1)}, bf16[512,3072]{1,0:T(8,128)(2,1)}, u32[]{:S(2)}) copy-start(bf16[512,3072]{1,0:T(8,128)(2,1)} %copy-done.1) | copy-start | bytes 9437188
  103.2 10.0 %collective-permute-start.6 = (bf16[64,512]{1,0:T(8,128)(2,1)S(1)}, bf16[64,512]{1,0:T(8,128)(2,1)S(1)}, u32[]{:S(2)}, u32[]{:S(2)}) collective-permute-start(bf16[64,512]{1,0:T(8,128)(2,1)S(1)} %get-tuple-element.39), channel_id=1, source_target_pairs={{0,1},{1,2},{2,3},{3,4},{4,5},{5,6},{6,7},{7,8},{8,9},{9,10},{10,1... | collective-permute-start | bytes 196616 | tf_op jit(solution)/shard_map/ppermute | solution.py:391
  103.2 10.0 %collective-permute-start.7 = (bf16[64,512]{1,0:T(8,128)(2,1)S(1)}, bf16[64,512]{1,0:T(8,128)(2,1)S(1)}, u32[]{:S(2)}, u32[]{:S(2)}) collective-permute-start(bf16[64,512]{1,0:T(8,128)(2,1)S(1)} %get-tuple-element.40), channel_id=1, source_target_pairs={{1,0},{2,1},{3,2},{4,3},{5,4},{6,5},{7,6},{8,7},{9,8},{10,9},{11,1... | collective-permute-start | bytes 196616 | tf_op jit(solution)/shard_map/ppermute | solution.py:391
  137.7 3.4 %collective-permute-start.10 = (bf16[112,128]{1,0:T(8,128)(2,1)S(1)}, bf16[112,128]{1,0:T(8,128)(2,1)S(1)}, u32[]{:S(2)}, u32[]{:S(2)}) collective-permute-start(bf16[112,128]{1,0:T(8,128)(2,1)S(1)} %reduce_sum.22), channel_id=1, source_target_pairs={{0,96},{32,64},{64,32},{96,0},{1,97},{33,65},{65,33},{97,1},{2,98}... | collective-permute-start | bytes 86024 | tf_op jit(solution)/shard_map/ppermute | solution.py:401
  137.8 3.3 %collective-permute-start.8 = (bf16[112,128]{1,0:T(8,128)(2,1)S(1)}, bf16[112,128]{1,0:T(8,128)(2,1)S(1)}, u32[]{:S(2)}, u32[]{:S(2)}) collective-permute-start(bf16[112,128]{1,0:T(8,128)(2,1)S(1)} %reduce_sum.22), channel_id=1, source_target_pairs={{0,32},{32,0},{64,96},{96,64},{1,33},{33,1},{65,97},{97,65},{2,34}... | collective-permute-start | bytes 86024 | tf_op jit(solution)/shard_map/ppermute | solution.py:401
  138.5 3.9 %collective-permute-start.9 = (bf16[112,128]{1,0:T(8,128)(2,1)S(1)}, bf16[112,128]{1,0:T(8,128)(2,1)S(1)}, u32[]{:S(2)}, u32[]{:S(2)}) collective-permute-start(bf16[112,128]{1,0:T(8,128)(2,1)S(1)} %reduce_sum.22), channel_id=1, source_target_pairs={{0,64},{32,96},{64,0},{96,32},{1,65},{33,97},{65,1},{97,33},{2,66}... | collective-permute-start | bytes 86024 | tf_op jit(solution)/shard_map/ppermute | solution.py:401

commit v6 on v5

--- a/solution.py
+++ b/solution.py
@@ -15,7 +15,7 @@
 RANK = 32
 LOG2E = 1.4426950408889634
 ATTEND_FLOPS = 4_600_000_000
-CHUNKS = (6, 4, 2)
+CHUNKS = (4, 4, 2, 2)
 QBLOCK = 512
 PADDING = 8
 PER_STEP = 2
@@ -370,18 +370,26 @@
 
 def unpack_kernel(packed, down, up):
     tiles = 3 * RANK // 16
-    g = 0
+    first = 2 * pl.program_id(0)
+    at = 0
     for out in (down, up):
         for c in range(out.shape[2] // HEAD):
-            for r in range(tiles):
-                rows = slice(16 * (r % 2), 16 * (r % 2) + 16)
-                out[r // 2, rows, c * HEAD:(c + 1) * HEAD] = packed[g].astype(F32)
-                g += 1
+            for half in (0, 1):
+                rows = slice(16 * half, 16 * half + 16)
+                piece = packed[at + c * tiles + half + first]
+                out[0, rows, c * HEAD:(c + 1) * HEAD] = piece.astype(F32)
+        at += out.shape[2] // HEAD * tiles
 
 
 def unpack(packed, width, across):
-    shapes = [jax.ShapeDtypeStruct((3, RANK, n), F32) for n in (width, across)]
-    return pl.pallas_call(unpack_kernel, out_shape=shapes, name="unpack")(packed)
+    return pl.pallas_call(
+        unpack_kernel,
+        grid=(3,),
+        in_specs=[whole(packed)],
+        out_specs=[pl.BlockSpec((1, RANK, n), lambda i: (i, 0, 0)) for n in (width, across)],
+        out_shape=[jax.ShapeDtypeStruct((3, RANK, n), F32) for n in (width, across)],
+        name="unpack",
+    )(packed)
 
 
 def neighbours(before, after, axis):

time: 166 us -> 167 us (level)
  waiting for transfers between devices: 31.9 us -> 23.2 us
  Pallas kernels: 56.6 us -> 59.8 us
  starting transfers between devices: 29 us -> 31.6 us
  local copies, waits for them, and re-layouts: 0.48 us -> 2.21 us
    ppermute x8 -> x10, waiting for transfers between devices: 29.5 us -> 20.7 us  [neighbours(): return (lax.ppermute(before, axis, up), lax.ppermute(after, axis, down))]
    ppermute x8 -> x10, starting transfers between devices: 26.8 us -> 29.7 us  [neighbours(): return (lax.ppermute(before, axis, up), lax.ppermute(after, axis, down))]
    pallas_call x3 -> x4, Pallas kernels: 46.9 us -> 49 us  [attend_chunk(): pl.pallas_call(functools.partial(attend_kernel, first, last, slab), grid=...]
  transfers between devices with their start and end apart: 11 -> 13, of which waited for: 4 -> 5; matrix products, arithmetic and copies ran while one was open for 2% -> 3% of each run, Pallas kernels for 23% -> 24%
where the time goes in v6:
time: 167 us; the launch traced here: 166 us
  Pallas kernels  59.8 us (36%)
  blocking collectives  44.1 us (26%)
  starting transfers between devices  31.6 us (19%)
  waiting for transfers between devices  23.2 us (14%)
  other arithmetic  3.81 us (2%)
  local copies, waits for them, and re-layouts  2.21 us (1%)
    pallas_call x4, Pallas kernels, attend_chunk(): pl.pallas_call(functools.partial(attend_kernel, first, last, slab), grid=...  49 us
    ppermute x10, starting transfers between devices, neighbours(): return (lax.ppermute(before, axis, up), lax.ppermute(after, axis, down))  29.7 us
    all_to_all x1, blocking collectives, reduce_everywhere(): got = lax.all_to_all(parts, tiles, 0, 0, tiled=True)  22.7 us
    all_to_all x1, blocking collectives, reduce_everywhere(): return lax.all_to_all(spread, tiles, 0, 0, tiled=True).reshape(x.shape)  21.4 us
    ppermute x10, waiting for transfers between devices, neighbours(): return (lax.ppermute(before, axis, up), lax.ppermute(after, axis, down))  20.7 us
    pallas_call x1, Pallas kernels, prologue(): pl.pallas_call(prologue_kernel, grid_spec=pltpu.PrefetchScalarGridSpec(nu...  6.26 us
  transfers between devices with their start and end apart: 13, of which 5 were waited for; matrix products, arithmetic and copies ran while one was open for 3% of the time, Pallas kernels for 24%

profile of v6, /device:TPU:0, one launch (start us, length us, event | category | flops | bytes accessed | tf_op | source)
XLA Modules:
  0.0 166.1 jit_solution(9159429514748184666)
XLA Ops:
  1.3 6.3 %prologue.1 = (bf16[512,3072]{1,0:T(8,128)(2,1)S(1)}, bf16[9,512,128]{2,1,0:T(8,128)(2,1)}, bf16[32,512]{1,0:T(8,128)(2,1)S(1)}) custom-call(s32[1]{0:T(128)S(6)} %copy.23.step, bf16[1,512,3072]{2,1,0:T(8,128)(2,1)} %x.7, f32[50,2,3072]{2,1,0:T(2,128)} %shift_scale.1, bf16[3,32,3072]{2,1,0:T(8,128)(2,1)} %bitcast.29, bf16[1,512,1536]{2,1,0:T(8,128)(2,1)} %refs_6_.7, ...), custom_call_target="tpu_custom_call" | custom-call | tf_op jit(solution)/shard_map/prologue/pallas_call | solution.py:288
  7.5 1.7 %collective-permute-start = (bf16[9,512,128]{2,1,0:T(8,128)(2,1)}, bf16[9,512,128]{2,1,0:T(8,128)(2,1)}, u32[]{:S(2)}, u32[]{:S(2)}) collective-permute-start(bf16[9,512,128]{2,1,0:T(8,128)(2,1)} %get-tuple-element.30), channel_id=1, source_target_pairs={{0,1},{1,2},{2,3},{3,4},{4,5},{5,6},{6,7},{7,8},{8,9},{9,10},{10,1... | collective-permute-start | bytes 3538952 | tf_op jit(solution)/shard_map/ppermute | solution.py:399
  9.3 7.4 %collective-permute-start.1 = (bf16[9,512,128]{2,1,0:T(8,128)(2,1)}, bf16[9,512,128]{2,1,0:T(8,128)(2,1)}, u32[]{:S(2)}, u32[]{:S(2)}) collective-permute-start(bf16[9,512,128]{2,1,0:T(8,128)(2,1)} %get-tuple-element.30), channel_id=1, source_target_pairs={{1,0},{2,1},{3,2},{4,3},{5,4},{6,5},{7,6},{8,7},{9,8},{10,9},{11,1... | collective-permute-start | bytes 3538952 | tf_op jit(solution)/shard_map/ppermute | solution.py:399
  16.7 1.1 pad_maximum_fusion.1
  17.8 7.7 %collective-permute-start.7 = (bf16[2,512,512]{2,1,0:T(8,128)(2,1)}, bf16[2,512,512]{2,1,0:T(8,128)(2,1)}, u32[]{:S(2)}, u32[]{:S(2)}) collective-permute-start(bf16[2,512,512]{2,1,0:T(8,128)(2,1)} %pad_maximum_fusion.1), channel_id=1, source_target_pairs={{1,0},{2,1},{3,2},{4,3},{5,4},{6,5},{7,6},{8,7},{9,8},{10,9},{11,1... | collective-permute-start | bytes 3145736 | tf_op jit(solution)/shard_map/ppermute | solution.py:399
  25.5 0.9 fusion.9
  28.0 0.9 slice_bitcast_fusion.refs_1_
  28.9 1.1 pad_maximum_fusion.2
  30.3 13.4 %collective-permute-done.refs_3_.refs_11_.refs_12_ = bf16[9,512,128]{2,1,0:T(8,128)(2,1)} collective-permute-done((bf16[9,512,128]{2,1,0:T(8,128)(2,1)}, bf16[9,512,128]{2,1,0:T(8,128)(2,1)}, u32[]{:S(2)}, u32[]{:S(2)}) %collective-permute-start) | collective-permute-done | bytes 1179680 | tf_op jit(solution)/shard_map/ppermute | solution.py:399
  43.7 2.1 %collective-permute-start.5 = (bf16[2,512,256]{2,1,0:T(8,128)(2,1)}, bf16[2,512,256]{2,1,0:T(8,128)(2,1)S(1)}, u32[]{:S(2)}, u32[]{:S(2)}) collective-permute-start(bf16[2,512,256]{2,1,0:T(8,128)(2,1)} %pad_maximum_fusion.3), channel_id=1, source_target_pairs={{1,0},{2,1},{3,2},{4,3},{5,4},{6,5},{7,6},{8,7},{9,8},{10,9},{11,1... | collective-permute-start | bytes 1572872 | tf_op jit(solution)/shard_map/ppermute | solution.py:399
  45.8 15.4 %attend_0.1 = (bf16[1,512,1536]{2,1,0:T(8,128)(2,1)}, f32[3,32,512]{2,1,0:T(8,128)S(1)}, f32[32,512]{1,0:T(8,128)S(1)}, f32[64,1536]{1,0:T(8,128)S(1)}) custom-call(f32[4,1536]{1,0:T(4,128)S(1)} %bitcast.24, bf16[512,128]{1,0:T(8,128)(2,1)S(1)} %slice_bitcast_fusion.refs_1_, bf16[32,512]{1,0:T(8,128)(2,1)S(1)} %get-tuple-element.31.refs_2_, ...), custom_call_target="tpu_custom_call" | custom-call | flops 18400000000 | bytes 5242880 | tf_op jit(solution)/shard_map/attend_0/pallas_call | solution.py:219
  61.2 5.0 %collective-permute-done.6.refs_11_.refs_12_ = bf16[2,512,512]{2,1,0:T(8,128)(2,1)} collective-permute-done((bf16[2,512,512]{2,1,0:T(8,128)(2,1)}, bf16[2,512,512]{2,1,0:T(8,128)(2,1)}, u32[]{:S(2)}, u32[]{:S(2)}) %collective-permute-start.6) | collective-permute-done | bytes 1048608 | tf_op jit(solution)/shard_map/ppermute | solution.py:399
  66.2 2.9 %collective-permute-start.3 = (bf16[2,512,256]{2,1,0:T(8,128)(2,1)S(1)}, bf16[2,512,256]{2,1,0:T(8,128)(2,1)S(1)}, u32[]{:S(2)}, u32[]{:S(2)}) collective-permute-start(bf16[2,512,256]{2,1,0:T(8,128)(2,1)S(1)} %pad_maximum_fusion.2), channel_id=1, source_target_pairs={{1,0},{2,1},{3,2},{4,3},{5,4},{6,5},{7,6},{8,7},{9,8},{10,9},{11,1... | collective-permute-start | bytes 1572872 | tf_op jit(solution)/shard_map/ppermute | solution.py:399
  69.2 15.9 %attend_4.1 = (bf16[1,512,1536]{2,1,0:T(8,128)(2,1)}, f32[3,32,512]{2,1,0:T(8,128)S(1)}, f32[32,512]{1,0:T(8,128)S(1)}, f32[64,1536]{1,0:T(8,128)S(1)}) custom-call(f32[4,1536]{1,0:T(4,128)S(1)} %bitcast.25, bf16[512,128]{1,0:T(8,128)(2,1)S(1)} %slice_bitcast_fusion.refs_1_, ...), custom_call_target="tpu_custom_call", output_to_operand_aliasing={{0}: (17, {})} | custom-call | flops 18400000000 | bytes 5242880 | tf_op jit(solution)/shard_map/attend_4/pallas_call | solution.py:219
  85.1 8.8 %attend_8.1 = (bf16[1,512,1536]{2,1,0:T(8,128)(2,1)}, f32[3,32,256]{2,1,0:T(8,128)S(1)}, f32[32,512]{1,0:T(8,128)S(1)}, f32[64,1536]{1,0:T(8,128)S(1)}) custom-call(f32[4,1536]{1,0:T(4,128)S(1)} %bitcast.26, bf16[512,128]{1,0:T(8,128)(2,1)S(1)} %slice_bitcast_fusion.refs_1_, ...), custom_call_target="tpu_custom_call", output_to_operand_aliasing={{0}: (17, {})} | custom-call | flops 9200000000 | bytes 2621440 | tf_op jit(solution)/shard_map/attend_8/pallas_call | solution.py:219
  93.9 8.9 %attend_10.1 = (bf16[1,512,1536]{2,1,0:T(8,128)(2,1)}, f32[3,32,256]{2,1,0:T(8,128)S(1)}, f32[32,512]{1,0:T(8,128)S(1)}, f32[64,1536]{1,0:T(8,128)S(1)}, bf16[64...) custom-call(f32[4,1536]{1,0:T(4,128)S(1)} %bitcast.27, ...), custom_call_target="tpu_custom_call", output_to_operand_aliasing={{0}: (17, {})} | custom-call | flops 9200000000 | bytes 2621440 | tf_op jit(solution)/shard_map/attend_10/pallas_call | solution.py:219
  102.9 7.7 %collective-permute-start.9 = (bf16[64,512]{1,0:T(8,128)(2,1)S(1)}, bf16[64,512]{1,0:T(8,128)(2,1)S(1)}, u32[]{:S(2)}, u32[]{:S(2)}) collective-permute-start(bf16[64,512]{1,0:T(8,128)(2,1)S(1)} %get-tuple-element.47), channel_id=1, source_target_pairs={{1,0},{2,1},{3,2},{4,3},{5,4},{6,5},{7,6},{8,7},{9,8},{10,9},{11,1... | collective-permute-start | bytes 196616 | tf_op jit(solution)/shard_map/ppermute | solution.py:399
  110.6 2.2 %collective-permute-done.8.from_prev = bf16[64,512]{1,0:T(8,128)(2,1)S(1)} collective-permute-done((bf16[64,512]{1,0:T(8,128)(2,1)S(1)}, bf16[64,512]{1,0:T(8,128)(2,1)S(1)}, u32[]{:S(2)}, u32[]{:S(2)}) %collective-permute-start.8) | collective-permute-done | bytes 65568 | tf_op jit(solution)/shard_map/ppermute | solution.py:399
  112.8 1.7 %project.1 = bf16[224,16,128]{2,1,0:T(8,128)(2,1)S(1)} custom-call(f32[32,512]{1,0:T(8,128)S(1)} %get-tuple-element.44.rq, f32[64,1536]{1,0:T(8,128)S(1)} %get-tuple-element.45.rkv, bf16[64,512]{1,0:T(8,128)(2,1)S(1)} %collective-permute-done.8.from_prev, bf16[64,512]{1,0:T(8,128)(2,1)S(1)} %collective-permute-done.9.from_next, ...), custom_call_target="tpu_custom_call" | custom-call | tf_op jit(solution)/shard_map/project/pallas_call | solution.py:352
  114.5 22.7 %all_to_all.10 = bf16[32,112,128]{2,1,0:T(8,128)(2,1)S(1)} all-to-all(bf16[32,112,128]{2,1,0:T(8,128)(2,1)S(1)} %bitcast.23), channel_id=1, replica_groups=mesh['batch'=4,'tiles'=32] {'tiles'}, dimensions={0} | all-to-all | bytes 1835008 | tf_op jit(solution)/shard_map/all_to_all | solution.py:405
  138.2 1.2 collective-permute-start.12
  139.3 2.3 %collective-permute-done.11 = bf16[112,128]{1,0:T(8,128)(2,1)S(1)} collective-permute-done((bf16[112,128]{1,0:T(8,128)(2,1)S(1)}, bf16[112,128]{1,0:T(8,128)(2,1)S(1)}, u32[]{:S(2)}, u32[]{:S(2)}) %collective-permute-start.11) | collective-permute-done | bytes 28704 | tf_op jit(solution)/shard_map/ppermute | solution.py:409
  141.9 21.4 %all_to_all.11 = bf16[32,112,128]{2,1,0:T(8,128)(2,1)} all-to-all(bf16[32,112,128]{2,1,0:T(8,128)(2,1)S(1)} %broadcast_in_dim.43), channel_id=1, replica_groups=mesh['batch'=4,'tiles'=32] {'tiles'}, dimensions={0} | all-to-all | bytes 1835008 | tf_op jit(solution)/shard_map/all_to_all | solution.py:413
  163.3 2.8 %unpack.1 = (f32[3,32,3072]{2,1,0:T(8,128)}, f32[3,32,1536]{2,1,0:T(8,128)}) custom-call(bf16[224,16,128]{2,1,0:T(8,128)(2,1)} %bitcast.28), custom_call_target="tpu_custom_call" | custom-call | tf_op jit(solution)/shard_map/unpack/pallas_call | solution.py:385
  (49 shorter events, 3.0 us)
Async XLA Ops:
  7.5 9.2 %slice-start = ((bf16[1,512,1536]{2,1,0:T(8,128)(2,1)}), bf16[1,512,512]{2,1,0:T(8,128)(2,1)S(1)}, s32[]{:S(2)}) async-start(bf16[1,512,1536]{2,1,0:T(8,128)(2,1)} %refs_6_.7), calls=%async_computation.2 | async-start | bytes 1048576 | tf_op jit(solution)/shard_map/slice | solution.py:439
  7.5 9.2 %slice-start.1 = ((bf16[1,512,1536]{2,1,0:T(8,128)(2,1)}), bf16[1,512,512]{2,1,0:T(8,128)(2,1)S(1)}, s32[]{:S(2)}) async-start(bf16[1,512,1536]{2,1,0:T(8,128)(2,1)} %refs_7_.7), calls=%async_computation.3 | async-start | bytes 1048576 | tf_op jit(solution)/shard_map/slice | solution.py:439
  7.5 36.2 %collective-permute-start = (bf16[9,512,128]{2,1,0:T(8,128)(2,1)}, bf16[9,512,128]{2,1,0:T(8,128)(2,1)}, u32[]{:S(2)}, u32[]{:S(2)}) collective-permute-start(bf16[9,512,128]{2,1,0:T(8,128)(2,1)} %get-tuple-element.30), channel_id=1, source_target_pairs={{0,1},{1,2},{2,3},{3,4},{4,5},{5,6},{6,7},{7,8},{8,9},{9,10},{10,1... | collective-permute-start | bytes 3538952 | tf_op jit(solution)/shard_map/ppermute | solution.py:399
  9.3 36.5 %collective-permute-start.1 = (bf16[9,512,128]{2,1,0:T(8,128)(2,1)}, bf16[9,512,128]{2,1,0:T(8,128)(2,1)}, u32[]{:S(2)}, u32[]{:S(2)}) collective-permute-start(bf16[9,512,128]{2,1,0:T(8,128)(2,1)} %get-tuple-element.30), channel_id=1, source_target_pairs={{1,0},{2,1},{3,2},{4,3},{5,4},{6,5},{7,6},{8,7},{9,8},{10,9},{11,1... | collective-permute-start | bytes 3538952 | tf_op jit(solution)/shard_map/ppermute | solution.py:399
  16.7 8.8 %copy-start.3 = (bf16[1,512,1536]{2,1,0:T(8,128)(2,1)S(1)}, bf16[1,512,1536]{2,1,0:T(8,128)(2,1)}, u32[]{:S(2)}) copy-start(bf16[1,512,1536]{2,1,0:T(8,128)(2,1)} %refs_6_.7) | copy-start | bytes 4718596
  16.7 8.8 %copy-start.4 = (bf16[1,512,1536]{2,1,0:T(8,128)(2,1)S(1)}, bf16[1,512,1536]{2,1,0:T(8,128)(2,1)}, u32[]{:S(2)}) copy-start(bf16[1,512,1536]{2,1,0:T(8,128)(2,1)} %refs_7_.7) | copy-start | bytes 4718596
  17.8 9.6 %copy-start.5 = (s32[4,27]{1,0:T(4,128)S(1)}, s32[4,27]{1,0:T(4,128)}, u32[]{:S(2)}) copy-start(s32[4,27]{1,0:T(4,128)} %param.19) | copy-start | bytes 1300
  17.8 48.4 %collective-permute-start.6 = (bf16[2,512,512]{2,1,0:T(8,128)(2,1)}, bf16[2,512,512]{2,1,0:T(8,128)(2,1)}, u32[]{:S(2)}, u32[]{:S(2)}) collective-permute-start(bf16[2,512,512]{2,1,0:T(8,128)(2,1)} %pad_maximum_fusion.1), channel_id=1, source_target_pairs={{0,1},{1,2},{2,3},{3,4},{4,5},{5,6},{6,7},{7,8},{8,9},{9,10},{10,1... | collective-permute-start | bytes 3145736 | tf_op jit(solution)/shard_map/ppermute | solution.py:399
  17.8 51.4 %collective-permute-start.7 = (bf16[2,512,512]{2,1,0:T(8,128)(2,1)}, bf16[2,512,512]{2,1,0:T(8,128)(2,1)}, u32[]{:S(2)}, u32[]{:S(2)}) collective-permute-start(bf16[2,512,512]{2,1,0:T(8,128)(2,1)} %pad_maximum_fusion.1), channel_id=1, source_target_pairs={{1,0},{2,1},{3,2},{4,3},{5,4},{6,5},{7,6},{8,7},{9,8},{10,9},{11,1... | collective-permute-start | bytes 3145736 | tf_op jit(solution)/shard_map/ppermute | solution.py:399
  26.4 3.6 %copy-start.2 = (bf16[3,32,1536]{2,1,0:T(8,128)(2,1)S(1)}, bf16[3,32,1536]{2,1,0:T(8,128)(2,1)}, u32[]{:S(2)}) copy-start(bf16[3,32,1536]{2,1,0:T(8,128)(2,1)} %refs_10_.7) | copy-start | bytes 884740
  27.2 57.8 %collective-permute-start.4 = (bf16[2,512,256]{2,1,0:T(8,128)(2,1)}, bf16[2,512,256]{2,1,0:T(8,128)(2,1)}, u32[]{:S(2)}, u32[]{:S(2)}) collective-permute-start(bf16[2,512,256]{2,1,0:T(8,128)(2,1)} %pad_maximum_fusion.3), channel_id=1, source_target_pairs={{0,1},{1,2},{2,3},{3,4},{4,5},{5,6},{6,7},{7,8},{8,9},{9,10},{10,1... | collective-permute-start | bytes 1572872 | tf_op jit(solution)/shard_map/ppermute | solution.py:399
  30.3 30.9 %copy-start = (bf16[3,128,1536]{2,1,0:T(8,128)(2,1)}, bf16[3,128,1536]{2,1,0:T(8,128)(2,1)S(1)}, u32[]{:S(2)}) copy-start(bf16[3,128,1536]{2,1,0:T(8,128)(2,1)S(1)} %pad_maximum_fusion.refs_9_) | copy-start | bytes 3538948
  43.7 41.3 %collective-permute-start.5 = (bf16[2,512,256]{2,1,0:T(8,128)(2,1)}, bf16[2,512,256]{2,1,0:T(8,128)(2,1)S(1)}, u32[]{:S(2)}, u32[]{:S(2)}) collective-permute-start(bf16[2,512,256]{2,1,0:T(8,128)(2,1)} %pad_maximum_fusion.3), channel_id=1, source_target_pairs={{1,0},{2,1},{3,2},{4,3},{5,4},{6,5},{7,6},{8,7},{9,8},{10,9},{11,1... | collective-permute-start | bytes 1572872 | tf_op jit(solution)/shard_map/ppermute | solution.py:399
  45.8 48.1 %collective-permute-start.2 = (bf16[2,512,256]{2,1,0:T(8,128)(2,1)S(1)}, bf16[2,512,256]{2,1,0:T(8,128)(2,1)S(1)}, u32[]{:S(2)}, u32[]{:S(2)}) collective-permute-start(bf16[2,512,256]{2,1,0:T(8,128)(2,1)S(1)} %pad_maximum_fusion.2), channel_id=1, source_target_pairs={{0,1},{1,2},{2,3},{3,4},{4,5},{5,6},{6,7},{7,8},{8,9},{9,10},{10,1... | collective-permute-start | bytes 1572872 | tf_op jit(solution)/shard_map/ppermute | solution.py:399
  66.2 27.7 %collective-permute-start.3 = (bf16[2,512,256]{2,1,0:T(8,128)(2,1)S(1)}, bf16[2,512,256]{2,1,0:T(8,128)(2,1)S(1)}, u32[]{:S(2)}, u32[]{:S(2)}) collective-permute-start(bf16[2,512,256]{2,1,0:T(8,128)(2,1)S(1)} %pad_maximum_fusion.2), channel_id=1, source_target_pairs={{1,0},{2,1},{3,2},{4,3},{5,4},{6,5},{7,6},{8,7},{9,8},{10,9},{11,1... | collective-permute-start | bytes 1572872 | tf_op jit(solution)/shard_map/ppermute | solution.py:399
  69.2 15.9 %copy-start.1 = (bf16[3,128,1536]{2,1,0:T(8,128)(2,1)S(1)}, bf16[3,128,1536]{2,1,0:T(8,128)(2,1)}, u32[]{:S(2)}) copy-start(bf16[3,128,1536]{2,1,0:T(8,128)(2,1)} %copy-done) | copy-start | bytes 3538948
  102.9 10.0 %collective-permute-start.8 = (bf16[64,512]{1,0:T(8,128)(2,1)S(1)}, bf16[64,512]{1,0:T(8,128)(2,1)S(1)}, u32[]{:S(2)}, u32[]{:S(2)}) collective-permute-start(bf16[64,512]{1,0:T(8,128)(2,1)S(1)} %get-tuple-element.46), channel_id=1, source_target_pairs={{0,1},{1,2},{2,3},{3,4},{4,5},{5,6},{6,7},{7,8},{8,9},{9,10},{10,1... | collective-permute-start | bytes 196616 | tf_op jit(solution)/shard_map/ppermute | solution.py:399
  102.9 10.0 %collective-permute-start.9 = (bf16[64,512]{1,0:T(8,128)(2,1)S(1)}, bf16[64,512]{1,0:T(8,128)(2,1)S(1)}, u32[]{:S(2)}, u32[]{:S(2)}) collective-permute-start(bf16[64,512]{1,0:T(8,128)(2,1)S(1)} %get-tuple-element.47), channel_id=1, source_target_pairs={{1,0},{2,1},{3,2},{4,3},{5,4},{6,5},{7,6},{8,7},{9,8},{10,9},{11,1... | collective-permute-start | bytes 196616 | tf_op jit(solution)/shard_map/ppermute | solution.py:399
  137.4 2.0 %collective-permute-start.10 = (bf16[112,128]{1,0:T(8,128)(2,1)S(1)}, bf16[112,128]{1,0:T(8,128)(2,1)S(1)}, u32[]{:S(2)}, u32[]{:S(2)}) collective-permute-start(bf16[112,128]{1,0:T(8,128)(2,1)S(1)} %reduce_sum.22), channel_id=1, source_target_pairs={{0,32},{32,0},{64,96},{96,64},{1,33},{33,1},{65,97},{97,65},{2,34}... | collective-permute-start | bytes 86024 | tf_op jit(solution)/shard_map/ppermute | solution.py:409
  137.5 4.2 %collective-permute-start.11 = (bf16[112,128]{1,0:T(8,128)(2,1)S(1)}, bf16[112,128]{1,0:T(8,128)(2,1)S(1)}, u32[]{:S(2)}, u32[]{:S(2)}) collective-permute-start(bf16[112,128]{1,0:T(8,128)(2,1)S(1)} %reduce_sum.22), channel_id=1, source_target_pairs={{0,64},{32,96},{64,0},{96,32},{1,65},{33,97},{65,1},{97,33},{2,66}... | collective-permute-start | bytes 86024 | tf_op jit(solution)/shard_map/ppermute | solution.py:409
  138.2 3.6 %collective-permute-start.12 = (bf16[112,128]{1,0:T(8,128)(2,1)S(1)}, bf16[112,128]{1,0:T(8,128)(2,1)S(1)}, u32[]{:S(2)}, u32[]{:S(2)}) collective-permute-start(bf16[112,128]{1,0:T(8,128)(2,1)S(1)} %reduce_sum.22), channel_id=1, source_target_pairs={{0,96},{32,64},{64,32},{96,0},{1,97},{33,65},{65,33},{97,1},{2,98}... | collective-permute-start | bytes 86024 | tf_op jit(solution)/shard_map/ppermute | solution.py:409

commit v7 on v5

--- a/solution.py
+++ b/solution.py
@@ -15,7 +15,7 @@
 RANK = 32
 LOG2E = 1.4426950408889634
 ATTEND_FLOPS = 4_600_000_000
-CHUNKS = (6, 4, 2)
+CHUNKS = (4, 2, 4, 2)
 QBLOCK = 512
 PADDING = 8
 PER_STEP = 2
@@ -135,12 +135,13 @@
     def spread(n, rows, probs_low, score_grad):
         out = dot(probs_low, vl_s[n])
         attended[0, rows, n * HEAD:(n + 1) * HEAD] = out[:, :HEAD].astype(BF16)
-        cat_s[n, rows, :HEAD] = out[:, HEAD:]
+        rows_seen = out[:, HEAD:]
         out = dot(score_grad, kl_s[n])
         hi, lo = split_rows(out[:, :HEAD])
         dq_s[n, rows, :HEAD] = hi
         dq_s[n, rows, HEAD:] = lo
-        cat_s[n, rows, HEAD:] = out[:, HEAD:]
+        lane = lax.broadcasted_iota(jnp.int32, (QBLOCK, HEAD), 1)
+        cat_s[n, rows, :] = jnp.where(lane < RANK, rows_seen, out[:, HEAD:])
         return dot(xd_s[n, :, rows], probs_low), dot(xb_s[n, :, rows], score_grad)
 
     def finish(n, d_total, b_total):
@@ -148,7 +149,7 @@
         cat_t = cat_s[n].T
         both = dot(low0_t[...], dq_s[n])
         grad_up[0, :, cols] = both[:, :HEAD] + both[:, HEAD:]
-        grad_up[1, :, cols] = pair(cat_t[HEAD + 2 * RANK:HEAD + 3 * RANK], q_s[n])
+        grad_up[1, :, cols] = pair(cat_t[2 * RANK:3 * RANK], q_s[n])
         grad_up[2, :, cols] = pair(cat_t[:RANK], out_grad[0, :, cols])
         up0 = up[0, :, cols]
         return (dot_t(jnp.concatenate([up0, up0], axis=1), dq_s[n]),
@@ -239,7 +240,7 @@
             pltpu.VMEM((PER_STEP, 2 * RANK, slab), BF16),
             pltpu.VMEM((PER_STEP, 2 * RANK, slab), BF16),
             pltpu.VMEM((PER_STEP, slab, 2 * HEAD), BF16),
-            pltpu.VMEM((PER_STEP, slab, 2 * HEAD), F32),
+            pltpu.VMEM((PER_STEP, slab, HEAD), F32),
         ],
         input_output_aliases=aliases,
         compiler_params=pltpu.CompilerParams(

time: 166 us -> 166 us (level)
  waiting for transfers between devices: 31.9 us -> 18.2 us
  starting transfers between devices: 29 us -> 36.5 us
  Pallas kernels: 56.6 us -> 59 us
  local copies, waits for them, and re-layouts: 0.48 us -> 2.22 us
    ppermute x8 -> x10, waiting for transfers between devices: 29.5 us -> 15.8 us  [neighbours(): return (lax.ppermute(before, axis, up), lax.ppermute(after, axis, down))]
    ppermute x8 -> x10, starting transfers between devices: 26.8 us -> 34.6 us  [neighbours(): return (lax.ppermute(before, axis, up), lax.ppermute(after, axis, down))]
    pallas_call x3 -> x4, Pallas kernels: 46.9 us -> 48.5 us  [attend_chunk(): pl.pallas_call(functools.partial(attend_kernel, first, last, slab), grid=...]
  transfers between devices with their start and end apart: 11 -> 13, of which waited for: 4 -> 4; matrix products, arithmetic and copies ran while one was open for 2% -> 3% of each run, Pallas kernels for 23% -> 24%
where the time goes in v7:
time: 166 us; the launch traced here: 165 us
  Pallas kernels  59 us (36%)
  blocking collectives  44.2 us (27%)
  starting transfers between devices  36.5 us (22%)
  waiting for transfers between devices  18.2 us (11%)
  other arithmetic  3.81 us (2%)
  local copies, waits for them, and re-layouts  2.22 us (1%)
    pallas_call x4, Pallas kernels, attend_chunk(): pl.pallas_call(functools.partial(attend_kernel, first, last, slab), grid=...  48.5 us
    ppermute x10, starting transfers between devices, neighbours(): return (lax.ppermute(before, axis, up), lax.ppermute(after, axis, down))  34.6 us
    all_to_all x1, blocking collectives, reduce_everywhere(): got = lax.all_to_all(parts, tiles, 0, 0, tiled=True)  22.8 us
    all_to_all x1, blocking collectives, reduce_everywhere(): return lax.all_to_all(spread, tiles, 0, 0, tiled=True).reshape(x.shape)  21.4 us
    ppermute x10, waiting for transfers between devices, neighbours(): return (lax.ppermute(before, axis, up), lax.ppermute(after, axis, down))  15.8 us
    pallas_call x1, Pallas kernels, prologue(): pl.pallas_call(prologue_kernel, grid_spec=pltpu.PrefetchScalarGridSpec(nu...  6.39 us
  transfers between devices with their start and end apart: 13, of which 4 were waited for; matrix products, arithmetic and copies ran while one was open for 3% of the time, Pallas kernels for 24%

profile of v7, /device:TPU:0, one launch (start us, length us, event | category | flops | bytes accessed | tf_op | source)
XLA Modules:
  0.0 165.5 jit_solution(16640090719574527826)
XLA Ops:
  1.3 6.4 %prologue.1 = (bf16[512,3072]{1,0:T(8,128)(2,1)S(1)}, bf16[9,512,128]{2,1,0:T(8,128)(2,1)}, bf16[32,512]{1,0:T(8,128)(2,1)S(1)}) custom-call(s32[1]{0:T(128)S(6)} %copy.23.step, bf16[1,512,3072]{2,1,0:T(8,128)(2,1)} %x.7, f32[50,2,3072]{2,1,0:T(2,128)} %shift_scale.1, bf16[3,32,3072]{2,1,0:T(8,128)(2,1)} %bitcast.29, bf16[1,512,1536]{2,1,0:T(8,128)(2,1)} %refs_6_.7, ...), custom_call_target="tpu_custom_call" | custom-call | tf_op jit(solution)/shard_map/prologue/pallas_call | solution.py:289
  7.7 1.7 collective-permute-start
  9.3 7.4 %collective-permute-start.1 = (bf16[9,512,128]{2,1,0:T(8,128)(2,1)}, bf16[9,512,128]{2,1,0:T(8,128)(2,1)}, u32[]{:S(2)}, u32[]{:S(2)}) collective-permute-start(bf16[9,512,128]{2,1,0:T(8,128)(2,1)} %get-tuple-element.30), channel_id=1, source_target_pairs={{1,0},{2,1},{3,2},{4,3},{5,4},{6,5},{7,6},{8,7},{9,8},{10,9},{11,1... | collective-permute-start | bytes 3538952 | tf_op jit(solution)/shard_map/ppermute | solution.py:392
  16.7 0.9 fusion.9
  17.6 0.8 pad_maximum_fusion.3
  18.4 7.7 %collective-permute-start.7 = (bf16[2,512,256]{2,1,0:T(8,128)(2,1)}, bf16[2,512,256]{2,1,0:T(8,128)(2,1)}, u32[]{:S(2)}, u32[]{:S(2)}) collective-permute-start(bf16[2,512,256]{2,1,0:T(8,128)(2,1)} %pad_maximum_fusion.3), channel_id=1, source_target_pairs={{1,0},{2,1},{3,2},{4,3},{5,4},{6,5},{7,6},{8,7},{9,8},{10,9},{11,1... | collective-permute-start | bytes 1572872 | tf_op jit(solution)/shard_map/ppermute | solution.py:392
  26.2 1.1 pad_maximum_fusion.1
  28.0 0.9 slice_bitcast_fusion.refs_1_
  28.9 1.1 pad_maximum_fusion.2
  30.3 13.5 %collective-permute-done.refs_3_.refs_11_.refs_12_ = bf16[9,512,128]{2,1,0:T(8,128)(2,1)} collective-permute-done((bf16[9,512,128]{2,1,0:T(8,128)(2,1)}, bf16[9,512,128]{2,1,0:T(8,128)(2,1)}, u32[]{:S(2)}, u32[]{:S(2)}) %collective-permute-start) | collective-permute-done | bytes 1179680 | tf_op jit(solution)/shard_map/ppermute | solution.py:392
  43.8 2.1 %collective-permute-start.5 = (bf16[2,512,512]{2,1,0:T(8,128)(2,1)}, bf16[2,512,512]{2,1,0:T(8,128)(2,1)S(1)}, u32[]{:S(2)}, u32[]{:S(2)}) collective-permute-start(bf16[2,512,512]{2,1,0:T(8,128)(2,1)} %pad_maximum_fusion.1), channel_id=1, source_target_pairs={{1,0},{2,1},{3,2},{4,3},{5,4},{6,5},{7,6},{8,7},{9,8},{10,9},{11,1... | collective-permute-start | bytes 3145736 | tf_op jit(solution)/shard_map/ppermute | solution.py:392
  45.9 15.3 %attend_0.1 = (bf16[1,512,1536]{2,1,0:T(8,128)(2,1)}, f32[3,32,512]{2,1,0:T(8,128)S(1)}, f32[32,512]{1,0:T(8,128)S(1)}, f32[64,1536]{1,0:T(8,128)S(1)}) custom-call(f32[4,1536]{1,0:T(4,128)S(1)} %bitcast.24, bf16[512,128]{1,0:T(8,128)(2,1)S(1)} %slice_bitcast_fusion.refs_1_, bf16[32,512]{1,0:T(8,128)(2,1)S(1)} %get-tuple-element.31.refs_2_, ...), custom_call_target="tpu_custom_call" | custom-call | flops 18400000000 | bytes 5242880 | tf_op jit(solution)/shard_map/attend_0/pallas_call | solution.py:220
  61.2 8.0 %collective-permute-start.3 = (bf16[2,512,256]{2,1,0:T(8,128)(2,1)S(1)}, bf16[2,512,256]{2,1,0:T(8,128)(2,1)S(1)}, u32[]{:S(2)}, u32[]{:S(2)}) collective-permute-start(bf16[2,512,256]{2,1,0:T(8,128)(2,1)S(1)} %pad_maximum_fusion.2), channel_id=1, source_target_pairs={{1,0},{2,1},{3,2},{4,3},{5,4},{6,5},{7,6},{8,7},{9,8},{10,9},{11,1... | collective-permute-start | bytes 1572872 | tf_op jit(solution)/shard_map/ppermute | solution.py:392
  69.2 8.9 %attend_4.1 = (bf16[1,512,1536]{2,1,0:T(8,128)(2,1)}, f32[3,32,256]{2,1,0:T(8,128)S(1)}, f32[32,512]{1,0:T(8,128)S(1)}, f32[64,1536]{1,0:T(8,128)S(1)}) custom-call(f32[4,1536]{1,0:T(4,128)S(1)} %bitcast.25, bf16[512,128]{1,0:T(8,128)(2,1)S(1)} %slice_bitcast_fusion.refs_1_, ...), custom_call_target="tpu_custom_call", output_to_operand_aliasing={{0}: (17, {})} | custom-call | flops 9200000000 | bytes 2621440 | tf_op jit(solution)/shard_map/attend_4/pallas_call | solution.py:220
  78.1 15.7 %attend_6.1 = (bf16[1,512,1536]{2,1,0:T(8,128)(2,1)}, f32[3,32,512]{2,1,0:T(8,128)S(1)}, f32[32,512]{1,0:T(8,128)S(1)}, f32[64,1536]{1,0:T(8,128)S(1)}) custom-call(f32[4,1536]{1,0:T(4,128)S(1)} %bitcast.26, bf16[512,128]{1,0:T(8,128)(2,1)S(1)} %slice_bitcast_fusion.refs_1_, ...), custom_call_target="tpu_custom_call", output_to_operand_aliasing={{0}: (17, {})} | custom-call | flops 18400000000 | bytes 5242880 | tf_op jit(solution)/shard_map/attend_6/pallas_call | solution.py:220
  93.8 8.6 %attend_10.1 = (bf16[1,512,1536]{2,1,0:T(8,128)(2,1)}, f32[3,32,256]{2,1,0:T(8,128)S(1)}, f32[32,512]{1,0:T(8,128)S(1)}, f32[64,1536]{1,0:T(8,128)S(1)}, bf16[64...) custom-call(f32[4,1536]{1,0:T(4,128)S(1)} %bitcast.27, ...), custom_call_target="tpu_custom_call", output_to_operand_aliasing={{0}: (17, {})} | custom-call | flops 9200000000 | bytes 2621440 | tf_op jit(solution)/shard_map/attend_10/pallas_call | solution.py:220
  102.4 7.7 %collective-permute-start.9 = (bf16[64,512]{1,0:T(8,128)(2,1)S(1)}, bf16[64,512]{1,0:T(8,128)(2,1)S(1)}, u32[]{:S(2)}, u32[]{:S(2)}) collective-permute-start(bf16[64,512]{1,0:T(8,128)(2,1)S(1)} %get-tuple-element.47), channel_id=1, source_target_pairs={{1,0},{2,1},{3,2},{4,3},{5,4},{6,5},{7,6},{8,7},{9,8},{10,9},{11,1... | collective-permute-start | bytes 196616 | tf_op jit(solution)/shard_map/ppermute | solution.py:392
  110.2 2.2 %collective-permute-done.8.from_prev = bf16[64,512]{1,0:T(8,128)(2,1)S(1)} collective-permute-done((bf16[64,512]{1,0:T(8,128)(2,1)S(1)}, bf16[64,512]{1,0:T(8,128)(2,1)S(1)}, u32[]{:S(2)}, u32[]{:S(2)}) %collective-permute-start.8) | collective-permute-done | bytes 65568 | tf_op jit(solution)/shard_map/ppermute | solution.py:392
  112.4 1.7 %project.1 = bf16[224,16,128]{2,1,0:T(8,128)(2,1)S(1)} custom-call(f32[32,512]{1,0:T(8,128)S(1)} %get-tuple-element.44.rq, f32[64,1536]{1,0:T(8,128)S(1)} %get-tuple-element.45.rkv, bf16[64,512]{1,0:T(8,128)(2,1)S(1)} %collective-permute-done.8.from_prev, bf16[64,512]{1,0:T(8,128)(2,1)S(1)} %collective-permute-done.9.from_next, ...), custom_call_target="tpu_custom_call" | custom-call | tf_op jit(solution)/shard_map/project/pallas_call | solution.py:353
  114.1 22.8 %all_to_all.10 = bf16[32,112,128]{2,1,0:T(8,128)(2,1)S(1)} all-to-all(bf16[32,112,128]{2,1,0:T(8,128)(2,1)S(1)} %bitcast.23), channel_id=1, replica_groups=mesh['batch'=4,'tiles'=32] {'tiles'}, dimensions={0} | all-to-all | bytes 1835008 | tf_op jit(solution)/shard_map/all_to_all | solution.py:398
  137.9 1.2 collective-permute-start.12
  139.0 2.3 %collective-permute-done.11 = bf16[112,128]{1,0:T(8,128)(2,1)S(1)} collective-permute-done((bf16[112,128]{1,0:T(8,128)(2,1)S(1)}, bf16[112,128]{1,0:T(8,128)(2,1)S(1)}, u32[]{:S(2)}, u32[]{:S(2)}) %collective-permute-start.11) | collective-permute-done | bytes 28704 | tf_op jit(solution)/shard_map/ppermute | solution.py:402
  141.6 21.4 %all_to_all.11 = bf16[32,112,128]{2,1,0:T(8,128)(2,1)} all-to-all(bf16[32,112,128]{2,1,0:T(8,128)(2,1)S(1)} %broadcast_in_dim.43), channel_id=1, replica_groups=mesh['batch'=4,'tiles'=32] {'tiles'}, dimensions={0} | all-to-all | bytes 1835008 | tf_op jit(solution)/shard_map/all_to_all | solution.py:406
  163.0 2.5 %unpack.1 = (f32[3,32,3072]{2,1,0:T(8,128)}, f32[3,32,1536]{2,1,0:T(8,128)}) custom-call(bf16[224,16,128]{2,1,0:T(8,128)(2,1)} %bitcast.28), custom_call_target="tpu_custom_call" | custom-call | tf_op jit(solution)/shard_map/unpack/pallas_call | solution.py:385
  (49 shorter events, 2.2 us)
Async XLA Ops:
  1.3 15.4 %copy-start.3 = (bf16[1,512,1536]{2,1,0:T(8,128)(2,1)S(1)}, bf16[1,512,1536]{2,1,0:T(8,128)(2,1)}, u32[]{:S(2)}) copy-start(bf16[1,512,1536]{2,1,0:T(8,128)(2,1)} %refs_6_.7) | copy-start | bytes 4718596
  1.3 15.4 %copy-start.4 = (bf16[1,512,1536]{2,1,0:T(8,128)(2,1)S(1)}, bf16[1,512,1536]{2,1,0:T(8,128)(2,1)}, u32[]{:S(2)}) copy-start(bf16[1,512,1536]{2,1,0:T(8,128)(2,1)} %refs_7_.7) | copy-start | bytes 4718596
  7.7 36.1 %collective-permute-start = (bf16[9,512,128]{2,1,0:T(8,128)(2,1)}, bf16[9,512,128]{2,1,0:T(8,128)(2,1)}, u32[]{:S(2)}, u32[]{:S(2)}) collective-permute-start(bf16[9,512,128]{2,1,0:T(8,128)(2,1)} %get-tuple-element.30), channel_id=1, source_target_pairs={{0,1},{1,2},{2,3},{3,4},{4,5},{5,6},{6,7},{7,8},{8,9},{9,10},{10,1... | collective-permute-start | bytes 3538952 | tf_op jit(solution)/shard_map/ppermute | solution.py:392
  9.3 36.5 %collective-permute-start.1 = (bf16[9,512,128]{2,1,0:T(8,128)(2,1)}, bf16[9,512,128]{2,1,0:T(8,128)(2,1)}, u32[]{:S(2)}, u32[]{:S(2)}) collective-permute-start(bf16[9,512,128]{2,1,0:T(8,128)(2,1)} %get-tuple-element.30), channel_id=1, source_target_pairs={{1,0},{2,1},{3,2},{4,3},{5,4},{6,5},{7,6},{8,7},{9,8},{10,9},{11,1... | collective-permute-start | bytes 3538952 | tf_op jit(solution)/shard_map/ppermute | solution.py:392
  17.6 8.6 %slice-start = ((bf16[1,512,1536]{2,1,0:T(8,128)(2,1)}), bf16[1,512,512]{2,1,0:T(8,128)(2,1)S(1)}, s32[]{:S(2)}) async-start(bf16[1,512,1536]{2,1,0:T(8,128)(2,1)} %refs_6_.7), calls=%async_computation.2 | async-start | bytes 1048576 | tf_op jit(solution)/shard_map/slice | solution.py:432
  17.6 8.6 %slice-start.1 = ((bf16[1,512,1536]{2,1,0:T(8,128)(2,1)}), bf16[1,512,512]{2,1,0:T(8,128)(2,1)S(1)}, s32[]{:S(2)}) async-start(bf16[1,512,1536]{2,1,0:T(8,128)(2,1)} %refs_7_.7), calls=%async_computation.3 | async-start | bytes 1048576 | tf_op jit(solution)/shard_map/slice | solution.py:432
  18.4 42.7 %collective-permute-start.6 = (bf16[2,512,256]{2,1,0:T(8,128)(2,1)}, bf16[2,512,256]{2,1,0:T(8,128)(2,1)}, u32[]{:S(2)}, u32[]{:S(2)}) collective-permute-start(bf16[2,512,256]{2,1,0:T(8,128)(2,1)} %pad_maximum_fusion.3), channel_id=1, source_target_pairs={{0,1},{1,2},{2,3},{3,4},{4,5},{5,6},{6,7},{7,8},{8,9},{9,10},{10,1... | collective-permute-start | bytes 1572872 | tf_op jit(solution)/shard_map/ppermute | solution.py:392
  18.4 50.7 %collective-permute-start.7 = (bf16[2,512,256]{2,1,0:T(8,128)(2,1)}, bf16[2,512,256]{2,1,0:T(8,128)(2,1)}, u32[]{:S(2)}, u32[]{:S(2)}) collective-permute-start(bf16[2,512,256]{2,1,0:T(8,128)(2,1)} %pad_maximum_fusion.3), channel_id=1, source_target_pairs={{1,0},{2,1},{3,2},{4,3},{5,4},{6,5},{7,6},{8,7},{9,8},{10,9},{11,1... | collective-permute-start | bytes 1572872 | tf_op jit(solution)/shard_map/ppermute | solution.py:392
  26.2 1.2 copy-start.5
  26.2 3.8 %copy-start.2 = (bf16[3,32,1536]{2,1,0:T(8,128)(2,1)S(1)}, bf16[3,32,1536]{2,1,0:T(8,128)(2,1)}, u32[]{:S(2)}) copy-start(bf16[3,32,1536]{2,1,0:T(8,128)(2,1)} %refs_10_.7) | copy-start | bytes 884740
  27.3 50.8 %collective-permute-start.4 = (bf16[2,512,512]{2,1,0:T(8,128)(2,1)}, bf16[2,512,512]{2,1,0:T(8,128)(2,1)}, u32[]{:S(2)}, u32[]{:S(2)}) collective-permute-start(bf16[2,512,512]{2,1,0:T(8,128)(2,1)} %pad_maximum_fusion.1), channel_id=1, source_target_pairs={{0,1},{1,2},{2,3},{3,4},{4,5},{5,6},{6,7},{7,8},{8,9},{9,10},{10,1... | collective-permute-start | bytes 3145736 | tf_op jit(solution)/shard_map/ppermute | solution.py:392
  30.3 38.9 %copy-start = (bf16[3,128,1536]{2,1,0:T(8,128)(2,1)}, bf16[3,128,1536]{2,1,0:T(8,128)(2,1)S(1)}, u32[]{:S(2)}) copy-start(bf16[3,128,1536]{2,1,0:T(8,128)(2,1)S(1)} %pad_maximum_fusion.refs_9_) | copy-start | bytes 3538948
  43.8 34.2 %collective-permute-start.5 = (bf16[2,512,512]{2,1,0:T(8,128)(2,1)}, bf16[2,512,512]{2,1,0:T(8,128)(2,1)S(1)}, u32[]{:S(2)}, u32[]{:S(2)}) collective-permute-start(bf16[2,512,512]{2,1,0:T(8,128)(2,1)} %pad_maximum_fusion.1), channel_id=1, source_target_pairs={{1,0},{2,1},{3,2},{4,3},{5,4},{6,5},{7,6},{8,7},{9,8},{10,9},{11,1... | collective-permute-start | bytes 3145736 | tf_op jit(solution)/shard_map/ppermute | solution.py:392
  45.9 47.9 %collective-permute-start.2 = (bf16[2,512,256]{2,1,0:T(8,128)(2,1)S(1)}, bf16[2,512,256]{2,1,0:T(8,128)(2,1)S(1)}, u32[]{:S(2)}, u32[]{:S(2)}) collective-permute-start(bf16[2,512,256]{2,1,0:T(8,128)(2,1)S(1)} %pad_maximum_fusion.2), channel_id=1, source_target_pairs={{0,1},{1,2},{2,3},{3,4},{4,5},{5,6},{6,7},{7,8},{8,9},{9,10},{10,1... | collective-permute-start | bytes 1572872 | tf_op jit(solution)/shard_map/ppermute | solution.py:392
  61.2 32.6 %collective-permute-start.3 = (bf16[2,512,256]{2,1,0:T(8,128)(2,1)S(1)}, bf16[2,512,256]{2,1,0:T(8,128)(2,1)S(1)}, u32[]{:S(2)}, u32[]{:S(2)}) collective-permute-start(bf16[2,512,256]{2,1,0:T(8,128)(2,1)S(1)} %pad_maximum_fusion.2), channel_id=1, source_target_pairs={{1,0},{2,1},{3,2},{4,3},{5,4},{6,5},{7,6},{8,7},{9,8},{10,9},{11,1... | collective-permute-start | bytes 1572872 | tf_op jit(solution)/shard_map/ppermute | solution.py:392
  78.1 15.7 %copy-start.1 = (bf16[3,128,1536]{2,1,0:T(8,128)(2,1)S(1)}, bf16[3,128,1536]{2,1,0:T(8,128)(2,1)}, u32[]{:S(2)}) copy-start(bf16[3,128,1536]{2,1,0:T(8,128)(2,1)} %copy-done) | copy-start | bytes 3538948
  102.4 10.0 %collective-permute-start.8 = (bf16[64,512]{1,0:T(8,128)(2,1)S(1)}, bf16[64,512]{1,0:T(8,128)(2,1)S(1)}, u32[]{:S(2)}, u32[]{:S(2)}) collective-permute-start(bf16[64,512]{1,0:T(8,128)(2,1)S(1)} %get-tuple-element.46), channel_id=1, source_target_pairs={{0,1},{1,2},{2,3},{3,4},{4,5},{5,6},{6,7},{7,8},{8,9},{9,10},{10,1... | collective-permute-start | bytes 196616 | tf_op jit(solution)/shard_map/ppermute | solution.py:392
  102.4 10.0 %collective-permute-start.9 = (bf16[64,512]{1,0:T(8,128)(2,1)S(1)}, bf16[64,512]{1,0:T(8,128)(2,1)S(1)}, u32[]{:S(2)}, u32[]{:S(2)}) collective-permute-start(bf16[64,512]{1,0:T(8,128)(2,1)S(1)} %get-tuple-element.47), channel_id=1, source_target_pairs={{1,0},{2,1},{3,2},{4,3},{5,4},{6,5},{7,6},{8,7},{9,8},{10,9},{11,1... | collective-permute-start | bytes 196616 | tf_op jit(solution)/shard_map/ppermute | solution.py:392
  137.1 2.0 %collective-permute-start.10 = (bf16[112,128]{1,0:T(8,128)(2,1)S(1)}, bf16[112,128]{1,0:T(8,128)(2,1)S(1)}, u32[]{:S(2)}, u32[]{:S(2)}) collective-permute-start(bf16[112,128]{1,0:T(8,128)(2,1)S(1)} %reduce_sum.22), channel_id=1, source_target_pairs={{0,32},{32,0},{64,96},{96,64},{1,33},{33,1},{65,97},{97,65},{2,34}... | collective-permute-start | bytes 86024 | tf_op jit(solution)/shard_map/ppermute | solution.py:402
  137.2 4.2 %collective-permute-start.11 = (bf16[112,128]{1,0:T(8,128)(2,1)S(1)}, bf16[112,128]{1,0:T(8,128)(2,1)S(1)}, u32[]{:S(2)}, u32[]{:S(2)}) collective-permute-start(bf16[112,128]{1,0:T(8,128)(2,1)S(1)} %reduce_sum.22), channel_id=1, source_target_pairs={{0,64},{32,96},{64,0},{96,32},{1,65},{33,97},{65,1},{97,33},{2,66}... | collective-permute-start | bytes 86024 | tf_op jit(solution)/shard_map/ppermute | solution.py:402
  137.9 3.6 %collective-permute-start.12 = (bf16[112,128]{1,0:T(8,128)(2,1)S(1)}, bf16[112,128]{1,0:T(8,128)(2,1)S(1)}, u32[]{:S(2)}, u32[]{:S(2)}) collective-permute-start(bf16[112,128]{1,0:T(8,128)(2,1)S(1)} %reduce_sum.22), channel_id=1, source_target_pairs={{0,96},{32,64},{64,32},{96,0},{1,97},{33,65},{65,33},{97,1},{2,98}... | collective-permute-start | bytes 86024 | tf_op jit(solution)/shard_map/ppermute | solution.py:402

commit v8 on v7

--- a/solution.py
+++ b/solution.py
@@ -15,7 +15,7 @@
 RANK = 32
 LOG2E = 1.4426950408889634
 ATTEND_FLOPS = 4_600_000_000
-CHUNKS = (4, 2, 4, 2)
+CHUNKS = (6, 4, 2)
 QBLOCK = 512
 PADDING = 8
 PER_STEP = 2
@@ -385,11 +385,14 @@
     return pl.pallas_call(unpack_kernel, out_shape=shapes, name="unpack")(packed)
 
 
-def neighbours(before, after, axis):
-    count = lax.axis_size(axis)
-    up = [(i, (i + 1) % count) for i in range(count)]
+def neighbours(before, after, batch, tiles):
+    peers, count = lax.axis_size(batch), lax.axis_size(tiles)
+    up = [
+        (b * count + i, b * count + i + 1 if i + 1 < count else (b + peers // 2) % peers * count)
+        for b in range(peers) for i in range(count)
+    ]
     down = [(j, i) for i, j in up]
-    return lax.ppermute(before, axis, up), lax.ppermute(after, axis, down)
+    return lax.ppermute(before, (batch, tiles), up), lax.ppermute(after, (batch, tiles), down)
 
 
 def reduce_everywhere(x, batch, tiles):
@@ -435,10 +438,10 @@
         hidden, truncation_step, modulation, adapter_down_weight.transpose(0, 2, 1),
         frozen_keys, frozen_values, CHUNKS[0],
     )
-    halos = [neighbours(first_halo, first_halo, "tiles")]
+    halos = [neighbours(first_halo, first_halo, "batch", "tiles")]
     first_halo, keys, values = lax.optimization_barrier((first_halo, frozen_keys, frozen_values))
     parts = [frozen_part(keys, values, *b) for b in bounds[1:]]
-    halos += [neighbours(part, part, "tiles") for part in parts]
+    halos += [neighbours(part, part, "batch", "tiles") for part in parts]
     low = first_halo[2 * CHUNKS[0]]
 
     up = adapter_up_weight
@@ -460,7 +463,7 @@
         hidden.shape[0] * lax.axis_size("batch") * slab * lax.axis_size("tiles")
     )
     to_prev, to_next = sent
-    from_prev, from_next = neighbours(to_next, to_prev, "tiles")
+    from_prev, from_next = neighbours(to_next, to_prev, "batch", "tiles")
     packed = project(norm_factor, rq, rkv, from_prev, from_next, x_mod, grad_up_parts)
     packed = reduce_everywhere(packed, "batch", "tiles")
     grad_down, grad_up = unpack(packed, width, across)

time: 166 us -> 165 us (level)
  waiting for transfers between devices: 18.2 us -> 33.6 us
  starting transfers between devices: 36.5 us -> 28.7 us
  Pallas kernels: 59 us -> 56.4 us
  blocking collectives: 44.2 us -> 41.6 us
  local copies, waits for them, and re-layouts: 2.22 us -> 0.48 us
    ppermute x10 -> x8, waiting for transfers between devices: 15.8 us -> 29.8 us  [the longest x4 29.8 us: neighbours(): lax.ppermute(before, (batch, tiles), up)]
    ppermute x10 -> x8, starting transfers between devices: 34.6 us -> 25.9 us  [the longest x4 24.1 us: neighbours(): lax.ppermute(after, (batch, tiles), down)]
    all_to_all x1, blocking collectives: 22.8 us -> 20.8 us  [reduce_everywhere(): got = lax.all_to_all(parts, tiles, 0, 0, tiled=True)]
    pallas_call x4 -> x3, Pallas kernels: 48.5 us -> 46.6 us  [attend_chunk(): pl.pallas_call(functools.partial(attend_kernel, first, last, slab), grid=...]
  transfers between devices with their start and end apart: 13 -> 11, of which waited for: 4 -> 5; matrix products, arithmetic and copies ran while one was open for 3% -> 2% of each run, Pallas kernels for 24% -> 23%
where the time goes in v8:
time: 165 us
  Pallas kernels  56.4 us (34%)
  blocking collectives  41.6 us (25%)
  waiting for transfers between devices  33.6 us (20%)
  starting transfers between devices  28.7 us (17%)
  other arithmetic  2.73 us (2%)
    pallas_call x3, Pallas kernels, attend_chunk(): pl.pallas_call(functools.partial(attend_kernel, first, last, slab), grid=...  46.6 us
    ppermute x4, waiting for transfers between devices, neighbours(): lax.ppermute(before, (batch, tiles), up)  29.8 us
    ppermute x4, starting transfers between devices, neighbours(): lax.ppermute(after, (batch, tiles), down)  24.1 us
    all_to_all x1, blocking collectives, reduce_everywhere(): return lax.all_to_all(spread, tiles, 0, 0, tiled=True).reshape(x.shape)  20.8 us
    all_to_all x1, blocking collectives, reduce_everywhere(): got = lax.all_to_all(parts, tiles, 0, 0, tiled=True)  20.8 us
    pallas_call x1, Pallas kernels, prologue(): pl.pallas_call(prologue_kernel, grid_spec=pltpu.PrefetchScalarGridSpec(nu...  5.61 us
    ppermute x3, waiting for transfers between devices, reduce_everywhere(): lax.ppermute(mine, batch, [(i, i ^ d) for i in range(peers)]).astype(F32)  3.8 us
  transfers between devices with their start and end apart: 11, of which 5 were waited for; matrix products, arithmetic and copies ran while one was open for 2% of the time, Pallas kernels for 23%

profile of v8, /device:TPU:0, one launch (start us, length us, event | category | flops | bytes accessed | tf_op | source)
XLA Modules:
  0.0 165.0 jit_solution(7176039118598151283)
XLA Ops:
  1.3 5.6 %prologue.1 = (bf16[512,3072]{1,0:T(8,128)(2,1)S(1)}, bf16[13,512,128]{2,1,0:T(8,128)(2,1)S(1)}, bf16[32,512]{1,0:T(8,128)(2,1)S(1)}) custom-call(s32[1]{0:T(128)S(6)} %copy.21.step, bf16[1,512,3072]{2,1,0:T(8,128)(2,1)} %x.7, f32[50,2,3072]{2,1,0:T(2,128)} %shift_scale.1, bf16[3,32,3072]{2,1,0:T(8,128)(2,1)} %bitcast.28, bf16[1,512,1536]{2,1,0:T(8,128)(2,1)} %refs_6_.5, ...), custom_call_target="tpu_custom_call" | custom-call | tf_op jit(solution)/shard_map/prologue/pallas_call | solution.py:289
  6.9 1.7 %collective-permute-start = (bf16[13,512,128]{2,1,0:T(8,128)(2,1)S(1)}, bf16[13,512,128]{2,1,0:T(8,128)(2,1)}, u32[]{:S(2)}, u32[]{:S(2)}) collective-permute-start(bf16[13,512,128]{2,1,0:T(8,128)(2,1)S(1)} %get-tuple-element.26), channel_id=1, source_target_pairs={{0,1},{1,2},{2,3},{3,4},{4,5},{5,6},{6,7},{7,8},{8,9},{9,10},{10,1... | collective-permute-start | bytes 5111816 | tf_op jit(solution)/shard_map/ppermute | solution.py:395
  8.7 7.2 %collective-permute-start.1 = (bf16[13,512,128]{2,1,0:T(8,128)(2,1)S(1)}, bf16[13,512,128]{2,1,0:T(8,128)(2,1)}, u32[]{:S(2)}, u32[]{:S(2)}) collective-permute-start(bf16[13,512,128]{2,1,0:T(8,128)(2,1)S(1)} %get-tuple-element.26), channel_id=1, source_target_pairs={{1,0},{2,1},{3,2},{4,3},{5,4},{6,5},{7,6},{8,7},{9,8},{10,9},{11,1... | collective-permute-start | bytes 5111816 | tf_op jit(solution)/shard_map/ppermute | solution.py:395
  15.9 1.1 pad_maximum_fusion.1
  17.0 7.4 %collective-permute-start.5 = (bf16[2,512,512]{2,1,0:T(8,128)(2,1)}, bf16[2,512,512]{2,1,0:T(8,128)(2,1)}, u32[]{:S(2)}, u32[]{:S(2)}) collective-permute-start(bf16[2,512,512]{2,1,0:T(8,128)(2,1)} %pad_maximum_fusion.1), channel_id=1, source_target_pairs={{1,0},{2,1},{3,2},{4,3},{5,4},{6,5},{7,6},{8,7},{9,8},{10,9},{11,1... | collective-permute-start | bytes 3145736 | tf_op jit(solution)/shard_map/ppermute | solution.py:395
  24.5 0.8 pad_maximum_fusion.2
  25.5 0.3 select_reduce_fusion
  26.3 0.1 pad_maximum_fusion.refs_9_
  26.4 27.5 %collective-permute-done.refs_3_.refs_11_.refs_12_ = bf16[13,512,128]{2,1,0:T(8,128)(2,1)} collective-permute-done((bf16[13,512,128]{2,1,0:T(8,128)(2,1)S(1)}, bf16[13,512,128]{2,1,0:T(8,128)(2,1)}, u32[]{:S(2)}, u32[]{:S(2)}) %collective-permute-start) | collective-permute-done | bytes 1703968 | tf_op jit(solution)/shard_map/ppermute | solution.py:395
  53.9 2.1 %collective-permute-start.3 = (bf16[2,512,256]{2,1,0:T(8,128)(2,1)}, bf16[2,512,256]{2,1,0:T(8,128)(2,1)S(1)}, u32[]{:S(2)}, u32[]{:S(2)}) collective-permute-start(bf16[2,512,256]{2,1,0:T(8,128)(2,1)} %pad_maximum_fusion.2), channel_id=1, source_target_pairs={{1,0},{2,1},{3,2},{4,3},{5,4},{6,5},{7,6},{8,7},{9,8},{10,9},{11,1... | collective-permute-start | bytes 1572872 | tf_op jit(solution)/shard_map/ppermute | solution.py:395
  56.0 22.0 %attend_0.1 = (bf16[1,512,1536]{2,1,0:T(8,128)(2,1)}, f32[3,32,768]{2,1,0:T(8,128)S(1)}, f32[32,512]{1,0:T(8,128)S(1)}, f32[64,1536]{1,0:T(8,128)S(1)}) custom-call(f32[4,1536]{1,0:T(4,128)S(1)} %bitcast.24, bf16[512,128]{1,0:T(8,128)(2,1)S(1)} %slice_bitcast_fusion.refs_1_, bf16[32,512]{1,0:T(8,128)(2,1)S(1)} %copy-done.7, ...), custom_call_target="tpu_custom_call" | custom-call | flops 27599998976 | bytes 7864320 | tf_op jit(solution)/shard_map/attend_0/pallas_call | solution.py:220
  78.0 15.8 %attend_6.1 = (bf16[1,512,1536]{2,1,0:T(8,128)(2,1)}, f32[3,32,512]{2,1,0:T(8,128)S(1)}, f32[32,512]{1,0:T(8,128)S(1)}, f32[64,1536]{1,0:T(8,128)S(1)}) custom-call(f32[4,1536]{1,0:T(4,128)S(1)} %bitcast.25, bf16[512,128]{1,0:T(8,128)(2,1)S(1)} %slice_bitcast_fusion.refs_1_, bf16[32,512]{1,0:T(8,128)(2,1)S(1)} %copy-done.7, ...), custom_call_target="tpu_custom_call", output_to_operand_aliasing={{0}: (17, {})} | custom-call | flops 18400000000 | bytes 5242880 | tf_op jit(solution)/shard_map/attend_6/pallas_call | solution.py:220
  93.9 8.8 %attend_10.1 = (bf16[1,512,1536]{2,1,0:T(8,128)(2,1)}, f32[3,32,256]{2,1,0:T(8,128)S(1)}, f32[32,512]{1,0:T(8,128)S(1)}, f32[64,1536]{1,0:T(8,128)S(1)}, bf16[64...) custom-call(f32[4,1536]{1,0:T(4,128)S(1)} %bitcast.26, ...), custom_call_target="tpu_custom_call", output_to_operand_aliasing={{0}: (17, {})} | custom-call | flops 9200000000 | bytes 2621440 | tf_op jit(solution)/shard_map/attend_10/pallas_call | solution.py:220
  102.7 7.5 %collective-permute-start.7 = (bf16[64,512]{1,0:T(8,128)(2,1)S(1)}, bf16[64,512]{1,0:T(8,128)(2,1)S(1)}, u32[]{:S(2)}, u32[]{:S(2)}) collective-permute-start(bf16[64,512]{1,0:T(8,128)(2,1)S(1)} %get-tuple-element.40), channel_id=1, source_target_pairs={{1,0},{2,1},{3,2},{4,3},{5,4},{6,5},{7,6},{8,7},{9,8},{10,9},{11,1... | collective-permute-start | bytes 196616 | tf_op jit(solution)/shard_map/ppermute | solution.py:395
  110.2 2.2 %collective-permute-done.6.from_prev = bf16[64,512]{1,0:T(8,128)(2,1)S(1)} collective-permute-done((bf16[64,512]{1,0:T(8,128)(2,1)S(1)}, bf16[64,512]{1,0:T(8,128)(2,1)S(1)}, u32[]{:S(2)}, u32[]{:S(2)}) %collective-permute-start.6) | collective-permute-done | bytes 65568 | tf_op jit(solution)/shard_map/ppermute | solution.py:395
  112.4 1.7 %project.1 = bf16[224,16,128]{2,1,0:T(8,128)(2,1)S(1)} custom-call(f32[32,512]{1,0:T(8,128)S(1)} %get-tuple-element.37.rq, f32[64,1536]{1,0:T(8,128)S(1)} %get-tuple-element.38.rkv, bf16[64,512]{1,0:T(8,128)(2,1)S(1)} %collective-permute-done.6.from_prev, bf16[64,512]{1,0:T(8,128)(2,1)S(1)} %collective-permute-done.7.from_next, ...), custom_call_target="tpu_custom_call" | custom-call | tf_op jit(solution)/shard_map/project/pallas_call | solution.py:353
  114.1 20.8 %all_to_all.10 = bf16[32,112,128]{2,1,0:T(8,128)(2,1)S(1)} all-to-all(bf16[32,112,128]{2,1,0:T(8,128)(2,1)S(1)} %bitcast.23), channel_id=1, replica_groups=mesh['batch'=4,'tiles'=32] {'tiles'}, dimensions={0} | all-to-all | bytes 1835008 | tf_op jit(solution)/shard_map/all_to_all | solution.py:401
  134.9 0.1 reduce_sum.22
  135.1 2.6 %collective-permute-start.8 = (bf16[112,128]{1,0:T(8,128)(2,1)S(1)}, bf16[112,128]{1,0:T(8,128)(2,1)S(1)}, u32[]{:S(2)}, u32[]{:S(2)}) collective-permute-start(bf16[112,128]{1,0:T(8,128)(2,1)S(1)} %reduce_sum.22), channel_id=1, source_target_pairs={{0,32},{32,0},{64,96},{96,64},{1,33},{33,1},{65,97},{97,65},{2,34}... | collective-permute-start | bytes 86024 | tf_op jit(solution)/shard_map/ppermute | solution.py:405
  137.8 0.6 collective-permute-done.10
  138.4 0.2 collective-permute-done.8
  138.6 3.0 %collective-permute-done.9 = bf16[112,128]{1,0:T(8,128)(2,1)S(1)} collective-permute-done((bf16[112,128]{1,0:T(8,128)(2,1)S(1)}, bf16[112,128]{1,0:T(8,128)(2,1)S(1)}, u32[]{:S(2)}, u32[]{:S(2)}) %collective-permute-start.9) | collective-permute-done | bytes 28704 | tf_op jit(solution)/shard_map/ppermute | solution.py:405
  141.7 20.8 %all_to_all.11 = bf16[32,112,128]{2,1,0:T(8,128)(2,1)} all-to-all(bf16[32,112,128]{2,1,0:T(8,128)(2,1)S(1)} %broadcast_in_dim.43), channel_id=1, replica_groups=mesh['batch'=4,'tiles'=32] {'tiles'}, dimensions={0} | all-to-all | bytes 1835008 | tf_op jit(solution)/shard_map/all_to_all | solution.py:409
  162.6 2.5 %unpack.1 = (f32[3,32,3072]{2,1,0:T(8,128)}, f32[3,32,1536]{2,1,0:T(8,128)}) custom-call(bf16[224,16,128]{2,1,0:T(8,128)(2,1)} %bitcast.27), custom_call_target="tpu_custom_call" | custom-call | tf_op jit(solution)/shard_map/unpack/pallas_call | solution.py:385
  (52 shorter events, 0.9 us)
Async XLA Ops:
  6.9 10.0 %copy-start.1 = (bf16[512,3072]{1,0:T(8,128)(2,1)}, bf16[512,3072]{1,0:T(8,128)(2,1)S(1)}, u32[]{:S(2)}) copy-start(bf16[512,3072]{1,0:T(8,128)(2,1)S(1)} %get-tuple-element.41.x_mod) | copy-start | bytes 9437188
  6.9 10.0 %copy-start.6 = (bf16[32,512]{1,0:T(8,128)(2,1)}, bf16[32,512]{1,0:T(8,128)(2,1)S(1)}, u32[]{:S(2)}) copy-start(bf16[32,512]{1,0:T(8,128)(2,1)S(1)} %get-tuple-element.27.refs_2_) | copy-start | bytes 98308
  6.9 8.9 %slice-start = ((bf16[1,512,1536]{2,1,0:T(8,128)(2,1)}), bf16[1,512,512]{2,1,0:T(8,128)(2,1)S(1)}, s32[]{:S(2)}) async-start(bf16[1,512,1536]{2,1,0:T(8,128)(2,1)} %refs_6_.5), calls=%async_computation.2 | async-start | bytes 1048576 | tf_op jit(solution)/shard_map/slice | solution.py:435
  6.9 8.9 %slice-start.2 = ((bf16[1,512,1536]{2,1,0:T(8,128)(2,1)}), bf16[1,512,512]{2,1,0:T(8,128)(2,1)S(1)}, s32[]{:S(2)}) async-start(bf16[1,512,1536]{2,1,0:T(8,128)(2,1)} %refs_7_.5), calls=%async_computation.4 | async-start | bytes 1048576 | tf_op jit(solution)/shard_map/slice | solution.py:435
  6.9 47.0 %collective-permute-start = (bf16[13,512,128]{2,1,0:T(8,128)(2,1)S(1)}, bf16[13,512,128]{2,1,0:T(8,128)(2,1)}, u32[]{:S(2)}, u32[]{:S(2)}) collective-permute-start(bf16[13,512,128]{2,1,0:T(8,128)(2,1)S(1)} %get-tuple-element.26), channel_id=1, source_target_pairs={{0,1},{1,2},{2,3},{3,4},{4,5},{5,6},{6,7},{7,8},{8,9},{9,10},{10,1... | collective-permute-start | bytes 5111816 | tf_op jit(solution)/shard_map/ppermute | solution.py:395
  8.7 47.3 %collective-permute-start.1 = (bf16[13,512,128]{2,1,0:T(8,128)(2,1)S(1)}, bf16[13,512,128]{2,1,0:T(8,128)(2,1)}, u32[]{:S(2)}, u32[]{:S(2)}) collective-permute-start(bf16[13,512,128]{2,1,0:T(8,128)(2,1)S(1)} %get-tuple-element.26), channel_id=1, source_target_pairs={{1,0},{2,1},{3,2},{4,3},{5,4},{6,5},{7,6},{8,7},{9,8},{10,9},{11,1... | collective-permute-start | bytes 5111816 | tf_op jit(solution)/shard_map/ppermute | solution.py:395
  15.9 8.6 %slice-start.1 = ((bf16[1,512,1536]{2,1,0:T(8,128)(2,1)}), bf16[1,512,256]{2,1,0:T(8,128)(2,1)S(1)}, s32[]{:S(2)}) async-start(bf16[1,512,1536]{2,1,0:T(8,128)(2,1)} %refs_6_.5), calls=%async_computation.3 | async-start | bytes 524288 | tf_op jit(solution)/shard_map/slice | solution.py:435
  15.9 8.6 %slice-start.3 = ((bf16[1,512,1536]{2,1,0:T(8,128)(2,1)}), bf16[1,512,256]{2,1,0:T(8,128)(2,1)S(1)}, s32[]{:S(2)}) async-start(bf16[1,512,1536]{2,1,0:T(8,128)(2,1)} %refs_7_.5), calls=%async_computation.5 | async-start | bytes 524288 | tf_op jit(solution)/shard_map/slice | solution.py:435
  16.9 8.5 %copy-start.8 = (s32[4,27]{1,0:T(4,128)S(1)}, s32[4,27]{1,0:T(4,128)}, u32[]{:S(2)}) copy-start(s32[4,27]{1,0:T(4,128)} %param.19) | copy-start | bytes 1300
  16.9 9.2 %copy-start.3 = (bf16[3,32,1536]{2,1,0:T(8,128)(2,1)S(1)}, bf16[3,32,1536]{2,1,0:T(8,128)(2,1)}, u32[]{:S(2)}) copy-start(bf16[3,32,1536]{2,1,0:T(8,128)(2,1)} %refs_10_.5) | copy-start | bytes 884740
  17.0 61.0 %collective-permute-start.4 = (bf16[2,512,512]{2,1,0:T(8,128)(2,1)}, bf16[2,512,512]{2,1,0:T(8,128)(2,1)S(1)}, u32[]{:S(2)}, u32[]{:S(2)}) collective-permute-start(bf16[2,512,512]{2,1,0:T(8,128)(2,1)} %pad_maximum_fusion.1), channel_id=1, source_target_pairs={{0,1},{1,2},{2,3},{3,4},{4,5},{5,6},{6,7},{7,8},{8,9},{9,10},{10,1... | collective-permute-start | bytes 3145736 | tf_op jit(solution)/shard_map/ppermute | solution.py:395
  17.0 61.0 %collective-permute-start.5 = (bf16[2,512,512]{2,1,0:T(8,128)(2,1)}, bf16[2,512,512]{2,1,0:T(8,128)(2,1)}, u32[]{:S(2)}, u32[]{:S(2)}) collective-permute-start(bf16[2,512,512]{2,1,0:T(8,128)(2,1)} %pad_maximum_fusion.1), channel_id=1, source_target_pairs={{1,0},{2,1},{3,2},{4,3},{5,4},{6,5},{7,6},{8,7},{9,8},{10,9},{11,1... | collective-permute-start | bytes 3145736 | tf_op jit(solution)/shard_map/ppermute | solution.py:395
  25.3 68.5 %collective-permute-start.2 = (bf16[2,512,256]{2,1,0:T(8,128)(2,1)}, bf16[2,512,256]{2,1,0:T(8,128)(2,1)}, u32[]{:S(2)}, u32[]{:S(2)}) collective-permute-start(bf16[2,512,256]{2,1,0:T(8,128)(2,1)} %pad_maximum_fusion.2), channel_id=1, source_target_pairs={{0,1},{1,2},{2,3},{3,4},{4,5},{5,6},{6,7},{7,8},{8,9},{9,10},{10,1... | collective-permute-start | bytes 1572872 | tf_op jit(solution)/shard_map/ppermute | solution.py:395
  26.2 29.8 %copy-start = (bf16[1,512,1536]{2,1,0:T(8,128)(2,1)S(1)}, bf16[1,512,1536]{2,1,0:T(8,128)(2,1)}, u32[]{:S(2)}) copy-start(bf16[1,512,1536]{2,1,0:T(8,128)(2,1)} %refs_6_.5) | copy-start | bytes 4718596
  26.2 29.8 %copy-start.4 = (bf16[1,512,1536]{2,1,0:T(8,128)(2,1)S(1)}, bf16[1,512,1536]{2,1,0:T(8,128)(2,1)}, u32[]{:S(2)}) copy-start(bf16[1,512,1536]{2,1,0:T(8,128)(2,1)} %refs_5_.5) | copy-start | bytes 4718596
  26.2 29.8 %copy-start.7 = (bf16[32,512]{1,0:T(8,128)(2,1)S(1)}, bf16[32,512]{1,0:T(8,128)(2,1)}, u32[]{:S(2)}) copy-start(bf16[32,512]{1,0:T(8,128)(2,1)} %copy-done.6) | copy-start | bytes 98308
  53.9 40.0 %collective-permute-start.3 = (bf16[2,512,256]{2,1,0:T(8,128)(2,1)}, bf16[2,512,256]{2,1,0:T(8,128)(2,1)S(1)}, u32[]{:S(2)}, u32[]{:S(2)}) collective-permute-start(bf16[2,512,256]{2,1,0:T(8,128)(2,1)} %pad_maximum_fusion.2), channel_id=1, source_target_pairs={{1,0},{2,1},{3,2},{4,3},{5,4},{6,5},{7,6},{8,7},{9,8},{10,9},{11,1... | collective-permute-start | bytes 1572872 | tf_op jit(solution)/shard_map/ppermute | solution.py:395
  78.0 15.9 %copy-start.5 = (bf16[1,512,1536]{2,1,0:T(8,128)(2,1)S(1)}, bf16[1,512,1536]{2,1,0:T(8,128)(2,1)}, u32[]{:S(2)}) copy-start(bf16[1,512,1536]{2,1,0:T(8,128)(2,1)} %refs_5_.5) | copy-start | bytes 4718596
  93.9 18.5 %copy-start.2 = (bf16[512,3072]{1,0:T(8,128)(2,1)S(1)}, bf16[512,3072]{1,0:T(8,128)(2,1)}, u32[]{:S(2)}) copy-start(bf16[512,3072]{1,0:T(8,128)(2,1)} %copy-done.1) | copy-start | bytes 9437188
  102.7 9.7 %collective-permute-start.6 = (bf16[64,512]{1,0:T(8,128)(2,1)S(1)}, bf16[64,512]{1,0:T(8,128)(2,1)S(1)}, u32[]{:S(2)}, u32[]{:S(2)}) collective-permute-start(bf16[64,512]{1,0:T(8,128)(2,1)S(1)} %get-tuple-element.39), channel_id=1, source_target_pairs={{0,1},{1,2},{2,3},{3,4},{4,5},{5,6},{6,7},{7,8},{8,9},{9,10},{10,1... | collective-permute-start | bytes 196616 | tf_op jit(solution)/shard_map/ppermute | solution.py:395
  102.7 9.7 %collective-permute-start.7 = (bf16[64,512]{1,0:T(8,128)(2,1)S(1)}, bf16[64,512]{1,0:T(8,128)(2,1)S(1)}, u32[]{:S(2)}, u32[]{:S(2)}) collective-permute-start(bf16[64,512]{1,0:T(8,128)(2,1)S(1)} %get-tuple-element.40), channel_id=1, source_target_pairs={{1,0},{2,1},{3,2},{4,3},{5,4},{6,5},{7,6},{8,7},{9,8},{10,9},{11,1... | collective-permute-start | bytes 196616 | tf_op jit(solution)/shard_map/ppermute | solution.py:395
  135.0 3.4 %collective-permute-start.10 = (bf16[112,128]{1,0:T(8,128)(2,1)S(1)}, bf16[112,128]{1,0:T(8,128)(2,1)S(1)}, u32[]{:S(2)}, u32[]{:S(2)}) collective-permute-start(bf16[112,128]{1,0:T(8,128)(2,1)S(1)} %reduce_sum.22), channel_id=1, source_target_pairs={{0,96},{32,64},{64,32},{96,0},{1,97},{33,65},{65,33},{97,1},{2,98}... | collective-permute-start | bytes 86024 | tf_op jit(solution)/shard_map/ppermute | solution.py:405
  135.1 3.4 %collective-permute-start.8 = (bf16[112,128]{1,0:T(8,128)(2,1)S(1)}, bf16[112,128]{1,0:T(8,128)(2,1)S(1)}, u32[]{:S(2)}, u32[]{:S(2)}) collective-permute-start(bf16[112,128]{1,0:T(8,128)(2,1)S(1)} %reduce_sum.22), channel_id=1, source_target_pairs={{0,32},{32,0},{64,96},{96,64},{1,33},{33,1},{65,97},{97,65},{2,34}... | collective-permute-start | bytes 86024 | tf_op jit(solution)/shard_map/ppermute | solution.py:405
  137.7 3.9 %collective-permute-start.9 = (bf16[112,128]{1,0:T(8,128)(2,1)S(1)}, bf16[112,128]{1,0:T(8,128)(2,1)S(1)}, u32[]{:S(2)}, u32[]{:S(2)}) collective-permute-start(bf16[112,128]{1,0:T(8,128)(2,1)S(1)} %reduce_sum.22), channel_id=1, source_target_pairs={{0,64},{32,96},{64,0},{96,32},{1,65},{33,97},{65,1},{97,33},{2,66}... | collective-permute-start | bytes 86024 | tf_op jit(solution)/shard_map/ppermute | solution.py:405

commit v9 on v8

--- a/solution.py
+++ b/solution.py
@@ -17,6 +17,7 @@
 ATTEND_FLOPS = 4_600_000_000
 CHUNKS = (6, 4, 2)
 QBLOCK = 512
+ROWS = 256
 PADDING = 8
 PER_STEP = 2
 F32 = jnp.float32
@@ -285,23 +286,23 @@
         pltpu.with_memory_space_constraint(x, pltpu.HBM)
         for x in (hidden, modulation, down, frozen_keys, frozen_values)
     ]
-    frozen_spec = pl.BlockSpec((1, TILE, heads * HEAD), lambda i, step: (0, i, 0))
+    frozen_spec = pl.BlockSpec((1, ROWS, heads * HEAD), lambda i, step: (0, i, 0))
     return pl.pallas_call(
         prologue_kernel,
         grid_spec=pltpu.PrefetchScalarGridSpec(
             num_scalar_prefetch=1,
-            grid=(slab // TILE,),
+            grid=(slab // ROWS,),
             in_specs=[
-                pl.BlockSpec((1, TILE, width), lambda i, step: (0, i, 0)),
+                pl.BlockSpec((1, ROWS, width), lambda i, step: (0, i, 0)),
                 pl.BlockSpec((1, 2, width), lambda i, step: (step[0], 0, 0)),
                 whole(down),
                 frozen_spec,
                 frozen_spec,
             ],
             out_specs=[
-                pl.BlockSpec((TILE, width), lambda i, step: (i, 0)),
-                pl.BlockSpec((2 * heads + 1, TILE, HEAD), lambda i, step: (0, i, 0)),
-                pl.BlockSpec((RANK, TILE), lambda i, step: (0, i)),
+                pl.BlockSpec((ROWS, width), lambda i, step: (i, 0)),
+                pl.BlockSpec((2 * heads + 1, ROWS, HEAD), lambda i, step: (0, i, 0)),
+                pl.BlockSpec((RANK, ROWS), lambda i, step: (0, i)),
             ],
             scratch_shapes=[pltpu.VMEM((4 * RANK, width), BF16)],
         ),

time: 165 us -> 165 us (level)
  no operation moved by 1% of the time
where the time goes in v9:
time: 165 us
  Pallas kernels  55.9 us (34%)
  blocking collectives  41.6 us (25%)
  waiting for transfers between devices  33.6 us (20%)
  starting transfers between devices  28.7 us (17%)
  other arithmetic  2.73 us (2%)
    pallas_call x3, Pallas kernels, attend_chunk(): pl.pallas_call(functools.partial(attend_kernel, first, last, slab), grid=...  46.6 us
    ppermute x4, waiting for transfers between devices, neighbours(): lax.ppermute(before, (batch, tiles), up)  29.8 us
    ppermute x4, starting transfers between devices, neighbours(): lax.ppermute(after, (batch, tiles), down)  24.1 us
    all_to_all x1, blocking collectives, reduce_everywhere(): got = lax.all_to_all(parts, tiles, 0, 0, tiled=True)  20.8 us
    all_to_all x1, blocking collectives, reduce_everywhere(): return lax.all_to_all(spread, tiles, 0, 0, tiled=True).reshape(x.shape)  20.8 us
    pallas_call x1, Pallas kernels, prologue(): pl.pallas_call(prologue_kernel, grid_spec=pltpu.PrefetchScalarGridSpec(nu...  5.15 us
    ppermute x3, waiting for transfers between devices, reduce_everywhere(): lax.ppermute(mine, batch, [(i, i ^ d) for i in range(peers)]).astype(F32)  3.8 us
  transfers between devices with their start and end apart: 11, of which 5 were waited for; matrix products, arithmetic and copies ran while one was open for 2% of the time, Pallas kernels for 23%

profile of v9, /device:TPU:0, one launch (start us, length us, event | category | flops | bytes accessed | tf_op | source)
XLA Modules:
  0.0 164.6 jit_solution(6703063403319527801)
XLA Ops:
  1.3 5.1 %prologue.1 = (bf16[512,3072]{1,0:T(8,128)(2,1)S(1)}, bf16[13,512,128]{2,1,0:T(8,128)(2,1)S(1)}, bf16[32,512]{1,0:T(8,128)(2,1)S(1)}) custom-call(s32[1]{0:T(128)S(6)} %copy.21.step, bf16[1,512,3072]{2,1,0:T(8,128)(2,1)} %x.7, f32[50,2,3072]{2,1,0:T(2,128)} %shift_scale.1, bf16[3,32,3072]{2,1,0:T(8,128)(2,1)} %bitcast.28, bf16[1,512,1536]{2,1,0:T(8,128)(2,1)} %refs_6_.5, ...), custom_call_target="tpu_custom_call" | custom-call | tf_op jit(solution)/shard_map/prologue/pallas_call | solution.py:290
  6.5 1.7 %collective-permute-start = (bf16[13,512,128]{2,1,0:T(8,128)(2,1)S(1)}, bf16[13,512,128]{2,1,0:T(8,128)(2,1)}, u32[]{:S(2)}, u32[]{:S(2)}) collective-permute-start(bf16[13,512,128]{2,1,0:T(8,128)(2,1)S(1)} %get-tuple-element.26), channel_id=1, source_target_pairs={{0,1},{1,2},{2,3},{3,4},{4,5},{5,6},{6,7},{7,8},{8,9},{9,10},{10,1... | collective-permute-start | bytes 5111816 | tf_op jit(solution)/shard_map/ppermute | solution.py:396
  8.2 7.2 %collective-permute-start.1 = (bf16[13,512,128]{2,1,0:T(8,128)(2,1)S(1)}, bf16[13,512,128]{2,1,0:T(8,128)(2,1)}, u32[]{:S(2)}, u32[]{:S(2)}) collective-permute-start(bf16[13,512,128]{2,1,0:T(8,128)(2,1)S(1)} %get-tuple-element.26), channel_id=1, source_target_pairs={{1,0},{2,1},{3,2},{4,3},{5,4},{6,5},{7,6},{8,7},{9,8},{10,9},{11,1... | collective-permute-start | bytes 5111816 | tf_op jit(solution)/shard_map/ppermute | solution.py:396
  15.4 1.1 pad_maximum_fusion.1
  16.6 7.4 %collective-permute-start.5 = (bf16[2,512,512]{2,1,0:T(8,128)(2,1)}, bf16[2,512,512]{2,1,0:T(8,128)(2,1)}, u32[]{:S(2)}, u32[]{:S(2)}) collective-permute-start(bf16[2,512,512]{2,1,0:T(8,128)(2,1)} %pad_maximum_fusion.1), channel_id=1, source_target_pairs={{1,0},{2,1},{3,2},{4,3},{5,4},{6,5},{7,6},{8,7},{9,8},{10,9},{11,1... | collective-permute-start | bytes 3145736 | tf_op jit(solution)/shard_map/ppermute | solution.py:396
  24.0 0.8 pad_maximum_fusion.2
  25.0 0.3 select_reduce_fusion
  25.8 0.1 pad_maximum_fusion.refs_9_
  25.9 27.5 %collective-permute-done.refs_3_.refs_11_.refs_12_ = bf16[13,512,128]{2,1,0:T(8,128)(2,1)} collective-permute-done((bf16[13,512,128]{2,1,0:T(8,128)(2,1)S(1)}, bf16[13,512,128]{2,1,0:T(8,128)(2,1)}, u32[]{:S(2)}, u32[]{:S(2)}) %collective-permute-start) | collective-permute-done | bytes 1703968 | tf_op jit(solution)/shard_map/ppermute | solution.py:396
  53.4 2.1 %collective-permute-start.3 = (bf16[2,512,256]{2,1,0:T(8,128)(2,1)}, bf16[2,512,256]{2,1,0:T(8,128)(2,1)S(1)}, u32[]{:S(2)}, u32[]{:S(2)}) collective-permute-start(bf16[2,512,256]{2,1,0:T(8,128)(2,1)} %pad_maximum_fusion.2), channel_id=1, source_target_pairs={{1,0},{2,1},{3,2},{4,3},{5,4},{6,5},{7,6},{8,7},{9,8},{10,9},{11,1... | collective-permute-start | bytes 1572872 | tf_op jit(solution)/shard_map/ppermute | solution.py:396
  55.5 22.0 %attend_0.1 = (bf16[1,512,1536]{2,1,0:T(8,128)(2,1)}, f32[3,32,768]{2,1,0:T(8,128)S(1)}, f32[32,512]{1,0:T(8,128)S(1)}, f32[64,1536]{1,0:T(8,128)S(1)}) custom-call(f32[4,1536]{1,0:T(4,128)S(1)} %bitcast.24, bf16[512,128]{1,0:T(8,128)(2,1)S(1)} %slice_bitcast_fusion.refs_1_, bf16[32,512]{1,0:T(8,128)(2,1)S(1)} %copy-done.7, ...), custom_call_target="tpu_custom_call" | custom-call | flops 27599998976 | bytes 7864320 | tf_op jit(solution)/shard_map/attend_0/pallas_call | solution.py:221
  77.5 15.8 %attend_6.1 = (bf16[1,512,1536]{2,1,0:T(8,128)(2,1)}, f32[3,32,512]{2,1,0:T(8,128)S(1)}, f32[32,512]{1,0:T(8,128)S(1)}, f32[64,1536]{1,0:T(8,128)S(1)}) custom-call(f32[4,1536]{1,0:T(4,128)S(1)} %bitcast.25, bf16[512,128]{1,0:T(8,128)(2,1)S(1)} %slice_bitcast_fusion.refs_1_, bf16[32,512]{1,0:T(8,128)(2,1)S(1)} %copy-done.7, ...), custom_call_target="tpu_custom_call", output_to_operand_aliasing={{0}: (17, {})} | custom-call | flops 18400000000 | bytes 5242880 | tf_op jit(solution)/shard_map/attend_6/pallas_call | solution.py:221
  93.4 8.8 %attend_10.1 = (bf16[1,512,1536]{2,1,0:T(8,128)(2,1)}, f32[3,32,256]{2,1,0:T(8,128)S(1)}, f32[32,512]{1,0:T(8,128)S(1)}, f32[64,1536]{1,0:T(8,128)S(1)}, bf16[64...) custom-call(f32[4,1536]{1,0:T(4,128)S(1)} %bitcast.26, ...), custom_call_target="tpu_custom_call", output_to_operand_aliasing={{0}: (17, {})} | custom-call | flops 9200000000 | bytes 2621440 | tf_op jit(solution)/shard_map/attend_10/pallas_call | solution.py:221
  102.2 7.5 %collective-permute-start.7 = (bf16[64,512]{1,0:T(8,128)(2,1)S(1)}, bf16[64,512]{1,0:T(8,128)(2,1)S(1)}, u32[]{:S(2)}, u32[]{:S(2)}) collective-permute-start(bf16[64,512]{1,0:T(8,128)(2,1)S(1)} %get-tuple-element.40), channel_id=1, source_target_pairs={{1,0},{2,1},{3,2},{4,3},{5,4},{6,5},{7,6},{8,7},{9,8},{10,9},{11,1... | collective-permute-start | bytes 196616 | tf_op jit(solution)/shard_map/ppermute | solution.py:396
  109.7 2.2 %collective-permute-done.6.from_prev = bf16[64,512]{1,0:T(8,128)(2,1)S(1)} collective-permute-done((bf16[64,512]{1,0:T(8,128)(2,1)S(1)}, bf16[64,512]{1,0:T(8,128)(2,1)S(1)}, u32[]{:S(2)}, u32[]{:S(2)}) %collective-permute-start.6) | collective-permute-done | bytes 65568 | tf_op jit(solution)/shard_map/ppermute | solution.py:396
  111.9 1.7 %project.1 = bf16[224,16,128]{2,1,0:T(8,128)(2,1)S(1)} custom-call(f32[32,512]{1,0:T(8,128)S(1)} %get-tuple-element.37.rq, f32[64,1536]{1,0:T(8,128)S(1)} %get-tuple-element.38.rkv, bf16[64,512]{1,0:T(8,128)(2,1)S(1)} %collective-permute-done.6.from_prev, bf16[64,512]{1,0:T(8,128)(2,1)S(1)} %collective-permute-done.7.from_next, ...), custom_call_target="tpu_custom_call" | custom-call | tf_op jit(solution)/shard_map/project/pallas_call | solution.py:354
  113.6 20.8 %all_to_all.10 = bf16[32,112,128]{2,1,0:T(8,128)(2,1)S(1)} all-to-all(bf16[32,112,128]{2,1,0:T(8,128)(2,1)S(1)} %bitcast.23), channel_id=1, replica_groups=mesh['batch'=4,'tiles'=32] {'tiles'}, dimensions={0} | all-to-all | bytes 1835008 | tf_op jit(solution)/shard_map/all_to_all | solution.py:402
  134.4 0.1 reduce_sum.22
  134.7 2.6 %collective-permute-start.8 = (bf16[112,128]{1,0:T(8,128)(2,1)S(1)}, bf16[112,128]{1,0:T(8,128)(2,1)S(1)}, u32[]{:S(2)}, u32[]{:S(2)}) collective-permute-start(bf16[112,128]{1,0:T(8,128)(2,1)S(1)} %reduce_sum.22), channel_id=1, source_target_pairs={{0,32},{32,0},{64,96},{96,64},{1,33},{33,1},{65,97},{97,65},{2,34}... | collective-permute-start | bytes 86024 | tf_op jit(solution)/shard_map/ppermute | solution.py:406
  137.3 0.6 collective-permute-done.10
  137.9 0.2 collective-permute-done.8
  138.1 3.0 %collective-permute-done.9 = bf16[112,128]{1,0:T(8,128)(2,1)S(1)} collective-permute-done((bf16[112,128]{1,0:T(8,128)(2,1)S(1)}, bf16[112,128]{1,0:T(8,128)(2,1)S(1)}, u32[]{:S(2)}, u32[]{:S(2)}) %collective-permute-start.9) | collective-permute-done | bytes 28704 | tf_op jit(solution)/shard_map/ppermute | solution.py:406
  141.3 20.8 %all_to_all.11 = bf16[32,112,128]{2,1,0:T(8,128)(2,1)} all-to-all(bf16[32,112,128]{2,1,0:T(8,128)(2,1)S(1)} %broadcast_in_dim.43), channel_id=1, replica_groups=mesh['batch'=4,'tiles'=32] {'tiles'}, dimensions={0} | all-to-all | bytes 1835008 | tf_op jit(solution)/shard_map/all_to_all | solution.py:410
  162.1 2.5 %unpack.1 = (f32[3,32,3072]{2,1,0:T(8,128)}, f32[3,32,1536]{2,1,0:T(8,128)}) custom-call(bf16[224,16,128]{2,1,0:T(8,128)(2,1)} %bitcast.27), custom_call_target="tpu_custom_call" | custom-call | tf_op jit(solution)/shard_map/unpack/pallas_call | solution.py:386
  (52 shorter events, 0.9 us)
Async XLA Ops:
  6.4 10.0 %copy-start.1 = (bf16[512,3072]{1,0:T(8,128)(2,1)}, bf16[512,3072]{1,0:T(8,128)(2,1)S(1)}, u32[]{:S(2)}) copy-start(bf16[512,3072]{1,0:T(8,128)(2,1)S(1)} %get-tuple-element.41.x_mod) | copy-start | bytes 9437188
  6.4 10.0 %copy-start.6 = (bf16[32,512]{1,0:T(8,128)(2,1)}, bf16[32,512]{1,0:T(8,128)(2,1)S(1)}, u32[]{:S(2)}) copy-start(bf16[32,512]{1,0:T(8,128)(2,1)S(1)} %get-tuple-element.27.refs_2_) | copy-start | bytes 98308
  6.5 8.9 %slice-start = ((bf16[1,512,1536]{2,1,0:T(8,128)(2,1)}), bf16[1,512,512]{2,1,0:T(8,128)(2,1)S(1)}, s32[]{:S(2)}) async-start(bf16[1,512,1536]{2,1,0:T(8,128)(2,1)} %refs_6_.5), calls=%async_computation.2 | async-start | bytes 1048576 | tf_op jit(solution)/shard_map/slice | solution.py:436
  6.5 8.9 %slice-start.2 = ((bf16[1,512,1536]{2,1,0:T(8,128)(2,1)}), bf16[1,512,512]{2,1,0:T(8,128)(2,1)S(1)}, s32[]{:S(2)}) async-start(bf16[1,512,1536]{2,1,0:T(8,128)(2,1)} %refs_7_.5), calls=%async_computation.4 | async-start | bytes 1048576 | tf_op jit(solution)/shard_map/slice | solution.py:436
  6.5 47.0 %collective-permute-start = (bf16[13,512,128]{2,1,0:T(8,128)(2,1)S(1)}, bf16[13,512,128]{2,1,0:T(8,128)(2,1)}, u32[]{:S(2)}, u32[]{:S(2)}) collective-permute-start(bf16[13,512,128]{2,1,0:T(8,128)(2,1)S(1)} %get-tuple-element.26), channel_id=1, source_target_pairs={{0,1},{1,2},{2,3},{3,4},{4,5},{5,6},{6,7},{7,8},{8,9},{9,10},{10,1... | collective-permute-start | bytes 5111816 | tf_op jit(solution)/shard_map/ppermute | solution.py:396
  8.2 47.3 %collective-permute-start.1 = (bf16[13,512,128]{2,1,0:T(8,128)(2,1)S(1)}, bf16[13,512,128]{2,1,0:T(8,128)(2,1)}, u32[]{:S(2)}, u32[]{:S(2)}) collective-permute-start(bf16[13,512,128]{2,1,0:T(8,128)(2,1)S(1)} %get-tuple-element.26), channel_id=1, source_target_pairs={{1,0},{2,1},{3,2},{4,3},{5,4},{6,5},{7,6},{8,7},{9,8},{10,9},{11,1... | collective-permute-start | bytes 5111816 | tf_op jit(solution)/shard_map/ppermute | solution.py:396
  15.4 8.6 %slice-start.1 = ((bf16[1,512,1536]{2,1,0:T(8,128)(2,1)}), bf16[1,512,256]{2,1,0:T(8,128)(2,1)S(1)}, s32[]{:S(2)}) async-start(bf16[1,512,1536]{2,1,0:T(8,128)(2,1)} %refs_6_.5), calls=%async_computation.3 | async-start | bytes 524288 | tf_op jit(solution)/shard_map/slice | solution.py:436
  15.4 8.6 %slice-start.3 = ((bf16[1,512,1536]{2,1,0:T(8,128)(2,1)}), bf16[1,512,256]{2,1,0:T(8,128)(2,1)S(1)}, s32[]{:S(2)}) async-start(bf16[1,512,1536]{2,1,0:T(8,128)(2,1)} %refs_7_.5), calls=%async_computation.5 | async-start | bytes 524288 | tf_op jit(solution)/shard_map/slice | solution.py:436
  16.5 8.5 %copy-start.8 = (s32[4,27]{1,0:T(4,128)S(1)}, s32[4,27]{1,0:T(4,128)}, u32[]{:S(2)}) copy-start(s32[4,27]{1,0:T(4,128)} %param.19) | copy-start | bytes 1300
  16.5 9.2 %copy-start.3 = (bf16[3,32,1536]{2,1,0:T(8,128)(2,1)S(1)}, bf16[3,32,1536]{2,1,0:T(8,128)(2,1)}, u32[]{:S(2)}) copy-start(bf16[3,32,1536]{2,1,0:T(8,128)(2,1)} %refs_10_.5) | copy-start | bytes 884740
  16.5 61.0 %collective-permute-start.4 = (bf16[2,512,512]{2,1,0:T(8,128)(2,1)}, bf16[2,512,512]{2,1,0:T(8,128)(2,1)S(1)}, u32[]{:S(2)}, u32[]{:S(2)}) collective-permute-start(bf16[2,512,512]{2,1,0:T(8,128)(2,1)} %pad_maximum_fusion.1), channel_id=1, source_target_pairs={{0,1},{1,2},{2,3},{3,4},{4,5},{5,6},{6,7},{7,8},{8,9},{9,10},{10,1... | collective-permute-start | bytes 3145736 | tf_op jit(solution)/shard_map/ppermute | solution.py:396
  16.6 60.9 %collective-permute-start.5 = (bf16[2,512,512]{2,1,0:T(8,128)(2,1)}, bf16[2,512,512]{2,1,0:T(8,128)(2,1)}, u32[]{:S(2)}, u32[]{:S(2)}) collective-permute-start(bf16[2,512,512]{2,1,0:T(8,128)(2,1)} %pad_maximum_fusion.1), channel_id=1, source_target_pairs={{1,0},{2,1},{3,2},{4,3},{5,4},{6,5},{7,6},{8,7},{9,8},{10,9},{11,1... | collective-permute-start | bytes 3145736 | tf_op jit(solution)/shard_map/ppermute | solution.py:396
  24.9 68.5 %collective-permute-start.2 = (bf16[2,512,256]{2,1,0:T(8,128)(2,1)}, bf16[2,512,256]{2,1,0:T(8,128)(2,1)}, u32[]{:S(2)}, u32[]{:S(2)}) collective-permute-start(bf16[2,512,256]{2,1,0:T(8,128)(2,1)} %pad_maximum_fusion.2), channel_id=1, source_target_pairs={{0,1},{1,2},{2,3},{3,4},{4,5},{5,6},{6,7},{7,8},{8,9},{9,10},{10,1... | collective-permute-start | bytes 1572872 | tf_op jit(solution)/shard_map/ppermute | solution.py:396
  25.7 29.8 %copy-start = (bf16[1,512,1536]{2,1,0:T(8,128)(2,1)S(1)}, bf16[1,512,1536]{2,1,0:T(8,128)(2,1)}, u32[]{:S(2)}) copy-start(bf16[1,512,1536]{2,1,0:T(8,128)(2,1)} %refs_6_.5) | copy-start | bytes 4718596
  25.7 29.8 %copy-start.4 = (bf16[1,512,1536]{2,1,0:T(8,128)(2,1)S(1)}, bf16[1,512,1536]{2,1,0:T(8,128)(2,1)}, u32[]{:S(2)}) copy-start(bf16[1,512,1536]{2,1,0:T(8,128)(2,1)} %refs_5_.5) | copy-start | bytes 4718596
  25.7 29.8 %copy-start.7 = (bf16[32,512]{1,0:T(8,128)(2,1)S(1)}, bf16[32,512]{1,0:T(8,128)(2,1)}, u32[]{:S(2)}) copy-start(bf16[32,512]{1,0:T(8,128)(2,1)} %copy-done.6) | copy-start | bytes 98308
  53.4 39.9 %collective-permute-start.3 = (bf16[2,512,256]{2,1,0:T(8,128)(2,1)}, bf16[2,512,256]{2,1,0:T(8,128)(2,1)S(1)}, u32[]{:S(2)}, u32[]{:S(2)}) collective-permute-start(bf16[2,512,256]{2,1,0:T(8,128)(2,1)} %pad_maximum_fusion.2), channel_id=1, source_target_pairs={{1,0},{2,1},{3,2},{4,3},{5,4},{6,5},{7,6},{8,7},{9,8},{10,9},{11,1... | collective-permute-start | bytes 1572872 | tf_op jit(solution)/shard_map/ppermute | solution.py:396
  77.5 15.9 %copy-start.5 = (bf16[1,512,1536]{2,1,0:T(8,128)(2,1)S(1)}, bf16[1,512,1536]{2,1,0:T(8,128)(2,1)}, u32[]{:S(2)}) copy-start(bf16[1,512,1536]{2,1,0:T(8,128)(2,1)} %refs_5_.5) | copy-start | bytes 4718596
  93.4 18.5 %copy-start.2 = (bf16[512,3072]{1,0:T(8,128)(2,1)S(1)}, bf16[512,3072]{1,0:T(8,128)(2,1)}, u32[]{:S(2)}) copy-start(bf16[512,3072]{1,0:T(8,128)(2,1)} %copy-done.1) | copy-start | bytes 9437188
  102.2 9.7 %collective-permute-start.6 = (bf16[64,512]{1,0:T(8,128)(2,1)S(1)}, bf16[64,512]{1,0:T(8,128)(2,1)S(1)}, u32[]{:S(2)}, u32[]{:S(2)}) collective-permute-start(bf16[64,512]{1,0:T(8,128)(2,1)S(1)} %get-tuple-element.39), channel_id=1, source_target_pairs={{0,1},{1,2},{2,3},{3,4},{4,5},{5,6},{6,7},{7,8},{8,9},{9,10},{10,1... | collective-permute-start | bytes 196616 | tf_op jit(solution)/shard_map/ppermute | solution.py:396
  102.2 9.7 %collective-permute-start.7 = (bf16[64,512]{1,0:T(8,128)(2,1)S(1)}, bf16[64,512]{1,0:T(8,128)(2,1)S(1)}, u32[]{:S(2)}, u32[]{:S(2)}) collective-permute-start(bf16[64,512]{1,0:T(8,128)(2,1)S(1)} %get-tuple-element.40), channel_id=1, source_target_pairs={{1,0},{2,1},{3,2},{4,3},{5,4},{6,5},{7,6},{8,7},{9,8},{10,9},{11,1... | collective-permute-start | bytes 196616 | tf_op jit(solution)/shard_map/ppermute | solution.py:396
  134.6 3.4 %collective-permute-start.10 = (bf16[112,128]{1,0:T(8,128)(2,1)S(1)}, bf16[112,128]{1,0:T(8,128)(2,1)S(1)}, u32[]{:S(2)}, u32[]{:S(2)}) collective-permute-start(bf16[112,128]{1,0:T(8,128)(2,1)S(1)} %reduce_sum.22), channel_id=1, source_target_pairs={{0,96},{32,64},{64,32},{96,0},{1,97},{33,65},{65,33},{97,1},{2,98}... | collective-permute-start | bytes 86024 | tf_op jit(solution)/shard_map/ppermute | solution.py:406
  134.7 3.4 %collective-permute-start.8 = (bf16[112,128]{1,0:T(8,128)(2,1)S(1)}, bf16[112,128]{1,0:T(8,128)(2,1)S(1)}, u32[]{:S(2)}, u32[]{:S(2)}) collective-permute-start(bf16[112,128]{1,0:T(8,128)(2,1)S(1)} %reduce_sum.22), channel_id=1, source_target_pairs={{0,32},{32,0},{64,96},{96,64},{1,33},{33,1},{65,97},{97,65},{2,34}... | collective-permute-start | bytes 86024 | tf_op jit(solution)/shard_map/ppermute | solution.py:406
  137.2 3.9 %collective-permute-start.9 = (bf16[112,128]{1,0:T(8,128)(2,1)S(1)}, bf16[112,128]{1,0:T(8,128)(2,1)S(1)}, u32[]{:S(2)}, u32[]{:S(2)}) collective-permute-start(bf16[112,128]{1,0:T(8,128)(2,1)S(1)} %reduce_sum.22), channel_id=1, source_target_pairs={{0,64},{32,96},{64,0},{96,32},{1,65},{33,97},{65,1},{97,33},{2,66}... | collective-permute-start | bytes 86024 | tf_op jit(solution)/shard_map/ppermute | solution.py:406
